TPU v7x, 32 devices: a whole 2x2x4 slice. The times are simulated.
32 devices in a mesh: groups: 2 (over x), section: 16 (over z, y, core).
Axes of the slice: x: 2, y: 2, z: 4, core: 2. Of those that a mesh axis runs over, the one named last changes fastest.
Arguments:
- acts_down: bfloat16 [32, 128, 2048], P(('groups', 'section')), parts along dimension 0, may hold values from -6 to 6
- acts_up: bfloat16 [32, 128, 2048], P(('groups', 'section')), parts along dimension 0, may hold values from -6 to 6
- cotangent_down: bfloat16 [32, 128, 2048], P(('groups', 'section')), parts along dimension 0, may hold values from -6 to 6
- cotangent_up: bfloat16 [32, 128, 2048], P(('groups', 'section')), parts along dimension 0, may hold values from -6 to 6
- ln_gain: bfloat16 [16, 2048], P('section'), may hold values from 0.5 to 1.5
- w_qkv: bfloat16 [16, 2048, 768], P('section'), may hold values from -0.125 to 0.125
- w_out: bfloat16 [16, 256, 2048], P('section'), may hold values from -0.375 to 0.375
- band_offsets: int32 [4, 2], replicated, may hold values from 1 to 3
Outputs:
- out_down: bfloat16 [32, 128, 2048], P(('groups', 'section')), parts along dimension 0
- out_up: bfloat16 [32, 128, 2048], P(('groups', 'section')), parts along dimension 0
- back_down: bfloat16 [32, 128, 2048], P(('groups', 'section')), parts along dimension 0
- back_up: bfloat16 [32, 128, 2048], P(('groups', 'section')), parts along dimension 0
- grad_gain: bfloat16 [32, 2048], P(('groups', 'section')), parts along dimension 0
- grad_qkv: bfloat16 [32, 2048, 768], P(('groups', 'section')), parts along dimension 0
- grad_out: bfloat16 [32, 256, 2048], P(('groups', 'section')), parts along dimension 0
There are 2 independent parts, one for each index of `groups`. A program takes and returns all parts, laid end to end along the dimension named above; an argument that names none is the same for every part. Nothing has to cross between parts.
Inputs may be any that keep to these rules, and one draw needn't show every extreme that they name: `band_offsets`: for block row r of a banded section, block r - o is read for each listed o with r - o >= 0.
All inputs are finite; a program needn't handle non-finite values.
Results may differ from a plain program's by a relative error of at most 0.024.
Values may be sent and summed in bfloat16 or wider, within the bound.
No kernel may reach another device: no remote copies, remote signals or barrier semaphores. Data moves between devices by JAX's collectives and lax.ppermute only.
A program may use at most 128 MiB of HBM per device.

v0:
```python
import functools
import math

import jax
import jax.numpy as jnp
from jax import lax
from jax.experimental import pallas as pl
from jax.experimental.pallas import tpu as pltpu
from jax.sharding import PartitionSpec as P

HEADS_DEV = 2
HEAD_DIM = 128
BLOCK = 32
CHUNK = 16
F32 = jnp.float32
BF16 = jnp.bfloat16
NT = (((1,), (1,)), ((), ()))
TN = (((0,), (0,)), ((), ()))
SCALE = 1.0 / math.sqrt(HEAD_DIM)
VM = pl.BlockSpec(memory_space=pltpu.VMEM)
SM = pl.BlockSpec(memory_space=pltpu.SMEM)
ANY = pl.BlockSpec(memory_space=pl.ANY)


def dot(a, b, dims=(((1,), (0,)), ((), ()))):
    return lax.dot_general(a, b, dims, preferred_element_type=F32)


def mask_body(parity, offs_ref, rows):
    row = lax.broadcasted_iota(jnp.int32, (rows, rows), 0)
    col = lax.broadcasted_iota(jnp.int32, (rows, rows), 1)
    row_block = row // BLOCK
    col_block = col // BLOCK
    near = row_block == col_block
    for block in range(offs_ref.shape[0]):
        for listed in range(offs_ref.shape[1]):
            near = near | ((row_block == block) & (col_block == block - offs_ref[block, listed]))
    keep = (col <= row) & (near | (parity == 0))
    return jnp.where(keep, 1.0, 0.0).astype(F32)


def forward_body(h_ref, gain_ref, wq_ref, wo_ref, mask_ref, out_ref, u_ref, qkv_ref, p_ref, att_ref, st_ref):
    rows, width = h_ref.shape
    hd = HEADS_DEV * HEAD_DIM
    gain = gain_ref[...].astype(F32)
    for start in range(0, rows, CHUNK):
        part = pl.ds(start, CHUNK)
        x = h_ref[part, :].astype(F32)
        mean = jnp.sum(x, axis=-1, keepdims=True) * (1.0 / width)
        centred = x - mean
        rstd = lax.rsqrt(jnp.sum(centred * centred, axis=-1, keepdims=True) * (1.0 / width) + 1e-05)
        u_ref[part, :] = (centred * rstd * gain).astype(BF16)
        st_ref[part, :] = jnp.concatenate(
            [jnp.broadcast_to(mean, (CHUNK, 128)), jnp.broadcast_to(rstd, (CHUNK, 128))], axis=1)
    for n in range(3):
        qkv_ref[:, n * hd:(n + 1) * hd] = dot(u_ref[...], wq_ref[:, n * hd:(n + 1) * hd]).astype(BF16)
    keep = mask_ref[...]
    for head in range(HEADS_DEV):
        at = head * HEAD_DIM
        q = qkv_ref[:, at:at + HEAD_DIM]
        k = qkv_ref[:, hd + at:hd + at + HEAD_DIM]
        v = qkv_ref[:, 2 * hd + at:2 * hd + at + HEAD_DIM]
        weighted = jnp.where(keep > 0.0, jnp.exp(dot(q, k, NT) * SCALE), 0.0)
        probs = weighted / jnp.sum(weighted, axis=-1, keepdims=True)
        p_ref[head] = probs
        att_ref[:, at:at + HEAD_DIM] = dot(probs.astype(BF16), v).astype(BF16)
    for n in range(0, width, 512):
        cols = pl.ds(n, 512)
        out_ref[:, cols] = (h_ref[:, cols].astype(F32) + dot(att_ref[...], wo_ref[:, cols])).astype(BF16)


def backward_body(g_ref, h_ref, gain_ref, wq_ref, wo_ref, qkv_ref, p_ref, st_ref, e_ref, dqkv_ref, dg_ref, du_ref):
    rows, width = h_ref.shape
    hd = HEADS_DEV * HEAD_DIM
    datt = dot(g_ref[...], wo_ref[...], NT).astype(BF16)
    for head in range(HEADS_DEV):
        at = head * HEAD_DIM
        q = qkv_ref[:, at:at + HEAD_DIM]
        k = qkv_ref[:, hd + at:hd + at + HEAD_DIM]
        v = qkv_ref[:, 2 * hd + at:2 * hd + at + HEAD_DIM]
        probs = p_ref[head]
        da = datt[:, at:at + HEAD_DIM]
        dp = dot(da, v, NT).astype(BF16).astype(F32)
        dqkv_ref[:, 2 * hd + at:2 * hd + at + HEAD_DIM] = dot(probs.astype(BF16), da, TN).astype(BF16)
        ds = probs * (dp - jnp.sum(dp * probs, axis=-1, keepdims=True)) * SCALE
        ds = ds.astype(BF16)
        dqkv_ref[:, at:at + HEAD_DIM] = dot(ds, k).astype(BF16)
        dqkv_ref[:, hd + at:hd + at + HEAD_DIM] = dot(ds, q, TN).astype(BF16)
    for n in range(0, width, 512):
        cols = pl.ds(n, 512)
        du_ref[:, cols] = dot(dqkv_ref[...], wq_ref[cols, :], NT).astype(BF16)
    gain = gain_ref[...].astype(F32)
    dgain = jnp.zeros((8, width), F32)
    for start in range(0, rows, CHUNK):
        part = pl.ds(start, CHUNK)
        mean = st_ref[part, 0:1]
        rstd = st_ref[part, 128:129]
        xhat = (h_ref[part, :].astype(F32) - mean) * rstd
        du = du_ref[part, :].astype(F32)
        prod = du * xhat
        for piece in range(0, CHUNK, 8):
            dgain = dgain + prod[piece:piece + 8]
        dx = du * gain
        first = jnp.sum(dx, axis=-1, keepdims=True) * (1.0 / width)
        second = jnp.sum(dx * xhat, axis=-1, keepdims=True) * (1.0 / width)
        e = rstd * (dx - first - xhat * second) + g_ref[part, :].astype(F32)
        e_ref[part, :] = e.astype(BF16)
    dg_ref[...] = dgain


def shape_v(shape, dtype):
    return pltpu.VMEM(shape, dtype)


def params(mib):
    return pltpu.CompilerParams(vmem_limit_bytes=mib << 20)


def cost(us):
    return pl.CostEstimate(flops=int(us * 1e9), bytes_accessed=int(us * 1e5), transcendentals=0)


def first_kernel(parity, offs, gain, wq, wo, h):
    rows, width = h.shape

    def body(parity_ref, offs_ref, gain_ref, wq_ref, wo_ref, h_ref, *outs):
        mask_ref = outs[0]
        mask_ref[...] = mask_body(parity_ref[0], offs_ref, rows)
        forward_body(h_ref, gain_ref, wq_ref, wo_ref, mask_ref, *outs[1:])

    return pl.pallas_call(
        body,
        in_specs=[SM, SM, VM, VM, VM, VM],
        out_specs=[VM] * 7,
        out_shape=[shape_v((rows, rows), F32)] + forward_outs(rows, width),
        compiler_params=params(24),
        cost_estimate=cost(2),
        name="first",
    )(parity, offs, gain, wq, wo, h)


def forward_outs(rows, width):
    hd = HEADS_DEV * HEAD_DIM
    return [
        shape_v((rows, width), BF16),
        shape_v((rows, width), BF16),
        shape_v((rows, 3 * hd), BF16),
        shape_v((HEADS_DEV, rows, rows), F32),
        shape_v((rows, hd), BF16),
        shape_v((rows, 256), F32),
    ]


def forward_kernel(h, gain, wq, wo, mask):
    rows, width = h.shape
    return pl.pallas_call(
        forward_body,
        in_specs=[VM] * 5,
        out_specs=[VM] * 6,
        out_shape=forward_outs(rows, width),
        compiler_params=params(24),
        cost_estimate=cost(2),
        name="forward",
    )(h, gain, wq, wo, mask)


def backward_kernel(g, h, gain, wq, wo, saved):
    rows, width = h.shape
    hd = HEADS_DEV * HEAD_DIM
    u, qkv, probs, att, stats = saved
    e, dqkv, dgain = pl.pallas_call(
        backward_body,
        in_specs=[VM] * 8,
        out_specs=[VM] * 3,
        out_shape=[shape_v((rows, width), BF16), shape_v((rows, 3 * hd), BF16), shape_v((8, width), F32)],
        scratch_shapes=[pltpu.VMEM((rows, width), BF16)],
        compiler_params=params(24),
        cost_estimate=cost(3),
        name="backward",
    )(g, h, gain, wq, wo, qkv, probs, stats)
    return e, (u, dqkv, att, g, dgain)


def weight_kernel(uses):
    rows, width = uses[0][0].shape
    hd = HEADS_DEV * HEAD_DIM
    count = len(uses)
    step = 256

    def body(*refs):
        ins, (gain_out, wq_out, wo_out) = refs[:5 * count], refs[5 * count:5 * count + 3]
        use = [ins[5 * i:5 * i + 5] for i in range(count)]
        total = use[0][4][...]
        for i in range(1, count):
            total = total + use[i][4][...]
        gain_out[...] = jnp.sum(total, axis=0, keepdims=True).astype(BF16)
        att = jnp.concatenate([r[2][...] for r in use], axis=0)
        for n in range(0, width, 512):
            g = jnp.concatenate([r[3][:, n:n + 512] for r in use], axis=0)
            wo_out[:, n:n + 512] = dot(att, g, TN).astype(BF16)
        dqkv = jnp.concatenate([r[1][...] for r in use], axis=0)
        for m in range(0, width, step):
            u = jnp.concatenate([r[0][:, m:m + step] for r in use], axis=0)
            wq_out[m:m + step, :] = dot(u, dqkv, TN).astype(BF16)

    flat = [leaf for use in uses for leaf in use]
    return pl.pallas_call(
        body,
        in_specs=[VM] * len(flat),
        out_specs=[VM] * 3,
        out_shape=[
            jax.ShapeDtypeStruct((1, width), BF16),
            jax.ShapeDtypeStruct((width, 3 * hd), BF16),
            jax.ShapeDtypeStruct((hd, width), BF16),
        ],
        compiler_params=params(32),
        cost_estimate=cost(4),
        name="weights",
    )(*flat)


def shards(acts_down, acts_up, cotangent_down, cotangent_up, ln_gain, w_qkv, w_out, band_offsets):
    sections = lax.axis_size("section")
    index = lax.axis_index("section")
    odd = index % 2 == 1
    parity = (index % 2).astype(jnp.int32).reshape(1)
    near = [(i, i ^ 1) for i in range(sections)]
    far = [(i, (i + (1 if i % 2 else -1)) % sections) for i in range(sections)]

    def swap_near(x):
        return lax.ppermute(x, "section", near)

    def swap_far(x):
        return lax.ppermute(x, "section", far)

    gain, wq, wo = ln_gain, w_qkv[0], w_out[0]
    a0 = jnp.where(odd, acts_down[0], acts_up[0])
    b0 = jnp.where(odd, acts_up[0], acts_down[0])
    cot_a = jnp.where(odd, cotangent_down[0], cotangent_up[0])
    cot_b = jnp.where(odd, cotangent_up[0], cotangent_down[0])

    mask, a1_out, *a0_saved = first_kernel(parity, band_offsets, gain, wq, wo, a0)
    a1 = swap_far(a1_out)
    b1_out, *b0_saved = forward_kernel(b0, gain, wq, wo, mask)
    b1 = swap_near(b1_out)
    b2_out, *b1_saved = forward_kernel(b1, gain, wq, wo, mask)
    b2 = swap_far(b2_out)
    a2_out, *a1_saved = forward_kernel(a1, gain, wq, wo, mask)
    a2 = swap_near(a2_out)
    out_a, *a2_saved = forward_kernel(a2, gain, wq, wo, mask)
    ea2, use_a2 = backward_kernel(cot_a, a2, gain, wq, wo, a2_saved)
    ca1 = swap_near(ea2)
    ea1, use_a1 = backward_kernel(ca1, a1, gain, wq, wo, a1_saved)
    ca0 = swap_far(ea1)
    out_b, *b2_saved = forward_kernel(b2, gain, wq, wo, mask)
    eb2, use_b2 = backward_kernel(cot_b, b2, gain, wq, wo, b2_saved)
    cb1 = swap_far(eb2)
    eb1, use_b1 = backward_kernel(cb1, b1, gain, wq, wo, b1_saved)
    cb0 = swap_near(eb1)
    ea0, use_a0 = backward_kernel(ca0, a0, gain, wq, wo, a0_saved)
    eb0, use_b0 = backward_kernel(cb0, b0, gain, wq, wo, b0_saved)
    d_gain, d_wq, d_wo = weight_kernel([use_a2, use_a1, use_b2, use_b1, use_a0, use_b0])
    out_down = jnp.where(odd, out_a, out_b)
    out_up = jnp.where(odd, out_b, out_a)
    back_down = jnp.where(odd, ea0, eb0)
    back_up = jnp.where(odd, eb0, ea0)
    return (
        out_down[None], out_up[None], back_down[None], back_up[None], d_gain, d_wq[None], d_wo[None],
    )


def solution(mesh):
    both = ("groups", "section")
    in_specs = (
        P(both, None, None), P(both, None, None), P(both, None, None), P(both, None, None),
        P("section", None), P("section", None, None), P("section", None, None), P(),
    )
    out_specs = (
        P(both, None, None), P(both, None, None), P(both, None, None), P(both, None, None),
        P(both, None), P(both, None, None), P(both, None, None),
    )
    return jax.shard_map(shards, mesh=mesh, in_specs=in_specs, out_specs=out_specs, check_vma=False)
```

profile of v0, /device:TPU:1, one launch (start us, length us, event | category | flops | bytes accessed | tf_op | source)
XLA Modules:
  0.0 85.3 jit_solution(11731285070809000801)
XLA Ops:
  1.4 1.3 %select_bitcast_fusion.6 = (bf16[128,2048]{1,0:T(8,128)(2,1)S(1)}, bf16[128,2048]{1,0:T(8,128)(2,1)S(1)}) fusion(bf16[1,128,2048]{2,1,0:T(8,128)(2,1)} %param.9, bf16[1,128,2048]{2,1,0:T(8,128)(2,1)} %param.8, pred[]{:T(512)S(6)} %eq.6), kind=kLoop, calls=%fused_computation.6 | loop fusion | flops 524288 | bytes 2097153 | tf_op jit(solution)/shard_map/jit(_where)/select_n | solution.py:238
  2.7 1.9 %copy-done = bf16[1,2048,768]{2,1,0:T(8,128)(2,1)S(1)} copy-done((bf16[1,2048,768]{2,1,0:T(8,128)(2,1)S(1)}, bf16[1,2048,768]{2,1,0:T(8,128)(2,1)}, u32[]{:S(2)}) %copy-start) | copy-done | bytes 3145752
  4.6 1.2 %copy-done.2 = bf16[1,256,2048]{2,1,0:T(8,128)(2,1)S(1)} copy-done((bf16[1,256,2048]{2,1,0:T(8,128)(2,1)S(1)}, bf16[1,256,2048]{2,1,0:T(8,128)(2,1)}, u32[]{:S(2)}) %copy-start.2) | copy-done | bytes 1048600
  6.5 2.3 %first.1 = (f32[128,128]{1,0:T(8,128)S(1)}, bf16[128,2048]{1,0:T(8,128)(2,1)S(1)}, bf16[128,2048]{1,0:T(8,128)(2,1)S(1)}, bf16[128,768]{1,0:T(8,128)(2,1)S(1)}, ...) custom-call(s32[1]{0:T(128)} %bitcast.parity_ref, s32[4,2]{1,0:T(4,128)S(1)} %copy.15.offs_ref, ...), custom_call_target="tpu_custom_call" | custom-call | flops 2000000000 | bytes 200000 | tf_op jit(solution)/shard_map/first/pallas_call | solution.py:131
  8.9 1.8 %forward.7 = (bf16[128,2048]{1,0:T(8,128)(2,1)S(1)}, bf16[128,2048]{1,0:T(8,128)(2,1)S(1)}, bf16[128,768]{1,0:T(8,128)(2,1)S(1)}, f32[2,128,128]{2,1,0:T(8,128)S...) custom-call(bf16[128,2048]{1,0:T(8,128)(2,1)S(1)} %get-tuple-element.129.h_ref, bf16[1,2048]{1,0:T(2,128)(2,1)S(1)} %copy-done.4, ...), custom_call_target="tpu_custom_call" | custom-call | flops 2000000000 | bytes 200000 | tf_op jit(solution)/shard_map/forward/pallas_call | solution.py:156
  10.8 2.7 %collective-permute-start = (bf16[128,2048]{1,0:T(8,128)(2,1)S(1)}, bf16[128,2048]{1,0:T(8,128)(2,1)S(1)}, u32[]{:S(2)}, u32[]{:S(2)}) collective-permute-start(bf16[128,2048]{1,0:T(8,128)(2,1)S(1)} %get-tuple-element.65), channel_id=1, source_target_pairs={{0,15},{1,2},{2,1},{3,4},{4,3},{5,6},{6,5},{7,8},{8,7},{9,10},{10,... | collective-permute-start | bytes 1572872 | tf_op jit(solution)/shard_map/ppermute | solution.py:234
  13.4 1.8 %forward.8 = (bf16[128,2048]{1,0:T(8,128)(2,1)S(1)}, bf16[128,2048]{1,0:T(8,128)(2,1)S(1)}, bf16[128,768]{1,0:T(8,128)(2,1)S(1)}, f32[2,128,128]{2,1,0:T(8,128)S...) custom-call(bf16[128,2048]{1,0:T(8,128)(2,1)S(1)} %collective-permute-done.2.h_ref, ...), custom_call_target="tpu_custom_call" | custom-call | flops 2000000000 | bytes 200000 | tf_op jit(solution)/shard_map/forward/pallas_call | solution.py:156
  15.2 1.9 %collective-permute-start.3 = (bf16[128,2048]{1,0:T(8,128)(2,1)S(1)}, bf16[128,2048]{1,0:T(8,128)(2,1)S(1)}, u32[]{:S(2)}, u32[]{:S(2)}) collective-permute-start(bf16[128,2048]{1,0:T(8,128)(2,1)S(1)} %get-tuple-element.70), channel_id=1, source_target_pairs={{0,15},{1,2},{2,1},{3,4},{4,3},{5,6},{6,5},{7,8},{8,7},{9,10},{10,... | collective-permute-start | bytes 1572872 | tf_op jit(solution)/shard_map/ppermute | solution.py:234
  17.1 14.4 %collective-permute-done.h_ref = bf16[128,2048]{1,0:T(8,128)(2,1)S(1)} collective-permute-done((bf16[128,2048]{1,0:T(8,128)(2,1)S(1)}, bf16[128,2048]{1,0:T(8,128)(2,1)S(1)}, u32[]{:S(2)}, u32[]{:S(2)}) %collective-permute-start) | collective-permute-done | bytes 524320 | tf_op jit(solution)/shard_map/ppermute | solution.py:234
  31.5 1.8 %forward.5 = (bf16[128,2048]{1,0:T(8,128)(2,1)S(1)}, bf16[128,2048]{1,0:T(8,128)(2,1)S(1)}, bf16[128,768]{1,0:T(8,128)(2,1)S(1)}, f32[2,128,128]{2,1,0:T(8,128)S...) custom-call(bf16[128,2048]{1,0:T(8,128)(2,1)S(1)} %collective-permute-done.h_ref, ...), custom_call_target="tpu_custom_call" | custom-call | flops 2000000000 | bytes 200000 | tf_op jit(solution)/shard_map/forward/pallas_call | solution.py:156
  33.5 3.7 %collective-permute-done.3.h_ref = bf16[128,2048]{1,0:T(8,128)(2,1)S(1)} collective-permute-done((bf16[128,2048]{1,0:T(8,128)(2,1)S(1)}, bf16[128,2048]{1,0:T(8,128)(2,1)S(1)}, u32[]{:S(2)}, u32[]{:S(2)}) %collective-permute-start.3) | collective-permute-done | bytes 524320 | tf_op jit(solution)/shard_map/ppermute | solution.py:234
  37.1 1.8 %forward.9 = (bf16[128,2048]{1,0:T(8,128)(2,1)S(1)}, bf16[128,2048]{1,0:T(8,128)(2,1)S(1)}, bf16[128,768]{1,0:T(8,128)(2,1)S(1)}, f32[2,128,128]{2,1,0:T(8,128)S...) custom-call(bf16[128,2048]{1,0:T(8,128)(2,1)S(1)} %collective-permute-done.3.h_ref, ...), custom_call_target="tpu_custom_call" | custom-call | flops 2000000000 | bytes 200000 | tf_op jit(solution)/shard_map/forward/pallas_call | solution.py:156
  38.9 2.9 %backward.9 = (bf16[128,2048]{1,0:T(8,128)(2,1)S(1)}, bf16[128,768]{1,0:T(8,128)(2,1)S(1)}, f32[8,2048]{1,0:T(8,128)S(1)}) custom-call(bf16[128,2048]{1,0:T(8,128)(2,1)S(1)} %get-tuple-element.125.g_ref.refs_13_, bf16[128,2048]{1,0:T(8,128)(2,1)S(1)} %collective-permute-done.3.h_ref, bf16[1,2048]{1,0:T(2,128)(2,1)S(1)} %copy-done.4, ...), custom_call_target="tpu_custom_call" | custom-call | flops 3000000000 | bytes 300000 | tf_op jit(solution)/shard_map/backward/pallas_call | solution.py:171
  41.9 1.8 %collective-permute-start.6 = (bf16[128,2048]{1,0:T(8,128)(2,1)S(1)}, bf16[128,2048]{1,0:T(8,128)(2,1)S(1)}, u32[]{:S(2)}, u32[]{:S(2)}) collective-permute-start(bf16[128,2048]{1,0:T(8,128)(2,1)S(1)} %get-tuple-element.87), channel_id=1, source_target_pairs={{0,15},{1,2},{2,1},{3,4},{4,3},{5,6},{6,5},{7,8},{8,7},{9,10},{10,... | collective-permute-start | bytes 1572872 | tf_op jit(solution)/shard_map/ppermute | solution.py:234
  43.7 1.8 %forward.6 = (bf16[128,2048]{1,0:T(8,128)(2,1)S(1)}, bf16[128,2048]{1,0:T(8,128)(2,1)S(1)}, bf16[128,768]{1,0:T(8,128)(2,1)S(1)}, f32[2,128,128]{2,1,0:T(8,128)S...) custom-call(bf16[128,2048]{1,0:T(8,128)(2,1)S(1)} %collective-permute-done.1.h_ref, ...), custom_call_target="tpu_custom_call" | custom-call | flops 2000000000 | bytes 200000 | tf_op jit(solution)/shard_map/forward/pallas_call | solution.py:156
  45.5 2.9 %backward.6 = (bf16[128,2048]{1,0:T(8,128)(2,1)S(1)}, bf16[128,768]{1,0:T(8,128)(2,1)S(1)}, f32[8,2048]{1,0:T(8,128)S(1)}) custom-call(bf16[128,2048]{1,0:T(8,128)(2,1)S(1)} %get-tuple-element.126.g_ref.refs_3_, bf16[128,2048]{1,0:T(8,128)(2,1)S(1)} %collective-permute-done.1.h_ref, bf16[1,2048]{1,0:T(2,128)(2,1)S(1)} %copy-done.4, ...), custom_call_target="tpu_custom_call" | custom-call | flops 3000000000 | bytes 300000 | tf_op jit(solution)/shard_map/backward/pallas_call | solution.py:171
  48.5 6.9 %collective-permute-done.6.g_ref.refs_18_ = bf16[128,2048]{1,0:T(8,128)(2,1)S(1)} collective-permute-done((bf16[128,2048]{1,0:T(8,128)(2,1)S(1)}, bf16[128,2048]{1,0:T(8,128)(2,1)S(1)}, u32[]{:S(2)}, u32[]{:S(2)}) %collective-permute-start.6) | collective-permute-done | bytes 524320 | tf_op jit(solution)/shard_map/ppermute | solution.py:234
  55.3 3.1 %backward.10 = (bf16[128,2048]{1,0:T(8,128)(2,1)S(1)}, bf16[128,768]{1,0:T(8,128)(2,1)S(1)}, f32[8,2048]{1,0:T(8,128)S(1)}) custom-call(bf16[128,2048]{1,0:T(8,128)(2,1)S(1)} %collective-permute-done.6.g_ref.refs_18_, bf16[128,2048]{1,0:T(8,128)(2,1)S(1)} %collective-permute-done.2.h_ref, bf16[1,2048]{1,0:T(2,128)(2,1)S(1)} %copy-done.4, ...), custom_call_target="tpu_custom_call" | custom-call | flops 3000000000 | bytes 300000 | tf_op jit(solution)/shard_map/backward/pallas_call | solution.py:171
  58.5 2.9 %backward.7 = (bf16[128,2048]{1,0:T(8,128)(2,1)S(1)}, bf16[128,768]{1,0:T(8,128)(2,1)S(1)}, f32[8,2048]{1,0:T(8,128)S(1)}) custom-call(bf16[128,2048]{1,0:T(8,128)(2,1)S(1)} %collective-permute-done.4.g_ref.refs_8_, bf16[128,2048]{1,0:T(8,128)(2,1)S(1)} %collective-permute-done.h_ref, bf16[1,2048]{1,0:T(2,128)(2,1)S(1)} %copy-done.4, ...), custom_call_target="tpu_custom_call" | custom-call | flops 3000000000 | bytes 300000 | tf_op jit(solution)/shard_map/backward/pallas_call | solution.py:171
  63.0 2.9 %backward.11 = (bf16[128,2048]{1,0:T(8,128)(2,1)S(1)}, bf16[128,768]{1,0:T(8,128)(2,1)S(1)}, f32[8,2048]{1,0:T(8,128)S(1)}) custom-call(bf16[128,2048]{1,0:T(8,128)(2,1)S(1)} %collective-permute-done.7.g_ref.refs_28_, bf16[128,2048]{1,0:T(8,128)(2,1)S(1)} %get-tuple-element.129.h_ref, bf16[1,2048]{1,0:T(2,128)(2,1)S(1)} %copy-done.4, ...), custom_call_target="tpu_custom_call" | custom-call | flops 3000000000 | bytes 300000 | tf_op jit(solution)/shard_map/backward/pallas_call | solution.py:171
  66.0 9.8 %collective-permute-done.5.g_ref.refs_23_ = bf16[128,2048]{1,0:T(8,128)(2,1)S(1)} collective-permute-done((bf16[128,2048]{1,0:T(8,128)(2,1)S(1)}, bf16[128,2048]{1,0:T(8,128)(2,1)S(1)}, u32[]{:S(2)}, u32[]{:S(2)}) %collective-permute-start.5) | collective-permute-done | bytes 524320 | tf_op jit(solution)/shard_map/ppermute | solution.py:234
  75.8 2.9 %backward.8 = (bf16[128,2048]{1,0:T(8,128)(2,1)S(1)}, bf16[128,768]{1,0:T(8,128)(2,1)S(1)}, f32[8,2048]{1,0:T(8,128)S(1)}) custom-call(bf16[128,2048]{1,0:T(8,128)(2,1)S(1)} %collective-permute-done.5.g_ref.refs_23_, bf16[128,2048]{1,0:T(8,128)(2,1)S(1)} %get-tuple-element.130.h_ref, bf16[1,2048]{1,0:T(2,128)(2,1)S(1)} %copy-done.4, ...), custom_call_target="tpu_custom_call" | custom-call | flops 3000000000 | bytes 300000 | tf_op jit(solution)/shard_map/backward/pallas_call | solution.py:171
  78.7 1.0 %select_bitcast_fusion = (bf16[1,128,2048]{2,1,0:T(8,128)(2,1)}, bf16[1,128,2048]{2,1,0:T(8,128)(2,1)}) fusion(bf16[128,2048]{1,0:T(8,128)(2,1)S(1)} %get-tuple-element.95, bf16[128,2048]{1,0:T(8,128)(2,1)S(1)} %get-tuple-element.83, pred[]{:T(512)S(6)} %eq.6), kind=kLoop, calls=%fused_computation | loop fusion | flops 524288 | bytes 2097153 | tf_op jit(solution)/shard_map/broadcast_in_dim | solution.py:268
  79.8 5.5 %weights.1 = (bf16[1,2048]{1,0:T(2,128)(2,1)}, bf16[2048,768]{1,0:T(8,128)(2,1)}, bf16[256,2048]{1,0:T(8,128)(2,1)}) custom-call(bf16[128,2048]{1,0:T(8,128)(2,1)S(1)} %get-tuple-element.96.refs_0_, bf16[128,768]{1,0:T(8,128)(2,1)S(1)} %get-tuple-element.97.refs_1_, bf16[128,256]{1,0:T(8,128)(2,1)S(1)} %get-tuple-element.98.refs_2_, ...), custom_call_target="tpu_custom_call" | custom-call | flops 4000000000 | bytes 400000 | tf_op jit(solution)/shard_map/weights/pallas_call | solution.py:207
  (24 shorter events, 3.5 us)
Async XLA Ops:
  2.7 1.9 %copy-start = (bf16[1,2048,768]{2,1,0:T(8,128)(2,1)S(1)}, bf16[1,2048,768]{2,1,0:T(8,128)(2,1)}, u32[]{:S(2)}) copy-start(bf16[1,2048,768]{2,1,0:T(8,128)(2,1)} %param.13) | copy-start | bytes 9437188
  4.6 1.2 %copy-start.2 = (bf16[1,256,2048]{2,1,0:T(8,128)(2,1)S(1)}, bf16[1,256,2048]{2,1,0:T(8,128)(2,1)}, u32[]{:S(2)}) copy-start(bf16[1,256,2048]{2,1,0:T(8,128)(2,1)} %param.14) | copy-start | bytes 3145732
  5.8 0.7 copy-start.4
  6.5 2.3 %copy-start.1 = (bf16[1,2048,768]{2,1,0:T(8,128)(2,1)S(1)}, bf16[1,2048,768]{2,1,0:T(8,128)(2,1)}, u32[]{:S(2)}) copy-start(bf16[1,2048,768]{2,1,0:T(8,128)(2,1)} %param.13) | copy-start | bytes 9437188
  6.5 2.3 %copy-start.3 = (bf16[1,256,2048]{2,1,0:T(8,128)(2,1)S(1)}, bf16[1,256,2048]{2,1,0:T(8,128)(2,1)}, u32[]{:S(2)}) copy-start(bf16[1,256,2048]{2,1,0:T(8,128)(2,1)} %param.14) | copy-start | bytes 3145732
  10.6 2.8 %collective-permute-start.2 = (bf16[128,2048]{1,0:T(8,128)(2,1)S(1)}, bf16[128,2048]{1,0:T(8,128)(2,1)S(1)}, u32[]{:S(2)}, u32[]{:S(2)}) collective-permute-start(bf16[128,2048]{1,0:T(8,128)(2,1)S(1)} %get-tuple-element.69), channel_id=1, source_target_pairs={{0,1},{1,0},{2,3},{3,2},{4,5},{5,4},{6,7},{7,6},{8,9},{9,8},{10,11... | collective-permute-start | bytes 1572872 | tf_op jit(solution)/shard_map/ppermute | solution.py:231
  10.8 20.8 %collective-permute-start = (bf16[128,2048]{1,0:T(8,128)(2,1)S(1)}, bf16[128,2048]{1,0:T(8,128)(2,1)S(1)}, u32[]{:S(2)}, u32[]{:S(2)}) collective-permute-start(bf16[128,2048]{1,0:T(8,128)(2,1)S(1)} %get-tuple-element.65), channel_id=1, source_target_pairs={{0,15},{1,2},{2,1},{3,4},{4,3},{5,6},{6,5},{7,8},{8,7},{9,10},{10,... | collective-permute-start | bytes 1572872 | tf_op jit(solution)/shard_map/ppermute | solution.py:234
  15.2 18.2 %copy-start.5 = (bf16[1,128,2048]{2,1,0:T(8,128)(2,1)S(1)}, bf16[1,128,2048]{2,1,0:T(8,128)(2,1)}, u32[]{:S(2)}) copy-start(bf16[1,128,2048]{2,1,0:T(8,128)(2,1)} %param.11) | copy-start | bytes 1572868
  15.2 18.2 %copy-start.6 = (bf16[1,128,2048]{2,1,0:T(8,128)(2,1)S(1)}, bf16[1,128,2048]{2,1,0:T(8,128)(2,1)}, u32[]{:S(2)}) copy-start(bf16[1,128,2048]{2,1,0:T(8,128)(2,1)} %param.10) | copy-start | bytes 1572868
  15.2 21.9 %collective-permute-start.3 = (bf16[128,2048]{1,0:T(8,128)(2,1)S(1)}, bf16[128,2048]{1,0:T(8,128)(2,1)S(1)}, u32[]{:S(2)}, u32[]{:S(2)}) collective-permute-start(bf16[128,2048]{1,0:T(8,128)(2,1)S(1)} %get-tuple-element.70), channel_id=1, source_target_pairs={{0,15},{1,2},{2,1},{3,4},{4,3},{5,6},{6,5},{7,8},{8,7},{9,10},{10,... | collective-permute-start | bytes 1572872 | tf_op jit(solution)/shard_map/ppermute | solution.py:234
  33.3 10.4 %collective-permute-start.1 = (bf16[128,2048]{1,0:T(8,128)(2,1)S(1)}, bf16[128,2048]{1,0:T(8,128)(2,1)S(1)}, u32[]{:S(2)}, u32[]{:S(2)}) collective-permute-start(bf16[128,2048]{1,0:T(8,128)(2,1)S(1)} %get-tuple-element.67), channel_id=1, source_target_pairs={{0,1},{1,0},{2,3},{3,2},{4,5},{5,4},{6,7},{7,6},{8,9},{9,8},{10,11... | collective-permute-start | bytes 1572872 | tf_op jit(solution)/shard_map/ppermute | solution.py:231
  41.9 13.5 %collective-permute-start.6 = (bf16[128,2048]{1,0:T(8,128)(2,1)S(1)}, bf16[128,2048]{1,0:T(8,128)(2,1)S(1)}, u32[]{:S(2)}, u32[]{:S(2)}) collective-permute-start(bf16[128,2048]{1,0:T(8,128)(2,1)S(1)} %get-tuple-element.87), channel_id=1, source_target_pairs={{0,15},{1,2},{2,1},{3,4},{4,3},{5,6},{6,5},{7,8},{8,7},{9,10},{10,... | collective-permute-start | bytes 1572872 | tf_op jit(solution)/shard_map/ppermute | solution.py:234
  48.4 10.1 %collective-permute-start.4 = (bf16[128,2048]{1,0:T(8,128)(2,1)S(1)}, bf16[128,2048]{1,0:T(8,128)(2,1)S(1)}, u32[]{:S(2)}, u32[]{:S(2)}) collective-permute-start(bf16[128,2048]{1,0:T(8,128)(2,1)S(1)} %get-tuple-element.75), channel_id=1, source_target_pairs={{0,1},{1,0},{2,3},{3,2},{4,5},{5,4},{6,7},{7,6},{8,9},{9,8},{10,11... | collective-permute-start | bytes 1572872 | tf_op jit(solution)/shard_map/ppermute | solution.py:231
  58.4 4.6 %collective-permute-start.7 = (bf16[128,2048]{1,0:T(8,128)(2,1)S(1)}, bf16[128,2048]{1,0:T(8,128)(2,1)S(1)}, u32[]{:S(2)}, u32[]{:S(2)}) collective-permute-start(bf16[128,2048]{1,0:T(8,128)(2,1)S(1)} %get-tuple-element.91), channel_id=1, source_target_pairs={{0,1},{1,0},{2,3},{3,2},{4,5},{5,4},{6,7},{7,6},{8,9},{9,8},{10,11... | collective-permute-start | bytes 1572872 | tf_op jit(solution)/shard_map/ppermute | solution.py:231
  61.5 14.3 %collective-permute-start.5 = (bf16[128,2048]{1,0:T(8,128)(2,1)S(1)}, bf16[128,2048]{1,0:T(8,128)(2,1)S(1)}, u32[]{:S(2)}, u32[]{:S(2)}) collective-permute-start(bf16[128,2048]{1,0:T(8,128)(2,1)S(1)} %get-tuple-element.79), channel_id=1, source_target_pairs={{0,15},{1,2},{2,1},{3,4},{4,3},{5,6},{6,5},{7,8},{8,7},{9,10},{10,... | collective-permute-start | bytes 1572872 | tf_op jit(solution)/shard_map/ppermute | solution.py:234
where the time goes:
time: 85.5 us; the launch traced here: 85.3 us
  waiting for transfers between devices  34.7 us (41%)
  Pallas kernels  34.5 us (40%)
  starting transfers between devices  7.22 us (8%)
  local copies, waits for them, and re-layouts  4.59 us (5%)
  other arithmetic  3.42 us (4%)
    ppermute x4, waiting for transfers between devices, swap_far(): return lax.ppermute(x, 'section', far)  34.7 us
    pallas_call x6, Pallas kernels, backward_kernel(): pl.pallas_call(backward_body, in_specs=[VM] * 8, out_specs=[VM] * 3, out_...  17.8 us
    pallas_call x5, Pallas kernels, forward_kernel(): pl.pallas_call(forward_body, in_specs=[VM] * 5, out_specs=[VM] * 6, out_s...  8.88 us
    ppermute x4, starting transfers between devices, swap_far(): return lax.ppermute(x, 'section', far)  6.89 us
    pallas_call x1, Pallas kernels, weight_kernel(): pl.pallas_call(body, in_specs=[VM] * len(flat), out_specs=[VM] * 3, out_s...  5.5 us
    unnamed x15, local copies, waits for them, and re-layouts  4.59 us
    pallas_call x1, Pallas kernels, first_kernel(): pl.pallas_call(body, in_specs=[SM, SM, VM, VM, VM, VM], out_specs=[VM] *...  2.33 us
  transfers between devices with their start and end apart: 8, of which 4 were waited for; matrix products, arithmetic and copies ran while one was open for 1% of the time, Pallas kernels for 26%

commit v1 on v0

v1 whole, which is shorter than its diff:
```python
import math

import jax
import jax.numpy as jnp
from jax import lax
from jax.experimental import pallas as pl
from jax.experimental.pallas import tpu as pltpu
from jax.sharding import PartitionSpec as P

HEADS_DEV = 2
HEAD_DIM = 128
BLOCK = 32
CHUNK = 16
F32 = jnp.float32
BF16 = jnp.bfloat16
NT = (((1,), (1,)), ((), ()))
TN = (((0,), (0,)), ((), ()))
SCALE = 1.0 / math.sqrt(HEAD_DIM)
VM = pl.BlockSpec(memory_space=pltpu.VMEM)
FWD_COST = 0.002
BWD_COST = 0.003
W_COST = 0.004


def dot(a, b, dims=(((1,), (0,)), ((), ()))):
    return lax.dot_general(a, b, dims, preferred_element_type=F32)


def mask_body(odd, offs_ref, rows):
    row = lax.broadcasted_iota(jnp.int32, (rows, rows), 0)
    col = lax.broadcasted_iota(jnp.int32, (rows, rows), 1)
    row_block = row // BLOCK
    col_block = col // BLOCK
    near = row_block == col_block
    for block in range(offs_ref.shape[1]):
        for listed in range(offs_ref.shape[0]):
            near = near | ((row_block == block) & (col_block == block - offs_ref[listed, block]))
    keep = (col <= row) & (near | jnp.logical_not(odd))
    return jnp.where(keep, 1.0, 0.0).astype(F32)


def forward_body(h_ref, gain_ref, wq_ref, wo_ref, mask_ref, out_ref, u_ref, qkv_ref, p_ref, att_ref, st_ref, waits=None):
    rows, width = h_ref.shape
    hd = HEADS_DEV * HEAD_DIM
    gain = gain_ref[...].astype(F32)
    for start in range(0, rows, CHUNK):
        part = pl.ds(start, CHUNK)
        x = h_ref[part, :].astype(F32)
        mean = jnp.sum(x, axis=-1, keepdims=True) * (1.0 / width)
        centred = x - mean
        rstd = lax.rsqrt(jnp.sum(centred * centred, axis=-1, keepdims=True) * (1.0 / width) + 1e-05)
        u_ref[part, :] = (centred * rstd * gain).astype(BF16)
        st_ref[part, :] = jnp.concatenate(
            [jnp.broadcast_to(mean, (CHUNK, 128)), jnp.broadcast_to(rstd, (CHUNK, 128))], axis=1)
    for n in range(3):
        if waits:
            waits[n].wait()
        qkv_ref[:, n * hd:(n + 1) * hd] = dot(u_ref[...], wq_ref[:, n * hd:(n + 1) * hd]).astype(BF16)
    keep = mask_ref[...]
    for head in range(HEADS_DEV):
        at = head * HEAD_DIM
        q = qkv_ref[:, at:at + HEAD_DIM]
        k = qkv_ref[:, hd + at:hd + at + HEAD_DIM]
        v = qkv_ref[:, 2 * hd + at:2 * hd + at + HEAD_DIM]
        weighted = jnp.where(keep > 0.0, jnp.exp(dot(q, k, NT) * SCALE), 0.0)
        probs = weighted / jnp.sum(weighted, axis=-1, keepdims=True)
        p_ref[head] = probs
        att_ref[:, at:at + HEAD_DIM] = dot(probs.astype(BF16), v).astype(BF16)
    if waits:
        waits[3].wait()
    for n in range(0, width, 512):
        cols = pl.ds(n, 512)
        out_ref[:, cols] = (h_ref[:, cols].astype(F32) + dot(att_ref[...], wo_ref[:, cols])).astype(BF16)


def backward_body(g_ref, h_ref, gain_ref, wq_ref, wo_ref, qkv_ref, p_ref, st_ref, e_ref, dqkv_ref, dg_ref, du_ref):
    rows, width = h_ref.shape
    hd = HEADS_DEV * HEAD_DIM
    datt = dot(g_ref[...], wo_ref[...], NT).astype(BF16)
    for head in range(HEADS_DEV):
        at = head * HEAD_DIM
        q = qkv_ref[:, at:at + HEAD_DIM]
        k = qkv_ref[:, hd + at:hd + at + HEAD_DIM]
        v = qkv_ref[:, 2 * hd + at:2 * hd + at + HEAD_DIM]
        probs = p_ref[head]
        da = datt[:, at:at + HEAD_DIM]
        dp = dot(da, v, NT).astype(BF16).astype(F32)
        dqkv_ref[:, 2 * hd + at:2 * hd + at + HEAD_DIM] = dot(probs.astype(BF16), da, TN).astype(BF16)
        ds = probs * (dp - jnp.sum(dp * probs, axis=-1, keepdims=True)) * SCALE
        ds = ds.astype(BF16)
        dqkv_ref[:, at:at + HEAD_DIM] = dot(ds, k).astype(BF16)
        dqkv_ref[:, hd + at:hd + at + HEAD_DIM] = dot(ds, q, TN).astype(BF16)
    for n in range(0, width, 512):
        cols = pl.ds(n, 512)
        du_ref[:, cols] = dot(dqkv_ref[...], wq_ref[cols, :], NT).astype(BF16)
    gain = gain_ref[...].astype(F32)
    dgain = jnp.zeros((8, width), F32)
    for start in range(0, rows, CHUNK):
        part = pl.ds(start, CHUNK)
        mean = st_ref[part, 0:1]
        rstd = st_ref[part, 128:129]
        xhat = (h_ref[part, :].astype(F32) - mean) * rstd
        du = du_ref[part, :].astype(F32)
        prod = du * xhat
        for piece in range(0, CHUNK, 8):
            dgain = dgain + prod[piece:piece + 8]
        dx = du * gain
        first = jnp.sum(dx, axis=-1, keepdims=True) * (1.0 / width)
        second = jnp.sum(dx * xhat, axis=-1, keepdims=True) * (1.0 / width)
        e = rstd * (dx - first - xhat * second) + g_ref[part, :].astype(F32)
        e_ref[part, :] = e.astype(BF16)
    dg_ref[...] = dgain


def shape_v(shape, dtype):
    return pltpu.VMEM(shape, dtype)


def params(mib):
    return pltpu.CompilerParams(vmem_limit_bytes=mib << 20)


def cost(us):
    return pl.CostEstimate(flops=int(us * 1e9), bytes_accessed=int(us * 1e5), transcendentals=0)


def picked(odd, when_odd, when_even, target, sem):
    def start():
        @pl.when(odd)
        def _():
            pltpu.make_async_copy(when_odd, target, sem).start()

        @pl.when(jnp.logical_not(odd))
        def _():
            pltpu.make_async_copy(when_even, target, sem).start()

    def wait():
        pltpu.make_async_copy(when_odd, target, sem).wait()

    return start, wait


def placed(odd, source, when_odd, when_even, sem):
    def start():
        @pl.when(odd)
        def _():
            pltpu.make_async_copy(source, when_odd, sem).start()

        @pl.when(jnp.logical_not(odd))
        def _():
            pltpu.make_async_copy(source, when_even, sem).start()

    def wait():
        pltpu.make_async_copy(source, when_odd, sem).wait()

    return start, wait


def is_odd():
    return lax.axis_index("section") % 2 == 1


def first_kernel(offs, gain, wq, wo, down, up):
    _, rows, width = down.shape
    hd = HEADS_DEV * HEAD_DIM

    def body(offs_hbm, gain_hbm, wq_hbm, wo_hbm, down_hbm, up_hbm,
             a_ref, b_ref, gain_ref, wq_ref, wo_ref, mask_ref, *rest):
        outs, (offs_ref, sems) = rest[:6], rest[6:]
        odd = is_odd()
        a_start, a_wait = picked(odd, down_hbm.at[0], up_hbm.at[0], a_ref, sems.at[0])
        b_start, b_wait = picked(odd, up_hbm.at[0], down_hbm.at[0], b_ref, sems.at[1])
        offs_copy = pltpu.make_async_copy(offs_hbm, offs_ref, sems.at[2])
        gain_copy = pltpu.make_async_copy(gain_hbm, gain_ref, sems.at[3])
        wo_copy = pltpu.make_async_copy(wo_hbm.at[0], wo_ref, sems.at[4])
        cols = [pl.ds(n * hd, hd) for n in range(3)]
        wq_copies = [
            pltpu.make_async_copy(wq_hbm.at[0, :, cols[n]], wq_ref.at[:, cols[n]], sems.at[5 + n]) for n in range(3)
        ]
        a_start()
        gain_copy.start()
        offs_copy.start()
        for copy in wq_copies:
            copy.start()
        wo_copy.start()
        b_start()
        offs_copy.wait()
        mask_ref[...] = mask_body(odd, offs_ref, rows)
        a_wait()
        gain_copy.wait()
        forward_body(a_ref, gain_ref, wq_ref, wo_ref, mask_ref, *outs, waits=wq_copies + [wo_copy])
        b_wait()

    hbm = pl.BlockSpec(memory_space=pltpu.HBM)
    return pl.pallas_call(
        body,
        in_specs=[hbm] * 6,
        out_specs=[VM] * 12,
        out_shape=[
            shape_v((rows, width), BF16),
            shape_v((rows, width), BF16),
            shape_v(gain.shape, BF16),
            shape_v(wq.shape[1:], BF16),
            shape_v(wo.shape[1:], BF16),
            shape_v((rows, rows), F32),
        ] + forward_outs(rows, width),
        scratch_shapes=[pltpu.SMEM(offs.shape, jnp.int32), pltpu.SemaphoreType.DMA((8,))],
        compiler_params=params(24),
        cost_estimate=cost(FWD_COST),
        name="first",
    )(offs, gain, wq, wo, down, up)


def forward_outs(rows, width):
    hd = HEADS_DEV * HEAD_DIM
    return [
        shape_v((rows, width), BF16),
        shape_v((rows, width), BF16),
        shape_v((rows, 3 * hd), BF16),
        shape_v((HEADS_DEV, rows, rows), F32),
        shape_v((rows, hd), BF16),
        shape_v((rows, 256), F32),
    ]


def forward_kernel(h, gain, wq, wo, mask):
    rows, width = h.shape
    return pl.pallas_call(
        forward_body,
        in_specs=[VM] * 5,
        out_specs=[VM] * 6,
        out_shape=forward_outs(rows, width),
        compiler_params=params(24),
        cost_estimate=cost(FWD_COST),
        name="forward",
    )(h, gain, wq, wo, mask)


def turn_kernel(h, gain, wq, wo, mask, when_odd, when_even, out_odd=None, out_even=None):
    rows, width = h.shape
    hd = HEADS_DEV * HEAD_DIM
    again = out_odd is not None

    def body(h_ref, gain_ref, wq_ref, wo_ref, mask_ref, odd_hbm, even_hbm, *rest):
        rest = rest[2:] if again else rest
        to_odd, to_even, e_ref, g_ref, u_ref, dqkv_ref, att_ref, dg_ref = rest[:8]
        out_ref, qkv_ref, p_ref, st_ref, du_ref, sems = rest[8:]
        odd = is_odd()
        g_start, g_wait = picked(odd, odd_hbm.at[0], even_hbm.at[0], g_ref, sems.at[0])
        out_start, out_wait = placed(odd, out_ref, to_odd.at[0], to_even.at[0], sems.at[1])
        g_start()
        forward_body(h_ref, gain_ref, wq_ref, wo_ref, mask_ref, out_ref, u_ref, qkv_ref, p_ref, att_ref, st_ref)
        out_start()
        g_wait()
        backward_body(g_ref, h_ref, gain_ref, wq_ref, wo_ref, qkv_ref, p_ref, st_ref, e_ref, dqkv_ref, dg_ref, du_ref)
        out_wait()

    hbm = pl.BlockSpec(memory_space=pltpu.HBM)
    operands = [h, gain, wq, wo, mask, when_odd, when_even] + ([out_odd, out_even] if again else [])
    to_odd, to_even, e, g, u, dqkv, att, dgain = pl.pallas_call(
        body,
        in_specs=[VM] * 5 + [hbm] * (len(operands) - 5),
        out_specs=[hbm] * 2 + [VM] * 6,
        out_shape=[jax.ShapeDtypeStruct((1, rows, width), BF16)] * 2 + [
            shape_v((rows, width), BF16),
            shape_v((rows, width), BF16),
            shape_v((rows, width), BF16),
            shape_v((rows, 3 * hd), BF16),
            shape_v((rows, hd), BF16),
            shape_v((8, width), F32),
        ],
        scratch_shapes=[
            pltpu.VMEM((rows, width), BF16),
            pltpu.VMEM((rows, 3 * hd), BF16),
            pltpu.VMEM((HEADS_DEV, rows, rows), F32),
            pltpu.VMEM((rows, 256), F32),
            pltpu.VMEM((rows, width), BF16),
            pltpu.SemaphoreType.DMA((2,)),
        ],
        input_output_aliases={7: 0, 8: 1} if again else {},
        compiler_params=params(24),
        cost_estimate=cost(FWD_COST + BWD_COST),
        name="turn",
    )(*operands)
    return to_odd, to_even, e, (u, dqkv, att, g, dgain)


def backward_kernel(g, h, gain, wq, wo, saved):
    rows, width = h.shape
    hd = HEADS_DEV * HEAD_DIM
    u, qkv, probs, att, stats = saved
    e, dqkv, dgain = pl.pallas_call(
        backward_body,
        in_specs=[VM] * 8,
        out_specs=[VM] * 3,
        out_shape=[shape_v((rows, width), BF16), shape_v((rows, 3 * hd), BF16), shape_v((8, width), F32)],
        scratch_shapes=[pltpu.VMEM((rows, width), BF16)],
        compiler_params=params(24),
        cost_estimate=cost(BWD_COST),
        name="backward",
    )(g, h, gain, wq, wo, qkv, probs, stats)
    return e, (u, dqkv, att, g, dgain)


def last_backward_kernel(g, h, gain, wq, wo, saved, out_odd=None, out_even=None):
    rows, width = h.shape
    hd = HEADS_DEV * HEAD_DIM
    u, qkv, probs, att, stats = saved
    again = out_odd is not None

    def body(*refs):
        ins, rest = refs[:8], refs[10 if again else 8:]
        to_odd, to_even, dqkv_ref, dg_ref, e_ref, du_ref, sem = rest
        start, wait = placed(is_odd(), e_ref, to_odd.at[0], to_even.at[0], sem)
        backward_body(*ins, e_ref, dqkv_ref, dg_ref, du_ref)
        start()
        wait()

    hbm = pl.BlockSpec(memory_space=pltpu.HBM)
    extra = [out_odd, out_even] if again else []
    to_odd, to_even, dqkv, dgain = pl.pallas_call(
        body,
        in_specs=[VM] * 8 + [hbm] * len(extra),
        out_specs=[hbm] * 2 + [VM] * 2,
        out_shape=[jax.ShapeDtypeStruct((1, rows, width), BF16)] * 2
        + [shape_v((rows, 3 * hd), BF16), shape_v((8, width), F32)],
        scratch_shapes=[
            pltpu.VMEM((rows, width), BF16), pltpu.VMEM((rows, width), BF16), pltpu.SemaphoreType.DMA,
        ],
        input_output_aliases={8: 0, 9: 1} if again else {},
        compiler_params=params(24),
        cost_estimate=cost(BWD_COST),
        name="last_backward",
    )(g, h, gain, wq, wo, qkv, probs, stats, *extra)
    return to_odd, to_even, (u, dqkv, att, g, dgain)


def weight_sums(use, width, hd, put_gain, put_wo, put_wq):
    total = use[0][4][...]
    for part in use[1:]:
        total = total + part[4][...]
    put_gain(total)
    att = jnp.concatenate([r[2][...] for r in use], axis=0)
    for n in range(0, width, 512):
        g = jnp.concatenate([r[3][:, n:n + 512] for r in use], axis=0)
        put_wo(pl.ds(n, 512), dot(att, g, TN))
    dqkv = jnp.concatenate([r[1][...] for r in use], axis=0)
    for m in range(0, width, 256):
        u = jnp.concatenate([r[0][:, m:m + 256] for r in use], axis=0)
        put_wq(pl.ds(m, 256), dot(u, dqkv, TN))


def early_weights(uses):
    rows, width = uses[0][0].shape
    hd = HEADS_DEV * HEAD_DIM
    count = len(uses)

    def body(*refs):
        gain_out, wo_out, wq_out = refs[5 * count:]

        def put_gain(value):
            gain_out[...] = value

        def put_wo(cols, value):
            wo_out[:, cols] = value

        def put_wq(at, value):
            wq_out[at, :] = value

        weight_sums([refs[5 * i:5 * i + 5] for i in range(count)], width, hd, put_gain, put_wo, put_wq)

    flat = [leaf for use in uses for leaf in use]
    return pl.pallas_call(
        body,
        in_specs=[VM] * len(flat),
        out_specs=[VM] * 3,
        out_shape=[shape_v((8, width), F32), shape_v((hd, width), F32), shape_v((width, 3 * hd), F32)],
        compiler_params=params(24),
        cost_estimate=cost(W_COST),
        name="early_weights",
    )(*flat)


def last_weights(uses, sums):
    rows, width = uses[0][0].shape
    hd = HEADS_DEV * HEAD_DIM
    count = len(uses)

    def body(*refs):
        gain_sum, wo_sum, wq_sum = refs[5 * count:5 * count + 3]
        gain_out, wo_hbm, wq_hbm, wo_buf, wq_buf, sems = refs[5 * count + 3:]
        copies = []

        def put_gain(value):
            gain_out[...] = jnp.sum(gain_sum[...] + value, axis=0, keepdims=True).astype(BF16)

        def put_wo(cols, value):
            wo_buf[:, cols] = (wo_sum[:, cols] + value).astype(BF16)
            copy = pltpu.make_async_copy(wo_buf.at[:, cols], wo_hbm.at[0, :, cols], sems.at[len(copies)])
            copy.start()
            copies.append(copy)

        def put_wq(at, value):
            wq_buf[at, :] = (wq_sum[at, :] + value).astype(BF16)
            copy = pltpu.make_async_copy(wq_buf.at[at], wq_hbm.at[0, at], sems.at[len(copies)])
            copy.start()
            copies.append(copy)

        weight_sums([refs[5 * i:5 * i + 5] for i in range(count)], width, hd, put_gain, put_wo, put_wq)
        for copy in copies:
            copy.wait()

    flat = [leaf for use in uses for leaf in use] + list(sums)
    hbm = pl.BlockSpec(memory_space=pltpu.HBM)
    return pl.pallas_call(
        body,
        in_specs=[VM] * len(flat),
        out_specs=[VM, hbm, hbm],
        out_shape=[
            jax.ShapeDtypeStruct((1, width), BF16),
            jax.ShapeDtypeStruct((1, hd, width), BF16),
            jax.ShapeDtypeStruct((1, width, 3 * hd), BF16),
        ],
        scratch_shapes=[
            pltpu.VMEM((hd, width), BF16),
            pltpu.VMEM((width, 3 * hd), BF16),
            pltpu.SemaphoreType.DMA((width // 512 + width // 256,)),
        ],
        compiler_params=params(24),
        cost_estimate=cost(W_COST),
        name="last_weights",
    )(*flat)


def shards(acts_down, acts_up, cotangent_down, cotangent_up, ln_gain, w_qkv, w_out, band_offsets):
    sections = lax.axis_size("section")
    near = [(i, i ^ 1) for i in range(sections)]
    far = [(i, (i + (1 if i % 2 else -1)) % sections) for i in range(sections)]

    def swap_near(x):
        return lax.ppermute(x, "section", near)

    def swap_far(x):
        return lax.ppermute(x, "section", far)

    def after(x, *others):
        return lax.optimization_barrier((x, *others))[0]

    def in_hbm(*arrays):
        return [pltpu.with_memory_space_constraint(x, pltpu.HBM) for x in arrays]

    cotangent_down, cotangent_up = in_hbm(cotangent_down, cotangent_up)
    a0, b0, gain, wq, wo, mask, a1_out, *a0_saved = first_kernel(
        *in_hbm(band_offsets.T, ln_gain, w_qkv, w_out, acts_down, acts_up))
    a1 = swap_far(a1_out)
    b1_out, *b0_saved = forward_kernel(after(b0, a0_saved[4]), gain, wq, wo, mask)
    b1 = swap_near(b1_out)
    b2_out, *b1_saved = forward_kernel(after(b1, b0_saved[4]), gain, wq, wo, mask)
    a1, b2_out = lax.optimization_barrier((a1, b2_out))
    b2 = swap_far(b2_out)
    a2_out, *a1_saved = forward_kernel(a1, gain, wq, wo, mask)
    a2 = swap_near(a2_out)
    out_odd, out_even, ea2, use_a2 = turn_kernel(
        after(a2, a1_saved[4]), gain, wq, wo, mask, cotangent_down, cotangent_up)
    ca1 = swap_near(ea2)
    ea1, use_a1 = backward_kernel(after(ca1, use_a2[4]), a1, gain, wq, wo, a1_saved)
    ca0 = swap_far(ea1)
    out_even, out_odd, eb2, use_b2 = turn_kernel(
        after(b2, use_a1[4]), gain, wq, wo, mask, cotangent_up, cotangent_down, out_even, out_odd)
    cb1 = swap_far(eb2)
    sums = early_weights([use_a2, use_a1, (after(use_b2[0], use_b2[4]), *use_b2[1:])])
    eb1, use_b1 = backward_kernel(after(cb1, sums[0]), b1, gain, wq, wo, b1_saved)
    cb0 = swap_near(eb1)
    back_odd, back_even, use_a0 = last_backward_kernel(after(ca0, use_b1[4]), a0, gain, wq, wo, a0_saved)
    back_even, back_odd, use_b0 = last_backward_kernel(
        after(cb0, use_a0[4]), b0, gain, wq, wo, b0_saved, back_even, back_odd)
    d_gain, d_wo, d_wq = last_weights([use_b1, use_a0, use_b0], sums)
    return out_odd, out_even, back_odd, back_even, d_gain, d_wq, d_wo


def solution(mesh):
    both = ("groups", "section")
    in_specs = (
        P(both, None, None), P(both, None, None), P(both, None, None), P(both, None, None),
        P("section", None), P("section", None, None), P("section", None, None), P(),
    )
    out_specs = (
        P(both, None, None), P(both, None, None), P(both, None, None), P(both, None, None),
        P(both, None), P(both, None, None), P(both, None, None),
    )
    return jax.shard_map(shards, mesh=mesh, in_specs=in_specs, out_specs=out_specs, check_vma=False)
```

time: 85.5 us -> 86.7 us (1.014)
  waiting for transfers between devices: 34.7 us -> 40.3 us
  local copies, waits for them, and re-layouts: 4.59 us -> 0 us
  Pallas kernels: 34.5 us -> 38.6 us
  other arithmetic: 3.42 us -> 0 us
    pallas_call x2 -> x7, Pallas kernels: 7.83 us -> 27.4 us  [the longest x2 9.99 us: turn_kernel(): pl.pallas_call(body, in_specs=[VM] * 5 + [hbm] * (len(operands) - 5), out...]
    pallas_call x6 -> x2, Pallas kernels: 17.8 us -> 5.88 us  [backward_kernel(): pl.pallas_call(backward_body, in_specs=[VM] * 8, out_specs=[VM] * 3, out_...]
    unnamed x15 -> x0, local copies, waits for them, and re-layouts: 4.59 us -> none
    ppermute x4, waiting for transfers between devices: 34.7 us -> 38.3 us  [swap_far(): return lax.ppermute(x, 'section', far)]
    pallas_call x5 -> x3, Pallas kernels: 8.88 us -> 5.33 us  [forward_kernel(): pl.pallas_call(forward_body, in_specs=[VM] * 5, out_specs=[VM] * 6, out_s...]
    broadcast_in_dim x2 -> x0, other arithmetic: 2.08 us -> none  [the longest x1 1.04 us: shards(): back_up[None]]
    ppermute x4, waiting for transfers between devices: 0.01 us -> 1.94 us  [swap_near(): return lax.ppermute(x, 'section', near)]
    select_n x2 -> x0, other arithmetic: 1.35 us -> none  [the longest x1 1.27 us: shards(): b0 = jnp.where(odd, acts_up[0], acts_down[0])]
  transfers between devices with their start and end apart: 8 -> 8, of which waited for: 4 -> 5; matrix products, arithmetic and copies ran while one was open for 1% -> 0% of each run, Pallas kernels for 26% -> 16%
where the time goes in v1:
time: 86.7 us; the launch traced here: 86.5 us
  waiting for transfers between devices  40.3 us (46%)
  Pallas kernels  38.6 us (45%)
  starting transfers between devices  6.73 us (8%)
  between operations  0.9 us (1%)
    ppermute x4, waiting for transfers between devices, swap_far(): return lax.ppermute(x, 'section', far)  38.3 us
    pallas_call x2, Pallas kernels, turn_kernel(): pl.pallas_call(body, in_specs=[VM] * 5 + [hbm] * (len(operands) - 5), out...  9.99 us
    pallas_call x2, Pallas kernels, last_backward_kernel(): pl.pallas_call(body, in_specs=[VM] * 8 + [hbm] * len(extra), out_specs=[h...  7.49 us
    ppermute x4, starting transfers between devices, swap_far(): return lax.ppermute(x, 'section', far)  6.27 us
    pallas_call x2, Pallas kernels, backward_kernel(): pl.pallas_call(backward_body, in_specs=[VM] * 8, out_specs=[VM] * 3, out_...  5.88 us
    pallas_call x3, Pallas kernels, forward_kernel(): pl.pallas_call(forward_body, in_specs=[VM] * 5, out_specs=[VM] * 6, out_s...  5.33 us
    pallas_call x1, Pallas kernels, last_weights(): pl.pallas_call(body, in_specs=[VM] * len(flat), out_specs=[VM, hbm, hbm],...  3.98 us
    pallas_call x1, Pallas kernels, first_kernel(): pl.pallas_call(body, in_specs=[hbm] * 6, out_specs=[VM] * 12, out_shape=[...  3.56 us
  transfers between devices with their start and end apart: 8, of which 5 were waited for; matrix products, arithmetic and copies ran while one was open for 0% of the time, Pallas kernels for 16%

profile of v1, /device:TPU:1, one launch (start us, length us, event | category | flops | bytes accessed | tf_op | source)
XLA Modules:
  0.0 86.5 jit_solution(5354470231130478977)
XLA Ops:
  0.6 3.6 %first.1 = (bf16[128,2048]{1,0:T(8,128)(2,1)S(1)}, bf16[128,2048]{1,0:T(8,128)(2,1)S(1)}, bf16[1,2048]{1,0:T(2,128)(2,1)S(1)}, bf16[2048,768]{1,0:T(8,128)(2,1)S...) custom-call(s32[2,4]{1,0:T(2,128)} %bitcast.1, ...), custom_call_target="tpu_custom_call" | custom-call | flops 2000000 | bytes 200 | tf_op jit(solution)/shard_map/first/pallas_call | solution.py:195
  4.2 1.8 %forward.3 = (bf16[128,2048]{1,0:T(8,128)(2,1)S(1)}, bf16[128,2048]{1,0:T(8,128)(2,1)S(1)}, bf16[128,768]{1,0:T(8,128)(2,1)S(1)}, f32[2,128,128]{2,1,0:T(8,128)S...) custom-call(bf16[128,2048]{1,0:T(8,128)(2,1)S(1)} %get-tuple-element.87.h_ref.refs_1_, ...), custom_call_target="tpu_custom_call" | custom-call | flops 2000000 | bytes 200 | tf_op jit(solution)/shard_map/forward/pallas_call | solution.py:228
  6.0 0.1 collective-permute-start.1
  6.1 2.7 %collective-permute-start = (bf16[128,2048]{1,0:T(8,128)(2,1)S(1)}, bf16[128,2048]{1,0:T(8,128)(2,1)S(1)}, u32[]{:S(2)}, u32[]{:S(2)}) collective-permute-start(bf16[128,2048]{1,0:T(8,128)(2,1)S(1)} %get-tuple-element.84), channel_id=1, source_target_pairs={{0,15},{1,2},{2,1},{3,4},{4,3},{5,6},{6,5},{7,8},{8,7},{9,10},{10,... | collective-permute-start | bytes 1572872 | tf_op jit(solution)/shard_map/ppermute | solution.py:444
  8.8 1.8 %forward.4 = (bf16[128,2048]{1,0:T(8,128)(2,1)S(1)}, bf16[128,2048]{1,0:T(8,128)(2,1)S(1)}, bf16[128,768]{1,0:T(8,128)(2,1)S(1)}, f32[2,128,128]{2,1,0:T(8,128)S...) custom-call(bf16[128,2048]{1,0:T(8,128)(2,1)S(1)} %collective-permute-done.1.h_ref, ...), custom_call_target="tpu_custom_call" | custom-call | flops 2000000 | bytes 200 | tf_op jit(solution)/shard_map/forward/pallas_call | solution.py:228
  10.5 10.7 %collective-permute-done.h_ref = bf16[128,2048]{1,0:T(8,128)(2,1)S(1)} collective-permute-done((bf16[128,2048]{1,0:T(8,128)(2,1)S(1)}, bf16[128,2048]{1,0:T(8,128)(2,1)S(1)}, u32[]{:S(2)}, u32[]{:S(2)}) %collective-permute-start) | collective-permute-done | bytes 524320 | tf_op jit(solution)/shard_map/ppermute | solution.py:444
  21.3 1.8 %forward.5 = (bf16[128,2048]{1,0:T(8,128)(2,1)S(1)}, bf16[128,2048]{1,0:T(8,128)(2,1)S(1)}, bf16[128,768]{1,0:T(8,128)(2,1)S(1)}, f32[2,128,128]{2,1,0:T(8,128)S...) custom-call(bf16[128,2048]{1,0:T(8,128)(2,1)S(1)} %collective-permute-done.h_ref, ...), custom_call_target="tpu_custom_call" | custom-call | flops 2000000 | bytes 200 | tf_op jit(solution)/shard_map/forward/pallas_call | solution.py:228
  23.0 0.1 collective-permute-start.3
  23.1 1.9 %collective-permute-done.3.h_ref = bf16[128,2048]{1,0:T(8,128)(2,1)S(1)} collective-permute-done((bf16[128,2048]{1,0:T(8,128)(2,1)S(1)}, bf16[128,2048]{1,0:T(8,128)(2,1)S(1)}, u32[]{:S(2)}, u32[]{:S(2)}) %collective-permute-start.3) | collective-permute-done | bytes 524320 | tf_op jit(solution)/shard_map/ppermute | solution.py:441
  25.0 4.9 %turn.2 = (bf16[1,128,2048]{2,1,0:T(8,128)(2,1)}, bf16[1,128,2048]{2,1,0:T(8,128)(2,1)}, bf16[128,2048]{1,0:T(8,128)(2,1)S(1)}, bf16[128,2048]{1,0:T(8,128)(2,1)...) custom-call(bf16[128,2048]{1,0:T(8,128)(2,1)S(1)} %collective-permut, ...), custom_call_target="tpu_custom_call" | custom-call | flops 5000000 | bytes 500 | tf_op jit(solution)/shard_map/turn/pallas_call | solution.py:260
  30.0 0.2 collective-permute-start.4
  30.2 1.7 %collective-permute-start.2 = (bf16[128,2048]{1,0:T(8,128)(2,1)S(1)}, bf16[128,2048]{1,0:T(8,128)(2,1)S(1)}, u32[]{:S(2)}, u32[]{:S(2)}) collective-permute-start(bf16[128,2048]{1,0:T(8,128)(2,1)S(1)} %get-tuple-element.96), channel_id=1, source_target_pairs={{0,15},{1,2},{2,1},{3,4},{4,3},{5,6},{6,5},{7,8},{8,7},{9,10},{10,... | collective-permute-start | bytes 1572872 | tf_op jit(solution)/shard_map/ppermute | solution.py:444
  31.9 2.9 %backward.2 = (bf16[128,2048]{1,0:T(8,128)(2,1)S(1)}, bf16[128,768]{1,0:T(8,128)(2,1)S(1)}, f32[8,2048]{1,0:T(8,128)S(1)}) custom-call(bf16[128,2048]{1,0:T(8,128)(2,1)S(1)} %collective-permute-done.4.g_ref.refs_8_, bf16[128,2048]{1,0:T(8,128)(2,1)S(1)} %collective-permute-done.h_ref, bf16[1,2048]{1,0:T(2,128)(2,1)S(1)} %get-tuple-element.88.gain_ref.refs_2_, ...), custom_call_target="tpu_custom_call" | custom-call | flops 3000000 | bytes 300 | tf_op jit(solution)/shard_map/backward/pallas_call | solution.py:292
  34.9 9.5 %collective-permute-done.2.h_ref = bf16[128,2048]{1,0:T(8,128)(2,1)S(1)} collective-permute-done((bf16[128,2048]{1,0:T(8,128)(2,1)S(1)}, bf16[128,2048]{1,0:T(8,128)(2,1)S(1)}, u32[]{:S(2)}, u32[]{:S(2)}) %collective-permute-start.2) | collective-permute-done | bytes 524320 | tf_op jit(solution)/shard_map/ppermute | solution.py:444
  44.4 5.0 %turn.3 = (bf16[1,128,2048]{2,1,0:T(8,128)(2,1)}, bf16[1,128,2048]{2,1,0:T(8,128)(2,1)}, bf16[128,2048]{1,0:T(8,128)(2,1)S(1)}, bf16[128,2048]{1,0:T(8,128)(2,1)...) custom-call(bf16[128,2048]{1,0:T(8,128)(2,1)S(1)} %collective-permut, ...), custom_call_target="tpu_custom_call", output_to_operand_aliasing={{0}: (7, {}), {1}: (8, {})} | custom-call | flops 5000000 | bytes 500 | tf_op jit(solution)/shard_map/turn/pallas_call | solution.py:260
  49.4 1.8 %collective-permute-start.5 = (bf16[128,2048]{1,0:T(8,128)(2,1)S(1)}, bf16[128,2048]{1,0:T(8,128)(2,1)S(1)}, u32[]{:S(2)}, u32[]{:S(2)}) collective-permute-start(bf16[128,2048]{1,0:T(8,128)(2,1)S(1)} %get-tuple-element.112), channel_id=1, source_target_pairs={{0,15},{1,2},{2,1},{3,4},{4,3},{5,6},{6,5},{7,8},{8,7},{9,10},{10,... | collective-permute-start | bytes 1572872 | tf_op jit(solution)/shard_map/ppermute | solution.py:444
  51.2 0.1 collective-permute-start.7
  51.3 2.4 %early_weights.1 = (f32[8,2048]{1,0:T(8,128)S(1)}, f32[256,2048]{1,0:T(8,128)S(1)}, f32[2048,768]{1,0:T(8,128)S(1)}) custom-call(bf16[128,2048]{1,0:T(8,128)(2,1)S(1)} %get-tuple-element.113.refs_0_, bf16[128,768]{1,0:T(8,128)(2,1)S(1)} %get-tuple-element.114.refs_1_, bf16[128,256]{1,0:T(8,128)(2,1)S(1)} %get-tuple-element.115.refs_2_, ...), custom_call_target="tpu_custom_call" | custom-call | flops 4000000 | bytes 400 | tf_op jit(solution)/shard_map/early_weights/pallas_call | solution.py:373
  53.7 15.5 %collective-permute-done.5.g_ref.refs_3_ = bf16[128,2048]{1,0:T(8,128)(2,1)S(1)} collective-permute-done((bf16[128,2048]{1,0:T(8,128)(2,1)S(1)}, bf16[128,2048]{1,0:T(8,128)(2,1)S(1)}, u32[]{:S(2)}, u32[]{:S(2)}) %collective-permute-start.5) | collective-permute-done | bytes 524320 | tf_op jit(solution)/shard_map/ppermute | solution.py:444
  69.2 2.9 %backward.3 = (bf16[128,2048]{1,0:T(8,128)(2,1)S(1)}, bf16[128,768]{1,0:T(8,128)(2,1)S(1)}, f32[8,2048]{1,0:T(8,128)S(1)}) custom-call(bf16[128,2048]{1,0:T(8,128)(2,1)S(1)} %collective-permute-done.5.g_ref.refs_3_, bf16[128,2048]{1,0:T(8,128)(2,1)S(1)} %collective-permute-done.1.h_ref, bf16[1,2048]{1,0:T(2,128)(2,1)S(1)} %get-tuple-element.88.gain_ref.refs_2_, ...), custom_call_target="tpu_custom_call" | custom-call | flops 3000000 | bytes 300 | tf_op jit(solution)/shard_map/backward/pallas_call | solution.py:292
  72.3 2.6 %collective-permute-done.7.refs_0_.refs_8_ = bf16[128,2048]{1,0:T(8,128)(2,1)S(1)} collective-permute-done((bf16[128,2048]{1,0:T(8,128)(2,1)S(1)}, bf16[128,2048]{1,0:T(8,128)(2,1)S(1)}, u32[]{:S(2)}, u32[]{:S(2)}) %collective-permute-start.7) | collective-permute-done | bytes 524320 | tf_op jit(solution)/shard_map/ppermute | solution.py:444
  74.9 3.7 %last_backward.2 = (bf16[1,128,2048]{2,1,0:T(8,128)(2,1)}, bf16[1,128,2048]{2,1,0:T(8,128)(2,1)}, bf16[128,768]{1,0:T(8,128)(2,1)S(1)}, f32[8,2048]{1,0:T(8,128)S(1)}) custom-call(bf16[128,2048]{1,0:T(8,128)(2,1)S(1)} %collective-permute-done.7.refs_0_.refs_8_, bf16[128,2048]{1,0:T(8,128)(2,1)S(1)} %get-tuple-element.135.refs_1_, ...), custom_call_target="tpu_custom_call" | custom-call | flops 3000000 | bytes 300 | tf_op jit(solution)/shard_map/last_backward/pallas_call | solution.py:321
  78.6 3.7 %last_backward.3 = (bf16[1,128,2048]{2,1,0:T(8,128)(2,1)}, bf16[1,128,2048]{2,1,0:T(8,128)(2,1)}, bf16[128,768]{1,0:T(8,128)(2,1)S(1)}, f32[8,2048]{1,0:T(8,128)S(1)}) custom-call(bf16[128,2048]{1,0:T(8,128)(2,1)S(1)} %collective-permute-done.6.refs_0_.refs_13_, ...), custom_call_target="tpu_custom_call", output_to_operand_aliasing={{0}: (8, {}), {1}: (9, {})} | custom-call | flops 3000000 | bytes 300 | tf_op jit(solution)/shard_map/last_backward/pallas_call | solution.py:321
  82.4 4.0 %last_weights.1 = (bf16[1,2048]{1,0:T(2,128)(2,1)}, bf16[1,256,2048]{2,1,0:T(8,128)(2,1)}, bf16[1,2048,768]{2,1,0:T(8,128)(2,1)}) custom-call(bf16[128,2048]{1,0:T(8,128)(2,1)S(1)} %get-tuple-element.146.refs_0_, bf16[128,768]{1,0:T(8,128)(2,1)S(1)} %get-tuple-element.147.refs_1_, bf16[128,256]{1,0:T(8,128)(2,1)S(1)} %get-tuple-element.148.refs_2_, ...), custom_call_target="tpu_custom_call" | custom-call | flops 4000000 | bytes 400 | tf_op jit(solution)/shard_map/last_weights/pallas_call | solution.py:415
  (4 shorter events, 0.1 us)
Async XLA Ops:
  6.0 2.8 %collective-permute-start.1 = (bf16[128,2048]{1,0:T(8,128)(2,1)S(1)}, bf16[128,2048]{1,0:T(8,128)(2,1)S(1)}, u32[]{:S(2)}, u32[]{:S(2)}) collective-permute-start(bf16[128,2048]{1,0:T(8,128)(2,1)S(1)} %get-tuple-element.92), channel_id=1, source_target_pairs={{0,1},{1,0},{2,3},{3,2},{4,5},{5,4},{6,7},{7,6},{8,9},{9,8},{10,11... | collective-permute-start | bytes 1572872 | tf_op jit(solution)/shard_map/ppermute | solution.py:441
  6.1 15.1 %collective-permute-start = (bf16[128,2048]{1,0:T(8,128)(2,1)S(1)}, bf16[128,2048]{1,0:T(8,128)(2,1)S(1)}, u32[]{:S(2)}, u32[]{:S(2)}) collective-permute-start(bf16[128,2048]{1,0:T(8,128)(2,1)S(1)} %get-tuple-element.84), channel_id=1, source_target_pairs={{0,15},{1,2},{2,1},{3,4},{4,3},{5,6},{6,5},{7,8},{8,7},{9,10},{10,... | collective-permute-start | bytes 1572872 | tf_op jit(solution)/shard_map/ppermute | solution.py:444
  23.0 2.0 %collective-permute-start.3 = (bf16[128,2048]{1,0:T(8,128)(2,1)S(1)}, bf16[128,2048]{1,0:T(8,128)(2,1)S(1)}, u32[]{:S(2)}, u32[]{:S(2)}) collective-permute-start(bf16[128,2048]{1,0:T(8,128)(2,1)S(1)} %get-tuple-element.98), channel_id=1, source_target_pairs={{0,1},{1,0},{2,3},{3,2},{4,5},{5,4},{6,7},{7,6},{8,9},{9,8},{10,11... | collective-permute-start | bytes 1572872 | tf_op jit(solution)/shard_map/ppermute | solution.py:441
  30.0 2.0 %collective-permute-start.4 = (bf16[128,2048]{1,0:T(8,128)(2,1)S(1)}, bf16[128,2048]{1,0:T(8,128)(2,1)S(1)}, u32[]{:S(2)}, u32[]{:S(2)}) collective-permute-start(bf16[128,2048]{1,0:T(8,128)(2,1)S(1)} %get-tuple-element.101), channel_id=1, source_target_pairs={{0,1},{1,0},{2,3},{3,2},{4,5},{5,4},{6,7},{7,6},{8,9},{9,8},{10,11... | collective-permute-start | bytes 1572872 | tf_op jit(solution)/shard_map/ppermute | solution.py:441
  30.2 14.2 %collective-permute-start.2 = (bf16[128,2048]{1,0:T(8,128)(2,1)S(1)}, bf16[128,2048]{1,0:T(8,128)(2,1)S(1)}, u32[]{:S(2)}, u32[]{:S(2)}) collective-permute-start(bf16[128,2048]{1,0:T(8,128)(2,1)S(1)} %get-tuple-element.96), channel_id=1, source_target_pairs={{0,15},{1,2},{2,1},{3,4},{4,3},{5,6},{6,5},{7,8},{8,7},{9,10},{10,... | collective-permute-start | bytes 1572872 | tf_op jit(solution)/shard_map/ppermute | solution.py:444
  49.4 19.8 %collective-permute-start.5 = (bf16[128,2048]{1,0:T(8,128)(2,1)S(1)}, bf16[128,2048]{1,0:T(8,128)(2,1)S(1)}, u32[]{:S(2)}, u32[]{:S(2)}) collective-permute-start(bf16[128,2048]{1,0:T(8,128)(2,1)S(1)} %get-tuple-element.112), channel_id=1, source_target_pairs={{0,15},{1,2},{2,1},{3,4},{4,3},{5,6},{6,5},{7,8},{8,7},{9,10},{10,... | collective-permute-start | bytes 1572872 | tf_op jit(solution)/shard_map/ppermute | solution.py:444
  51.2 23.6 %collective-permute-start.7 = (bf16[128,2048]{1,0:T(8,128)(2,1)S(1)}, bf16[128,2048]{1,0:T(8,128)(2,1)S(1)}, u32[]{:S(2)}, u32[]{:S(2)}) collective-permute-start(bf16[128,2048]{1,0:T(8,128)(2,1)S(1)} %get-tuple-element.132), channel_id=1, source_target_pairs={{0,15},{1,2},{2,1},{3,4},{4,3},{5,6},{6,5},{7,8},{8,7},{9,10},{10,... | collective-permute-start | bytes 1572872 | tf_op jit(solution)/shard_map/ppermute | solution.py:444
  72.2 6.4 %collective-permute-start.6 = (bf16[128,2048]{1,0:T(8,128)(2,1)S(1)}, bf16[128,2048]{1,0:T(8,128)(2,1)S(1)}, u32[]{:S(2)}, u32[]{:S(2)}) collective-permute-start(bf16[128,2048]{1,0:T(8,128)(2,1)S(1)} %get-tuple-element.131), channel_id=1, source_target_pairs={{0,1},{1,0},{2,3},{3,2},{4,5},{5,4},{6,7},{7,6},{8,9},{9,8},{10,11... | collective-permute-start | bytes 1572872 | tf_op jit(solution)/shard_map/ppermute | solution.py:441

commit v2 on v0

v2 whole, which is shorter than its diff:
```python
import math

import jax
import jax.numpy as jnp
from jax import lax
from jax.experimental import pallas as pl
from jax.experimental.pallas import tpu as pltpu
from jax.sharding import PartitionSpec as P

HEADS_DEV = 2
HEAD_DIM = 128
BLOCK = 32
CHUNK = 16
F32 = jnp.float32
BF16 = jnp.bfloat16
NT = (((1,), (1,)), ((), ()))
TN = (((0,), (0,)), ((), ()))
SCALE = 1.0 / math.sqrt(HEAD_DIM)
VM = pl.BlockSpec(memory_space=pltpu.VMEM)
NEAR_PARTS = 2


def dot(a, b, dims=(((1,), (0,)), ((), ()))):
    return lax.dot_general(a, b, dims, preferred_element_type=F32)


def mask_body(odd, offs_ref, rows):
    row = lax.broadcasted_iota(jnp.int32, (rows, rows), 0)
    col = lax.broadcasted_iota(jnp.int32, (rows, rows), 1)
    row_block = row // BLOCK
    col_block = col // BLOCK
    near = row_block == col_block
    for block in range(offs_ref.shape[1]):
        for listed in range(offs_ref.shape[0]):
            near = near | ((row_block == block) & (col_block == block - offs_ref[listed, block]))
    keep = (col <= row) & (near | jnp.logical_not(odd))
    return jnp.where(keep, 1.0, 0.0).astype(F32)


def read(refs, at, size, cols=slice(None)):
    held = refs[0].shape[0]
    return refs[at // held][pl.ds(at % held, size), cols]


def write(refs, at, size, value, cols=slice(None)):
    held = refs[0].shape[0]
    refs[at // held][pl.ds(at % held, size), cols] = value


def whole(refs, cols=slice(None)):
    return jnp.concatenate([ref[:, cols] for ref in refs], axis=0)


def forward_body(h, gain_ref, wq_ref, wo_ref, mask_ref, out, u_ref, qkv_ref, p_ref, att_ref, st_ref, waits=None):
    rows, width = u_ref.shape
    hd = HEADS_DEV * HEAD_DIM
    gain = gain_ref[...].astype(F32)
    for start in range(0, rows, CHUNK):
        part = pl.ds(start, CHUNK)
        x = read(h, start, CHUNK).astype(F32)
        mean = jnp.sum(x, axis=-1, keepdims=True) * (1.0 / width)
        centred = x - mean
        rstd = lax.rsqrt(jnp.sum(centred * centred, axis=-1, keepdims=True) * (1.0 / width) + 1e-05)
        u_ref[part, :] = (centred * rstd * gain).astype(BF16)
        st_ref[part, :] = jnp.concatenate(
            [jnp.broadcast_to(mean, (CHUNK, 128)), jnp.broadcast_to(rstd, (CHUNK, 128))], axis=1)
    for n in range(3):
        if waits:
            waits[n].wait()
        qkv_ref[:, n * hd:(n + 1) * hd] = dot(u_ref[...], wq_ref[:, n * hd:(n + 1) * hd]).astype(BF16)
    keep = mask_ref[...]
    for head in range(HEADS_DEV):
        at = head * HEAD_DIM
        q = qkv_ref[:, at:at + HEAD_DIM]
        k = qkv_ref[:, hd + at:hd + at + HEAD_DIM]
        v = qkv_ref[:, 2 * hd + at:2 * hd + at + HEAD_DIM]
        weighted = jnp.where(keep > 0.0, jnp.exp(dot(q, k, NT) * SCALE), 0.0)
        probs = weighted / jnp.sum(weighted, axis=-1, keepdims=True)
        p_ref[head] = probs
        att_ref[:, at:at + HEAD_DIM] = dot(probs.astype(BF16), v).astype(BF16)
    if waits:
        waits[3].wait()
    for n in range(0, width, 512):
        cols = pl.ds(n, 512)
        value = dot(att_ref[...], wo_ref[:, cols])
        size = min(out[0].shape[0], h[0].shape[0])
        for at in range(0, rows, size):
            write(out, at, size, (read(h, at, size, cols).astype(F32) + value[at:at + size]).astype(BF16), cols)


def backward_body(g, h, gain_ref, wq_ref, wo_ref, qkv_ref, p_ref, st_ref, e, dqkv_ref, dg_ref, du_ref, done=None):
    rows, width = du_ref.shape
    hd = HEADS_DEV * HEAD_DIM
    datt = dot(whole(g), wo_ref[...], NT).astype(BF16)
    for head in range(HEADS_DEV):
        at = head * HEAD_DIM
        q = qkv_ref[:, at:at + HEAD_DIM]
        k = qkv_ref[:, hd + at:hd + at + HEAD_DIM]
        v = qkv_ref[:, 2 * hd + at:2 * hd + at + HEAD_DIM]
        probs = p_ref[head]
        da = datt[:, at:at + HEAD_DIM]
        dp = dot(da, v, NT).astype(BF16).astype(F32)
        dqkv_ref[:, 2 * hd + at:2 * hd + at + HEAD_DIM] = dot(probs.astype(BF16), da, TN).astype(BF16)
        ds = probs * (dp - jnp.sum(dp * probs, axis=-1, keepdims=True)) * SCALE
        ds = ds.astype(BF16)
        dqkv_ref[:, at:at + HEAD_DIM] = dot(ds, k).astype(BF16)
        dqkv_ref[:, hd + at:hd + at + HEAD_DIM] = dot(ds, q, TN).astype(BF16)
    for n in range(0, width, 512):
        cols = pl.ds(n, 512)
        du_ref[:, cols] = dot(dqkv_ref[...], wq_ref[cols, :], NT).astype(BF16)
    gain = gain_ref[...].astype(F32)
    dgain = jnp.zeros((8, width), F32)
    for start in range(0, rows, CHUNK):
        part = pl.ds(start, CHUNK)
        mean = st_ref[part, 0:1]
        rstd = st_ref[part, 128:129]
        xhat = (read(h, start, CHUNK).astype(F32) - mean) * rstd
        du = du_ref[part, :].astype(F32)
        prod = du * xhat
        for piece in range(0, CHUNK, 8):
            dgain = dgain + prod[piece:piece + 8]
        dx = du * gain
        first = jnp.sum(dx, axis=-1, keepdims=True) * (1.0 / width)
        second = jnp.sum(dx * xhat, axis=-1, keepdims=True) * (1.0 / width)
        value = rstd * (dx - first - xhat * second) + read(g, start, CHUNK).astype(F32)
        write(e, start, CHUNK, value.astype(BF16))
        if done:
            done(part)
    dg_ref[...] = dgain


def params(mib):
    return pltpu.CompilerParams(vmem_limit_bytes=mib << 20)


def cost(us):
    return pl.CostEstimate(flops=int(us * 1e9), bytes_accessed=int(us * 1e5), transcendentals=0)


def by_place(odd, when_odd, when_even):
    def start():
        pl.when(odd)(when_odd.start)
        pl.when(jnp.logical_not(odd))(when_even.start)

    return start, when_odd.wait


def is_odd():
    return lax.axis_index("section") % 2 == 1


def call(name, body, operands, outs, scratch=(), hbm=(), alias=(), us=0.002, mib=24):
    flat_in, tree_in = jax.tree.flatten(operands, is_leaf=lambda x: isinstance(x, Far))
    flat_out, tree_out = jax.tree.flatten(outs, is_leaf=lambda x: isinstance(x, (jax.ShapeDtypeStruct, Mem)))

    def kernel(*refs):
        a, b = len(flat_in), len(flat_in) + len(flat_out)
        body(jax.tree.unflatten(tree_in, refs[:a]), jax.tree.unflatten(tree_out, refs[a:b]), refs[b:])

    far = pl.BlockSpec(memory_space=pltpu.HBM)
    result = pl.pallas_call(
        kernel,
        in_specs=[far if isinstance(x, Far) else VM for x in flat_in],
        out_specs=[far if isinstance(x, jax.ShapeDtypeStruct) else VM for x in flat_out],
        out_shape=[x if isinstance(x, jax.ShapeDtypeStruct) else pltpu.VMEM(x.shape, x.dtype) for x in flat_out],
        scratch_shapes=list(scratch),
        input_output_aliases=dict(alias),
        compiler_params=params(mib),
        cost_estimate=cost(us),
        name=name,
    )(*[x.array if isinstance(x, Far) else x for x in flat_in])
    return jax.tree.unflatten(tree_out, result)


class Far:
    def __init__(self, array):
        self.array = pltpu.with_memory_space_constraint(array, pltpu.HBM)


class Mem:
    def __init__(self, shape, dtype):
        self.shape, self.dtype = shape, dtype


def stream(rows, width, parts):
    return [Mem((rows // parts, width), BF16) for _ in range(parts)]


def saved_outs(rows, width):
    hd = HEADS_DEV * HEAD_DIM
    return [
        Mem((rows, width), BF16),
        Mem((rows, 3 * hd), BF16),
        Mem((HEADS_DEV, rows, rows), F32),
        Mem((rows, hd), BF16),
        Mem((rows, 256), F32),
    ]


def first_kernel(offs, gain, wq, wo, down, up, parts):
    _, rows, width = down.shape
    hd = HEADS_DEV * HEAD_DIM

    def body(ins, outs, scratch):
        offs_hbm, gain_hbm, wq_hbm, wo_hbm, down_hbm, up_hbm = ins
        (a_ref,), (b_ref,), gain_ref, wq_ref, wo_ref, mask_ref, out, saved = outs
        offs_ref, sems = scratch
        odd = is_odd()

        def pick(source, target, sem):
            return pltpu.make_async_copy(source, target, sems.at[sem])

        a_start, a_wait = by_place(odd, pick(down_hbm.at[0], a_ref, 0), pick(up_hbm.at[0], a_ref, 0))
        b_start, b_wait = by_place(odd, pick(up_hbm.at[0], b_ref, 1), pick(down_hbm.at[0], b_ref, 1))
        offs_copy = pick(offs_hbm, offs_ref, 2)
        gain_copy = pick(gain_hbm, gain_ref, 3)
        wo_copy = pick(wo_hbm.at[0], wo_ref, 4)
        cols = [pl.ds(n * hd, hd) for n in range(3)]
        wq_copies = [pick(wq_hbm.at[0, :, cols[n]], wq_ref.at[:, cols[n]], 5 + n) for n in range(3)]
        a_start()
        gain_copy.start()
        offs_copy.start()
        for copy in wq_copies:
            copy.start()
        wo_copy.start()
        b_start()
        offs_copy.wait()
        mask_ref[...] = mask_body(odd, offs_ref, rows)
        a_wait()
        gain_copy.wait()
        forward_body([a_ref], gain_ref, wq_ref, wo_ref, mask_ref, out, *saved, waits=wq_copies + [wo_copy])
        b_wait()

    return call(
        "first", body, [Far(x) for x in (offs, gain, wq, wo, down, up)],
        [
            stream(rows, width, 1), stream(rows, width, 1), Mem(gain.shape, BF16), Mem(wq.shape[1:], BF16),
            Mem(wo.shape[1:], BF16), Mem((rows, rows), F32), stream(rows, width, parts), saved_outs(rows, width),
        ],
        [pltpu.SMEM(offs.shape, jnp.int32), pltpu.SemaphoreType.DMA((8,))],
    )


def forward_kernel(h, fixed, mask, parts, us=0.002):
    rows, width = h[0].shape[0] * len(h), h[0].shape[1]

    def body(ins, outs, scratch):
        h, fixed, mask_ref = ins
        out, saved = outs
        forward_body(h, *fixed, mask_ref, out, *saved)

    return call("forward", body, [h, fixed, mask], [stream(rows, width, parts), saved_outs(rows, width)], us=us)


def turn_kernel(h, fixed, mask, when_odd, when_even, parts, so_far=()):
    rows, width = h[0].shape[0] * len(h), h[0].shape[1]
    hd = HEADS_DEV * HEAD_DIM

    def body(ins, outs, scratch):
        h, fixed, mask_ref, (odd_hbm, even_hbm), _ = ins
        (to_odd, to_even), e, (u_ref, dqkv_ref, att_ref, (g_ref,), dg_ref) = outs
        out_ref, qkv_ref, p_ref, st_ref, du_ref, sems = scratch
        odd = is_odd()
        g_start, g_wait = by_place(
            odd, pltpu.make_async_copy(odd_hbm.at[0], g_ref, sems.at[0]),
            pltpu.make_async_copy(even_hbm.at[0], g_ref, sems.at[0]))
        out_start, out_wait = by_place(
            odd, pltpu.make_async_copy(out_ref, to_odd.at[0], sems.at[1]),
            pltpu.make_async_copy(out_ref, to_even.at[0], sems.at[1]))
        g_start()
        forward_body(h, *fixed, mask_ref, [out_ref], u_ref, qkv_ref, p_ref, att_ref, st_ref)
        out_start()
        g_wait()
        backward_body([g_ref], h, *fixed, qkv_ref, p_ref, st_ref, e, dqkv_ref, dg_ref, du_ref)
        out_wait()

    operands = [h, fixed, mask, [Far(when_odd), Far(when_even)], [Far(x) for x in so_far]]
    first = len(jax.tree.leaves(operands[:3])) + 2
    return call(
        "turn", body, operands,
        [
            [jax.ShapeDtypeStruct((1, rows, width), BF16)] * 2,
            stream(rows, width, parts),
            [Mem((rows, width), BF16), Mem((rows, 3 * hd), BF16), Mem((rows, hd), BF16), stream(rows, width, 1),
             Mem((8, width), F32)],
        ],
        [
            pltpu.VMEM((rows, width), BF16),
            pltpu.VMEM((rows, 3 * hd), BF16),
            pltpu.VMEM((HEADS_DEV, rows, rows), F32),
            pltpu.VMEM((rows, 256), F32),
            pltpu.VMEM((rows, width), BF16),
            pltpu.SemaphoreType.DMA((2,)),
        ],
        alias=[(first, 0), (first + 1, 1)] if so_far else [],
    )


def backward_kernel(g, h, fixed, saved, parts):
    rows, width = saved[0].shape
    u, qkv, probs, att, stats = saved

    def body(ins, outs, scratch):
        g, h, fixed, (qkv_ref, p_ref, st_ref) = ins
        e, dqkv_ref, dg_ref = outs
        backward_body(g, h, *fixed, qkv_ref, p_ref, st_ref, e, dqkv_ref, dg_ref, *scratch)

    e, dqkv, dgain = call(
        "backward", body, [g, h, fixed, [qkv, probs, stats]],
        [stream(rows, width, parts), Mem(qkv.shape, BF16), Mem((8, width), F32)],
        [pltpu.VMEM((rows, width), BF16)],
    )
    return e, (u, dqkv, att, g, dgain)


def end_kernel(g, h, fixed, saved):
    rows, width = saved[0].shape
    u, qkv, probs, att, stats = saved

    def body(ins, outs, scratch):
        g, h, fixed, (qkv_ref, p_ref, st_ref) = ins
        (to_odd, to_even), dqkv_ref, dg_ref = outs
        e_ref, du_ref, sem = scratch
        start, wait = by_place(
            is_odd(), pltpu.make_async_copy(e_ref, to_odd.at[0], sem), pltpu.make_async_copy(e_ref, to_even.at[0], sem))
        backward_body(g, h, *fixed, qkv_ref, p_ref, st_ref, [e_ref], dqkv_ref, dg_ref, du_ref)
        start()
        wait()

    outs, dqkv, dgain = call(
        "end", body, [g, h, fixed, [qkv, probs, stats]],
        [[jax.ShapeDtypeStruct((1, rows, width), BF16)] * 2, Mem(qkv.shape, BF16), Mem((8, width), F32)],
        [pltpu.VMEM((rows, width), BF16), pltpu.VMEM((rows, width), BF16), pltpu.SemaphoreType.DMA],
    )
    return outs, (u, dqkv, att, g, dgain)


def weight_sums(uses, width, put_gain, put_wo, put_wq):
    total = uses[0][4][...]
    for use in uses[1:]:
        total = total + use[4][...]
    put_gain(total)
    att = jnp.concatenate([use[2][...] for use in uses], axis=0)
    for n in range(0, width, 512):
        cols = pl.ds(n, 512)
        put_wo(cols, dot(att, jnp.concatenate([whole(use[3], cols) for use in uses], axis=0), TN))
    dqkv = jnp.concatenate([use[1][...] for use in uses], axis=0)
    for m in range(0, width, 256):
        u = jnp.concatenate([use[0][:, m:m + 256] for use in uses], axis=0)
        put_wq(pl.ds(m, 256), dot(u, dqkv, TN))


def early_weights(uses):
    width = uses[0][0].shape[1]
    hd = HEADS_DEV * HEAD_DIM

    def body(ins, outs, scratch):
        gain_out, wo_out, wq_out = outs

        def put_gain(value):
            gain_out[...] = value

        def put_wo(cols, value):
            wo_out[:, cols] = value

        def put_wq(at, value):
            wq_out[at, :] = value

        weight_sums(ins, width, put_gain, put_wo, put_wq)

    return call(
        "early_weights", body, list(uses), [Mem((8, width), F32), Mem((hd, width), F32), Mem((width, 3 * hd), F32)])


def finish_kernel(g, h, fixed, saved, so_far, uses, sums):
    rows, width = saved[0].shape
    hd = HEADS_DEV * HEAD_DIM
    u, qkv, probs, att, stats = saved

    def body(ins, outs, scratch):
        g, h, fixed, (u_ref, qkv_ref, p_ref, att_ref, st_ref), _, uses, (gain_sum, wo_sum, wq_sum) = ins
        (to_odd, to_even), gain_out, wo_hbm, wq_hbm = outs
        e_ref, du_ref, dqkv_ref, dg_ref, wo_buf, wq_buf, sems = scratch
        copies = []
        odd = is_odd()

        def push(source, target):
            copy = pltpu.make_async_copy(source, target, sems.at[len(copies)])
            copies.append(copy.wait)
            copy.start()

        def put_gain(value):
            gain_out[...] = jnp.sum(gain_sum[...] + value, axis=0, keepdims=True).astype(BF16)

        def put_wo(cols, value):
            wo_buf[:, cols] = (wo_sum[:, cols] + value).astype(BF16)
            push(wo_buf.at[:, cols], wo_hbm.at[0, :, cols])

        def put_wq(at, value):
            wq_buf[at, :] = (wq_sum[at, :] + value).astype(BF16)
            push(wq_buf.at[at], wq_hbm.at[0, at])

        backward_body(g, h, *fixed, qkv_ref, p_ref, st_ref, [e_ref], dqkv_ref, dg_ref, du_ref)
        start, wait = by_place(
            odd, pltpu.make_async_copy(e_ref, to_odd.at[0], sems.at[0]),
            pltpu.make_async_copy(e_ref, to_even.at[0], sems.at[0]))
        start()
        copies.append(wait)
        weight_sums([*uses, (u_ref, dqkv_ref, att_ref, g, dg_ref)], width, put_gain, put_wo, put_wq)
        for wait in copies:
            wait()

    operands = [g, h, fixed, list(saved), [Far(x) for x in so_far], list(uses), list(sums)]
    first = len(jax.tree.leaves(operands[:4]))
    return call(
        "finish", body, operands,
        [
            [jax.ShapeDtypeStruct((1, rows, width), BF16)] * 2,
            Mem((1, width), BF16),
            jax.ShapeDtypeStruct((1, hd, width), BF16),
            jax.ShapeDtypeStruct((1, width, 3 * hd), BF16),
        ],
        [
            pltpu.VMEM((rows, width), BF16),
            pltpu.VMEM((rows, width), BF16),
            pltpu.VMEM(qkv.shape, BF16),
            pltpu.VMEM((8, width), F32),
            pltpu.VMEM((hd, width), BF16),
            pltpu.VMEM((width, 3 * hd), BF16),
            pltpu.SemaphoreType.DMA((1 + width // 512 + width // 256,)),
        ],
        alias=[(first, 0), (first + 1, 1)],
    )


def shards(acts_down, acts_up, cotangent_down, cotangent_up, ln_gain, w_qkv, w_out, band_offsets):
    sections = lax.axis_size("section")
    near = [(i, i ^ 1) for i in range(sections)]
    far = [(i, (i + (1 if i % 2 else -1)) % sections) for i in range(sections)]

    def swap_near(x):
        return [lax.ppermute(part, "section", near) for part in x]

    def swap_far(x):
        return [lax.ppermute(part, "section", far) for part in x]

    def after(x, other):
        return lax.optimization_barrier((x, other))[0]

    a0, b0, gain, wq, wo, mask, a1_out, a0_saved = first_kernel(
        band_offsets.T, ln_gain, w_qkv, w_out, acts_down, acts_up, 1)
    fixed = [gain, wq, wo]
    a1 = swap_far(a1_out)
    b1_out, b0_saved = forward_kernel(after(b0, a0_saved[4]), fixed, mask, NEAR_PARTS)
    b1 = swap_near(b1_out)
    b2_out, b1_saved = forward_kernel(after(b1, b0_saved[4]), fixed, mask, 1)
    b2 = swap_far(b2_out)
    a2_out, a1_saved = forward_kernel(after(a1, b1_saved[4]), fixed, mask, NEAR_PARTS, us=8)
    a2 = swap_near(a2_out)
    (out_even, out_odd), eb2, use_b2 = turn_kernel(
        after(b2, a1_saved[4]), fixed, mask, cotangent_up, cotangent_down, 1)
    cb1 = swap_far(eb2)
    (out_odd, out_even), ea2, use_a2 = turn_kernel(
        after(a2, use_b2[4]), fixed, mask, cotangent_down, cotangent_up, NEAR_PARTS, (out_odd, out_even))
    ca1 = swap_near(ea2)
    ea1, use_a1 = backward_kernel(after(ca1, use_a2[4]), a1, fixed, a1_saved, 1)
    ca0 = swap_far(ea1)
    eb1, use_b1 = backward_kernel(after(cb1, use_a1[4]), b1, fixed, b1_saved, NEAR_PARTS)
    cb0 = swap_near(eb1)
    sums = early_weights([use_b2, use_a2, use_a1, after(use_b1, use_b1[4])])
    (back_even, back_odd), use_b0 = end_kernel(after(cb0, sums[0]), b0, fixed, b0_saved)
    (back_odd, back_even), d_gain, d_wo, d_wq = finish_kernel(
        after(ca0, use_b0[4]), a0, fixed, a0_saved, (back_odd, back_even), [use_b0], sums)
    return out_odd, out_even, back_odd, back_even, d_gain, d_wq, d_wo


def solution(mesh):
    both = ("groups", "section")
    in_specs = (
        P(both, None, None), P(both, None, None), P(both, None, None), P(both, None, None),
        P("section", None), P("section", None, None), P("section", None, None), P(),
    )
    out_specs = (
        P(both, None, None), P(both, None, None), P(both, None, None), P(both, None, None),
        P(both, None), P(both, None, None), P(both, None, None),
    )
    return jax.shard_map(shards, mesh=mesh, in_specs=in_specs, out_specs=out_specs, check_vma=False)
```

time: 85.5 us -> 68.4 us (0.80)
  waiting for transfers between devices: 34.7 us -> 18.9 us
  local copies, waits for them, and re-layouts: 4.59 us -> 0.6 us
  starting transfers between devices: 7.22 us -> 11.1 us
  other arithmetic: 3.42 us -> 0 us
  Pallas kernels: 34.5 us -> 36.8 us
    ppermute x8 -> x12, waiting for transfers between devices: 34.7 us -> 18.9 us  [the longest x4 16 us: swap_far(): return [lax.ppermute(part, 'section', far) for part in x]]
    unnamed x15 -> x1, local copies, waits for them, and re-layouts: 4.59 us -> 0.6 us
    ppermute x8 -> x12, starting transfers between devices: 7.22 us -> 11.1 us  [the longest x8 6.48 us: swap_near(): return [lax.ppermute(part, 'section', near) for part in x]]
    pallas_call x13 -> x11, Pallas kernels: 34.5 us -> 36.8 us  [call(): pl.pallas_call(kernel, in_specs=[far if isinstance(x, Far) else VM for x...]
    broadcast_in_dim x2 -> x0, other arithmetic: 2.08 us -> none  [the longest x1 1.04 us: shards(): back_up[None]]
    select_n x2 -> x0, other arithmetic: 1.35 us -> none  [the longest x1 1.27 us: shards(): b0 = jnp.where(odd, acts_up[0], acts_down[0])]
  transfers between devices with their start and end apart: 8 -> 12, of which waited for: 4 -> 8; matrix products, arithmetic and copies ran while one was open for 1% -> 0% of each run, Pallas kernels for 26% -> 41%
where the time goes in v2:
time: 68.4 us; the launch traced here: 68.2 us
  Pallas kernels  36.8 us (54%)
  waiting for transfers between devices  18.9 us (28%)
  starting transfers between devices  11.1 us (16%)
  between operations  0.76 us (1%)
    pallas_call x11, Pallas kernels, call(): pl.pallas_call(kernel, in_specs=[far if isinstance(x, Far) else VM for x...  36.8 us
    ppermute x4, waiting for transfers between devices, swap_far(): return [lax.ppermute(part, 'section', far) for part in x]  16 us
    ppermute x8, starting transfers between devices, swap_near(): return [lax.ppermute(part, 'section', near) for part in x]  6.48 us
    ppermute x4, starting transfers between devices, swap_far(): return [lax.ppermute(part, 'section', far) for part in x]  4.66 us
    ppermute x8, waiting for transfers between devices, swap_near(): return [lax.ppermute(part, 'section', near) for part in x]  2.87 us
  transfers between devices with their start and end apart: 12, of which 8 were waited for; matrix products, arithmetic and copies ran while one was open for 0% of the time, Pallas kernels for 41%

profile of v2, /device:TPU:1, one launch (start us, length us, event | category | flops | bytes accessed | tf_op | source)
XLA Modules:
  0.0 68.2 jit_solution(8043682457047028397)
XLA Ops:
  0.6 3.6 %first.1 = (bf16[128,2048]{1,0:T(8,128)(2,1)S(1)}, bf16[128,2048]{1,0:T(8,128)(2,1)S(1)}, bf16[1,2048]{1,0:T(2,128)(2,1)S(1)}, bf16[2048,768]{1,0:T(8,128)(2,1)S...) custom-call(s32[2,4]{1,0:T(2,128)} %bitcast.1, ...), custom_call_target="tpu_custom_call" | custom-call | flops 2000000 | bytes 200 | tf_op jit(solution)/shard_map/first/pallas_call | solution.py:161
  4.2 2.7 %collective-permute-start = (bf16[128,2048]{1,0:T(8,128)(2,1)S(1)}, bf16[128,2048]{1,0:T(8,128)(2,1)S(1)}, u32[]{:S(2)}, u32[]{:S(2)}) collective-permute-start(bf16[128,2048]{1,0:T(8,128)(2,1)S(1)} %get-tuple-element.93), channel_id=1, source_target_pairs={{0,15},{1,2},{2,1},{3,4},{4,3},{5,6},{6,5},{7,8},{8,7},{9,10},{10,... | collective-permute-start | bytes 1572872 | tf_op jit(solution)/shard_map/ppermute | solution.py:445
  6.9 1.8 %forward.3 = (bf16[64,2048]{1,0:T(8,128)(2,1)S(1)}, bf16[64,2048]{1,0:T(8,128)(2,1)S(1)}, bf16[128,2048]{1,0:T(8,128)(2,1)S(1)}, bf16[128,768]{1,0:T(8,128)(2,1)...) custom-call(bf16[128,2048]{1,0:T(8,128)(2,1)S(1)} %get-tuple-element.96.refs_0_.refs_2_, ...), custom_call_target="tpu_custom_call" | custom-call | flops 2000000 | bytes 200 | tf_op jit(solution)/shard_map/forward/pallas_call | solution.py:161
  8.7 2.9 %collective-permute-start.1 = (bf16[64,2048]{1,0:T(8,128)(2,1)S(1)}, bf16[64,2048]{1,0:T(8,128)(2,1)S(1)}, u32[]{:S(2)}, u32[]{:S(2)}) collective-permute-start(bf16[64,2048]{1,0:T(8,128)(2,1)S(1)} %get-tuple-element.101), channel_id=1, source_target_pairs={{0,1},{1,0},{2,3},{3,2},{4,5},{5,4},{6,7},{7,6},{8,9},{9,8},{10,11... | collective-permute-start | bytes 786440 | tf_op jit(solution)/shard_map/ppermute | solution.py:442
  11.7 1.1 %collective-permute-done.1.refs_0_.refs_1_ = bf16[64,2048]{1,0:T(8,128)(2,1)S(1)} collective-permute-done((bf16[64,2048]{1,0:T(8,128)(2,1)S(1)}, bf16[64,2048]{1,0:T(8,128)(2,1)S(1)}, u32[]{:S(2)}, u32[]{:S(2)}) %collective-permute-start.1) | collective-permute-done | bytes 262176 | tf_op jit(solution)/shard_map/ppermute | solution.py:442
  13.1 1.8 %forward.4 = (bf16[128,2048]{1,0:T(8,128)(2,1)S(1)}, bf16[128,2048]{1,0:T(8,128)(2,1)S(1)}, bf16[128,768]{1,0:T(8,128)(2,1)S(1)}, f32[2,128,128]{2,1,0:T(8,128)S...) custom-call(bf16[64,2048]{1,0:T(8,128)(2,1)S(1)} %collective-permute-done.1.refs_0_.refs_1_, ...), custom_call_target="tpu_custom_call" | custom-call | flops 2000000 | bytes 200 | tf_op jit(solution)/shard_map/forward/pallas_call | solution.py:161
  15.0 9.2 %collective-permute-done.refs_0_.refs_2_ = bf16[128,2048]{1,0:T(8,128)(2,1)S(1)} collective-permute-done((bf16[128,2048]{1,0:T(8,128)(2,1)S(1)}, bf16[128,2048]{1,0:T(8,128)(2,1)S(1)}, u32[]{:S(2)}, u32[]{:S(2)}) %collective-permute-start) | collective-permute-done | bytes 524320 | tf_op jit(solution)/shard_map/ppermute | solution.py:445
  24.2 1.8 %forward.5 = (bf16[64,2048]{1,0:T(8,128)(2,1)S(1)}, bf16[64,2048]{1,0:T(8,128)(2,1)S(1)}, bf16[128,2048]{1,0:T(8,128)(2,1)S(1)}, bf16[128,768]{1,0:T(8,128)(2,1)...) custom-call(bf16[128,2048]{1,0:T(8,128)(2,1)S(1)} %collective-permute-done.refs_0_.refs_2_, ...), custom_call_target="tpu_custom_call" | custom-call | flops 8000000000 | bytes 800000 | tf_op jit(solution)/shard_map/forward/pallas_call | solution.py:161
  26.1 0.5 collective-permute-start.4
  26.6 4.0 %collective-permute-done.5.refs_0_ = bf16[128,2048]{1,0:T(8,128)(2,1)S(1)} collective-permute-done((bf16[128,2048]{1,0:T(8,128)(2,1)S(1)}, bf16[128,2048]{1,0:T(8,128)(2,1)S(1)}, u32[]{:S(2)}, u32[]{:S(2)}) %collective-permute-start.5) | collective-permute-done | bytes 524320 | tf_op jit(solution)/shard_map/ppermute | solution.py:445
  30.6 4.9 %turn.2 = (bf16[1,128,2048]{2,1,0:T(8,128)(2,1)}, bf16[1,128,2048]{2,1,0:T(8,128)(2,1)}, bf16[128,2048]{1,0:T(8,128)(2,1)S(1)}, bf16[128,2048]{1,0:T(8,128)(2,1)...) custom-call(bf16[128,2048]{1,0:T(8,128)(2,1)S(1)} %collective-permut, ...), custom_call_target="tpu_custom_call" | custom-call | flops 2000000 | bytes 200 | tf_op jit(solution)/shard_map/turn/pallas_call | solution.py:161
  35.5 1.8 %collective-permute-start.9 = (bf16[128,2048]{1,0:T(8,128)(2,1)S(1)}, bf16[128,2048]{1,0:T(8,128)(2,1)S(1)}, u32[]{:S(2)}, u32[]{:S(2)}) collective-permute-start(bf16[128,2048]{1,0:T(8,128)(2,1)S(1)} %get-tuple-element.128), channel_id=1, source_target_pairs={{0,15},{1,2},{2,1},{3,4},{4,3},{5,6},{6,5},{7,8},{8,7},{9,10},{10,... | collective-permute-start | bytes 1572872 | tf_op jit(solution)/shard_map/ppermute | solution.py:445
  37.3 5.6 %turn.3 = (bf16[1,128,2048]{2,1,0:T(8,128)(2,1)}, bf16[1,128,2048]{2,1,0:T(8,128)(2,1)}, bf16[64,2048]{1,0:T(8,128)(2,1)S(1)}, bf16[64,2048]{1,0:T(8,128)(2,1)S(...) custom-call(bf16[64,2048]{1,0:T(8,128)(2,1)S(1)} %collective-permute, ...), custom_call_target="tpu_custom_call", output_to_operand_aliasing={{0}: (8, {}), {1}: (9, {})} | custom-call | flops 2000000 | bytes 200 | tf_op jit(solution)/shard_map/turn/pallas_call | solution.py:161
  43.0 0.5 collective-permute-start.7
  43.5 1.0 %collective-permute-done.6.refs_0_.refs_13_ = bf16[64,2048]{1,0:T(8,128)(2,1)S(1)} collective-permute-done((bf16[64,2048]{1,0:T(8,128)(2,1)S(1)}, bf16[64,2048]{1,0:T(8,128)(2,1)S(1)}, u32[]{:S(2)}, u32[]{:S(2)}) %collective-permute-start.6) | collective-permute-done | bytes 262176 | tf_op jit(solution)/shard_map/ppermute | solution.py:442
  44.9 2.9 %backward.2 = (bf16[128,2048]{1,0:T(8,128)(2,1)S(1)}, bf16[128,768]{1,0:T(8,128)(2,1)S(1)}, f32[8,2048]{1,0:T(8,128)S(1)}) custom-call(bf16[64,2048]{1,0:T(8,128)(2,1)S(1)} %collective-permute-done.6.refs_0_.refs_13_, bf16[64,2048]{1,0:T(8,128)(2,1)S(1)} %collective-permute-done.7.refs_1_.refs_14_, ...), custom_call_target="tpu_custom_call" | custom-call | flops 2000000 | bytes 200 | tf_op jit(solution)/shard_map/backward/pallas_call | solution.py:161
  47.9 1.0 %collective-permute-done.9.refs_0_.refs_19_ = bf16[128,2048]{1,0:T(8,128)(2,1)S(1)} collective-permute-done((bf16[128,2048]{1,0:T(8,128)(2,1)S(1)}, bf16[128,2048]{1,0:T(8,128)(2,1)S(1)}, u32[]{:S(2)}, u32[]{:S(2)}) %collective-permute-start.9) | collective-permute-done | bytes 524320 | tf_op jit(solution)/shard_map/ppermute | solution.py:445
  49.0 2.9 %backward.3 = (bf16[64,2048]{1,0:T(8,128)(2,1)S(1)}, bf16[64,2048]{1,0:T(8,128)(2,1)S(1)}, bf16[128,768]{1,0:T(8,128)(2,1)S(1)}, f32[8,2048]{1,0:T(8,128)S(1)}) custom-call(bf16[128,2048]{1,0:T(8,128)(2,1)S(1)} %collective-permute-done.9.refs_0_.refs_19_, bf16[64,2048]{1,0:T(8,128)(2,1)S(1)} %collective-permute-done.1.refs_0_.refs_1_, ...), custom_call_target="tpu_custom_call" | custom-call | flops 2000000 | bytes 200 | tf_op jit(solution)/shard_map/backward/pallas_call | solution.py:161
  51.9 2.2 %collective-permute-start.10 = (bf16[64,2048]{1,0:T(8,128)(2,1)S(1)}, bf16[64,2048]{1,0:T(8,128)(2,1)S(1)}, u32[]{:S(2)}, u32[]{:S(2)}) collective-permute-start(bf16[64,2048]{1,0:T(8,128)(2,1)S(1)} %get-tuple-element.133), channel_id=1, source_target_pairs={{0,1},{1,0},{2,3},{3,2},{4,5},{5,4},{6,7},{7,6},{8,9},{9,8},{10,11... | collective-permute-start | bytes 786440 | tf_op jit(solution)/shard_map/ppermute | solution.py:442
  54.2 2.4 %early_weights.1 = (f32[8,2048]{1,0:T(8,128)S(1)}, f32[256,2048]{1,0:T(8,128)S(1)}, f32[2048,768]{1,0:T(8,128)S(1)}) custom-call(bf16[128,2048]{1,0:T(8,128)(2,1)S(1)} %get-tuple-element.135.refs_0_, bf16[128,768]{1,0:T(8,128)(2,1)S(1)} %get-tuple-element.136.refs_1_, bf16[128,256]{1,0:T(8,128)(2,1)S(1)} %get-tuple-element.137.refs_2_, ...), custom_call_target="tpu_custom_call" | custom-call | flops 2000000 | bytes 200 | tf_op jit(solution)/shard_map/early_weights/pallas_call | solution.py:161
  56.6 3.7 %end.1 = (bf16[1,128,2048]{2,1,0:T(8,128)(2,1)}, bf16[1,128,2048]{2,1,0:T(8,128)(2,1)}, bf16[128,768]{1,0:T(8,128)(2,1)S(1)}, f32[8,2048]{1,0:T(8,128)S(1)}) custom-call(bf16[64,2048]{1,0:T(8,128)(2,1)S(1)} %collective-permute-done.10.refs_0_.refs_15_, bf16[64,2048]{1,0:T(8,128)(2,1)S(1)} %collective-permute-done.11.refs_1_.refs_16_, ...), custom_call_target="tpu_custom_call" | custom-call | flops 2000000 | bytes 200 | tf_op jit(solution)/shard_map/end/pallas_call | solution.py:161
  60.4 1.7 %collective-permute-done.8.refs_0_ = bf16[128,2048]{1,0:T(8,128)(2,1)S(1)} collective-permute-done((bf16[128,2048]{1,0:T(8,128)(2,1)S(1)}, bf16[128,2048]{1,0:T(8,128)(2,1)S(1)}, u32[]{:S(2)}, u32[]{:S(2)}) %collective-permute-start.8) | collective-permute-done | bytes 524320 | tf_op jit(solution)/shard_map/ppermute | solution.py:445
  62.1 5.5 %finish.1 = (bf16[1,128,2048]{2,1,0:T(8,128)(2,1)}, bf16[1,128,2048]{2,1,0:T(8,128)(2,1)}, bf16[1,2048]{1,0:T(2,128)(2,1)S(1)}, bf16[1,256,2048]{2,1,0:T(8,128)(2,1)}, bf16[1,2048,768]{2,1,0:T(8,128)(2,1)}) custom-call(bf16[128,2048]{1,0:T(8,128)(2,1)S(1)} %collective-permute-done.8.refs_0_, ...), custom_call_target="tpu_custom_call", output_to_operand_aliasing={{0}: (10, {}), {1}: (11, {})} | custom-call | flops 2000000 | bytes 200 | tf_op jit(solution)/shard_map/finish/pallas_call | solution.py:161
  67.6 0.6 copy.23
  (12 shorter events, 1.2 us)
Async XLA Ops:
  4.2 20.1 %collective-permute-start = (bf16[128,2048]{1,0:T(8,128)(2,1)S(1)}, bf16[128,2048]{1,0:T(8,128)(2,1)S(1)}, u32[]{:S(2)}, u32[]{:S(2)}) collective-permute-start(bf16[128,2048]{1,0:T(8,128)(2,1)S(1)} %get-tuple-element.93), channel_id=1, source_target_pairs={{0,15},{1,2},{2,1},{3,4},{4,3},{5,6},{6,5},{7,8},{8,7},{9,10},{10,... | collective-permute-start | bytes 1572872 | tf_op jit(solution)/shard_map/ppermute | solution.py:445
  8.7 4.1 %collective-permute-start.1 = (bf16[64,2048]{1,0:T(8,128)(2,1)S(1)}, bf16[64,2048]{1,0:T(8,128)(2,1)S(1)}, u32[]{:S(2)}, u32[]{:S(2)}) collective-permute-start(bf16[64,2048]{1,0:T(8,128)(2,1)S(1)} %get-tuple-element.101), channel_id=1, source_target_pairs={{0,1},{1,0},{2,3},{3,2},{4,5},{5,4},{6,7},{7,6},{8,9},{9,8},{10,11... | collective-permute-start | bytes 786440 | tf_op jit(solution)/shard_map/ppermute | solution.py:442
  11.6 1.5 %collective-permute-start.2 = (bf16[64,2048]{1,0:T(8,128)(2,1)S(1)}, bf16[64,2048]{1,0:T(8,128)(2,1)S(1)}, u32[]{:S(2)}, u32[]{:S(2)}) collective-permute-start(bf16[64,2048]{1,0:T(8,128)(2,1)S(1)} %get-tuple-element.102), channel_id=1, source_target_pairs={{0,1},{1,0},{2,3},{3,2},{4,5},{5,4},{6,7},{7,6},{8,9},{9,8},{10,11... | collective-permute-start | bytes 786440 | tf_op jit(solution)/shard_map/ppermute | solution.py:442
  14.9 15.7 %collective-permute-start.5 = (bf16[128,2048]{1,0:T(8,128)(2,1)S(1)}, bf16[128,2048]{1,0:T(8,128)(2,1)S(1)}, u32[]{:S(2)}, u32[]{:S(2)}) collective-permute-start(bf16[128,2048]{1,0:T(8,128)(2,1)S(1)} %get-tuple-element.110), channel_id=1, source_target_pairs={{0,15},{1,2},{2,1},{3,4},{4,3},{5,6},{6,5},{7,8},{8,7},{9,10},{10,... | collective-permute-start | bytes 1572872 | tf_op jit(solution)/shard_map/ppermute | solution.py:445
  26.0 11.3 %collective-permute-start.3 = (bf16[64,2048]{1,0:T(8,128)(2,1)S(1)}, bf16[64,2048]{1,0:T(8,128)(2,1)S(1)}, u32[]{:S(2)}, u32[]{:S(2)}) collective-permute-start(bf16[64,2048]{1,0:T(8,128)(2,1)S(1)} %get-tuple-element.108), channel_id=1, source_target_pairs={{0,1},{1,0},{2,3},{3,2},{4,5},{5,4},{6,7},{7,6},{8,9},{9,8},{10,11... | collective-permute-start | bytes 786440 | tf_op jit(solution)/shard_map/ppermute | solution.py:442
  26.1 11.2 %collective-permute-start.4 = (bf16[64,2048]{1,0:T(8,128)(2,1)S(1)}, bf16[64,2048]{1,0:T(8,128)(2,1)S(1)}, u32[]{:S(2)}, u32[]{:S(2)}) collective-permute-start(bf16[64,2048]{1,0:T(8,128)(2,1)S(1)} %get-tuple-element.109), channel_id=1, source_target_pairs={{0,1},{1,0},{2,3},{3,2},{4,5},{5,4},{6,7},{7,6},{8,9},{9,8},{10,11... | collective-permute-start | bytes 786440 | tf_op jit(solution)/shard_map/ppermute | solution.py:442
  35.5 13.5 %collective-permute-start.9 = (bf16[128,2048]{1,0:T(8,128)(2,1)S(1)}, bf16[128,2048]{1,0:T(8,128)(2,1)S(1)}, u32[]{:S(2)}, u32[]{:S(2)}) collective-permute-start(bf16[128,2048]{1,0:T(8,128)(2,1)S(1)} %get-tuple-element.128), channel_id=1, source_target_pairs={{0,15},{1,2},{2,1},{3,4},{4,3},{5,6},{6,5},{7,8},{8,7},{9,10},{10,... | collective-permute-start | bytes 1572872 | tf_op jit(solution)/shard_map/ppermute | solution.py:445
  42.9 1.6 %collective-permute-start.6 = (bf16[64,2048]{1,0:T(8,128)(2,1)S(1)}, bf16[64,2048]{1,0:T(8,128)(2,1)S(1)}, u32[]{:S(2)}, u32[]{:S(2)}) collective-permute-start(bf16[64,2048]{1,0:T(8,128)(2,1)S(1)} %get-tuple-element.120), channel_id=1, source_target_pairs={{0,1},{1,0},{2,3},{3,2},{4,5},{5,4},{6,7},{7,6},{8,9},{9,8},{10,11... | collective-permute-start | bytes 786440 | tf_op jit(solution)/shard_map/ppermute | solution.py:442
  43.0 1.9 %collective-permute-start.7 = (bf16[64,2048]{1,0:T(8,128)(2,1)S(1)}, bf16[64,2048]{1,0:T(8,128)(2,1)S(1)}, u32[]{:S(2)}, u32[]{:S(2)}) collective-permute-start(bf16[64,2048]{1,0:T(8,128)(2,1)S(1)} %get-tuple-element.121), channel_id=1, source_target_pairs={{0,1},{1,0},{2,3},{3,2},{4,5},{5,4},{6,7},{7,6},{8,9},{9,8},{10,11... | collective-permute-start | bytes 786440 | tf_op jit(solution)/shard_map/ppermute | solution.py:442
  47.8 14.3 %collective-permute-start.8 = (bf16[128,2048]{1,0:T(8,128)(2,1)S(1)}, bf16[128,2048]{1,0:T(8,128)(2,1)S(1)}, u32[]{:S(2)}, u32[]{:S(2)}) collective-permute-start(bf16[128,2048]{1,0:T(8,128)(2,1)S(1)} %get-tuple-element.127), channel_id=1, source_target_pairs={{0,15},{1,2},{2,1},{3,4},{4,3},{5,6},{6,5},{7,8},{8,7},{9,10},{10,... | collective-permute-start | bytes 1572872 | tf_op jit(solution)/shard_map/ppermute | solution.py:445
  51.9 4.7 %collective-permute-start.10 = (bf16[64,2048]{1,0:T(8,128)(2,1)S(1)}, bf16[64,2048]{1,0:T(8,128)(2,1)S(1)}, u32[]{:S(2)}, u32[]{:S(2)}) collective-permute-start(bf16[64,2048]{1,0:T(8,128)(2,1)S(1)} %get-tuple-element.133), channel_id=1, source_target_pairs={{0,1},{1,0},{2,3},{3,2},{4,5},{5,4},{6,7},{7,6},{8,9},{9,8},{10,11... | collective-permute-start | bytes 786440 | tf_op jit(solution)/shard_map/ppermute | solution.py:442
  54.1 2.5 %collective-permute-start.11 = (bf16[64,2048]{1,0:T(8,128)(2,1)S(1)}, bf16[64,2048]{1,0:T(8,128)(2,1)S(1)}, u32[]{:S(2)}, u32[]{:S(2)}) collective-permute-start(bf16[64,2048]{1,0:T(8,128)(2,1)S(1)} %get-tuple-element.134), channel_id=1, source_target_pairs={{0,1},{1,0},{2,3},{3,2},{4,5},{5,4},{6,7},{7,6},{8,9},{9,8},{10,11... | collective-permute-start | bytes 786440 | tf_op jit(solution)/shard_map/ppermute | solution.py:442

commit v3 on v2

v3 whole, which is shorter than its diff:
```python
import math

import jax
import jax.numpy as jnp
from jax import lax
from jax.experimental import pallas as pl
from jax.experimental.pallas import tpu as pltpu
from jax.sharding import PartitionSpec as P

HEADS_DEV = 2
HEAD_DIM = 128
BLOCK = 32
CHUNK = 16
F32 = jnp.float32
BF16 = jnp.bfloat16
NT = (((1,), (1,)), ((), ()))
TN = (((0,), (0,)), ((), ()))
SCALE = 1.0 / math.sqrt(HEAD_DIM)
VM = pl.BlockSpec(memory_space=pltpu.VMEM)
NEAR_PARTS = 2


def dot(a, b, dims=(((1,), (0,)), ((), ()))):
    return lax.dot_general(a, b, dims, preferred_element_type=F32)


def mask_body(odd, offs_ref, rows):
    row = lax.broadcasted_iota(jnp.int32, (rows, rows), 0)
    col = lax.broadcasted_iota(jnp.int32, (rows, rows), 1)
    row_block = row // BLOCK
    col_block = col // BLOCK
    near = row_block == col_block
    for block in range(offs_ref.shape[1]):
        for listed in range(offs_ref.shape[0]):
            near = near | ((row_block == block) & (col_block == block - offs_ref[listed, block]))
    keep = (col <= row) & (near | jnp.logical_not(odd))
    return jnp.where(keep, 1.0, 0.0).astype(F32)


def read(refs, at, size, cols=slice(None)):
    held = refs[0].shape[0]
    return refs[at // held][pl.ds(at % held, size), cols]


def write(refs, at, size, value, cols=slice(None)):
    held = refs[0].shape[0]
    refs[at // held][pl.ds(at % held, size), cols] = value


def whole(refs, cols=slice(None)):
    return jnp.concatenate([ref[:, cols] for ref in refs], axis=0)


def forward_body(h, gain_ref, wq_ref, wo_ref, mask_ref, out, u_ref, qkv_ref, p_ref, att_ref, st_ref, waits=None):
    rows, width = u_ref.shape
    hd = HEADS_DEV * HEAD_DIM
    gain = gain_ref[...].astype(F32)
    for start in range(0, rows, CHUNK):
        part = pl.ds(start, CHUNK)
        x = read(h, start, CHUNK).astype(F32)
        mean = jnp.sum(x, axis=-1, keepdims=True) * (1.0 / width)
        centred = x - mean
        rstd = lax.rsqrt(jnp.sum(centred * centred, axis=-1, keepdims=True) * (1.0 / width) + 1e-05)
        u_ref[part, :] = (centred * rstd * gain).astype(BF16)
        st_ref[part, :] = jnp.concatenate(
            [jnp.broadcast_to(mean, (CHUNK, 128)), jnp.broadcast_to(rstd, (CHUNK, 128))], axis=1)
    for n in range(3):
        if waits:
            waits[n].wait()
        qkv_ref[:, n * hd:(n + 1) * hd] = dot(u_ref[...], wq_ref[:, n * hd:(n + 1) * hd]).astype(BF16)
    keep = mask_ref[...]
    heads = [pl.ds(head * HEAD_DIM, HEAD_DIM) for head in range(HEADS_DEV)]
    scores = [dot(qkv_ref[:, cols], qkv_ref[:, pl.ds(hd + cols.start, HEAD_DIM)], NT) for cols in heads]
    weighted = [jnp.where(keep > 0.0, jnp.exp(score * SCALE), 0.0) for score in scores]
    inverse = [1.0 / jnp.sum(value, axis=-1, keepdims=True) for value in weighted]
    probs = [value * scale for value, scale in zip(weighted, inverse)]
    mixed = [
        dot(value.astype(BF16), qkv_ref[:, pl.ds(2 * hd + cols.start, HEAD_DIM)]) for value, cols in zip(probs, heads)
    ]
    for head, cols in enumerate(heads):
        p_ref[head] = probs[head]
        att_ref[:, cols] = mixed[head].astype(BF16)
    if waits:
        waits[3].wait()
    for n in range(0, width, 512):
        cols = pl.ds(n, 512)
        value = dot(att_ref[...], wo_ref[:, cols])
        size = min(out[0].shape[0], h[0].shape[0])
        for at in range(0, rows, size):
            write(out, at, size, (read(h, at, size, cols).astype(F32) + value[at:at + size]).astype(BF16), cols)


def attention_reverse(g, wot_ref, qkv_ref, p_ref, dqkv_ref):
    hd = HEADS_DEV * HEAD_DIM
    datt = dot(whole(g), wot_ref[...]).astype(BF16)
    heads = [pl.ds(head * HEAD_DIM, HEAD_DIM) for head in range(HEADS_DEV)]
    keys = [pl.ds(hd + cols.start, HEAD_DIM) for cols in heads]
    values = [pl.ds(2 * hd + cols.start, HEAD_DIM) for cols in heads]
    das = [datt[:, cols.start:cols.start + HEAD_DIM] for cols in heads]
    probs = [p_ref[head] for head in range(HEADS_DEV)]
    dps = [dot(da, qkv_ref[:, cols], NT).astype(BF16).astype(F32) for da, cols in zip(das, values)]
    dvs = [dot(prob.astype(BF16), da, TN) for prob, da in zip(probs, das)]
    totals = [jnp.sum(dp * prob, axis=-1, keepdims=True) for dp, prob in zip(dps, probs)]
    dss = [(prob * (dp - total) * SCALE).astype(BF16) for prob, dp, total in zip(probs, dps, totals)]
    dqs = [dot(ds, qkv_ref[:, cols]) for ds, cols in zip(dss, keys)]
    dks = [dot(ds, qkv_ref[:, cols], TN) for ds, cols in zip(dss, heads)]
    for head in range(HEADS_DEV):
        dqkv_ref[:, values[head]] = dvs[head].astype(BF16)
        dqkv_ref[:, heads[head]] = dqs[head].astype(BF16)
        dqkv_ref[:, keys[head]] = dks[head].astype(BF16)


def lanes(column):
    return jnp.broadcast_to(column, (column.shape[0], 128))


def norm_reverse(g, h, gain_ref, wqt_ref, wg_ref, qkv_ref, st_ref, e, dqkv_ref, dg_ref, done=None):
    rows, width = dqkv_ref.shape[0], wqt_ref.shape[1]
    dqkv32 = dqkv_ref[...].astype(F32)
    first = jnp.sum(dqkv32 * wg_ref[...], axis=-1, keepdims=True) * (1.0 / width)
    second = jnp.sum(dqkv32 * qkv_ref[...].astype(F32), axis=-1, keepdims=True) * (1.0 / width)
    mean, rstd = st_ref[:, 0:128], st_ref[:, 128:256]
    first, second = lanes(first) * rstd, lanes(second) * rstd
    for block in range(0, width, 512):
        wide = dot(dqkv_ref[...], wqt_ref[:, block:block + 512])
        for n in range(0, 512, 128):
            cols = pl.ds(block + n, 128)
            du = wide[:, n:n + 128]
            xhat = (whole(h, cols).astype(F32) - mean) * rstd
            dg_ref[:, cols] = jnp.sum((du * xhat).reshape(rows // 8, 8, 128), axis=0)
            gain = gain_ref[:, cols].astype(F32)
            value = (du * gain) * rstd - first - xhat * second + whole(g, cols).astype(F32)
            size = e[0].shape[0]
            for part in range(len(e)):
                e[part][:, cols] = value[part * size:(part + 1) * size].astype(BF16)
        if done:
            done(pl.ds(block, 512))


def backward_body(g, h, gain_ref, wqt_ref, wot_ref, wg_ref, qkv_ref, p_ref, st_ref, e, dqkv_ref, dg_ref):
    attention_reverse(g, wot_ref, qkv_ref, p_ref, dqkv_ref)
    norm_reverse(g, h, gain_ref, wqt_ref, wg_ref, qkv_ref, st_ref, e, dqkv_ref, dg_ref)


def params(mib):
    return pltpu.CompilerParams(vmem_limit_bytes=mib << 20)


def cost(us):
    return pl.CostEstimate(flops=int(us * 1e9), bytes_accessed=int(us * 1e5), transcendentals=0)


def by_place(odd, when_odd, when_even):
    def start():
        pl.when(odd)(when_odd.start)
        pl.when(jnp.logical_not(odd))(when_even.start)

    return start, when_odd.wait


def is_odd():
    return lax.axis_index("section") % 2 == 1


def call(name, body, operands, outs, scratch=(), hbm=(), alias=(), us=0.002, mib=24):
    flat_in, tree_in = jax.tree.flatten(operands, is_leaf=lambda x: isinstance(x, Far))
    flat_out, tree_out = jax.tree.flatten(outs, is_leaf=lambda x: isinstance(x, (jax.ShapeDtypeStruct, Mem)))

    def kernel(*refs):
        a, b = len(flat_in), len(flat_in) + len(flat_out)
        body(jax.tree.unflatten(tree_in, refs[:a]), jax.tree.unflatten(tree_out, refs[a:b]), refs[b:])

    far = pl.BlockSpec(memory_space=pltpu.HBM)
    result = pl.pallas_call(
        kernel,
        in_specs=[far if isinstance(x, Far) else VM for x in flat_in],
        out_specs=[far if isinstance(x, jax.ShapeDtypeStruct) else VM for x in flat_out],
        out_shape=[x if isinstance(x, jax.ShapeDtypeStruct) else pltpu.VMEM(x.shape, x.dtype) for x in flat_out],
        scratch_shapes=list(scratch),
        input_output_aliases=dict(alias),
        compiler_params=params(mib),
        cost_estimate=cost(us),
        name=name,
    )(*[x.array if isinstance(x, Far) else x for x in flat_in])
    return jax.tree.unflatten(tree_out, result)


class Far:
    def __init__(self, array):
        self.array = pltpu.with_memory_space_constraint(array, pltpu.HBM)


class Mem:
    def __init__(self, shape, dtype):
        self.shape, self.dtype = shape, dtype


def stream(rows, width, parts):
    return [Mem((rows // parts, width), BF16) for _ in range(parts)]


def saved_outs(rows, width):
    hd = HEADS_DEV * HEAD_DIM
    return [
        Mem((rows, width), BF16),
        Mem((rows, 3 * hd), BF16),
        Mem((HEADS_DEV, rows, rows), F32),
        Mem((rows, hd), BF16),
        Mem((rows, 256), F32),
    ]


def first_kernel(offs, gain, wq, wo, down, up, parts):
    _, rows, width = down.shape
    hd = HEADS_DEV * HEAD_DIM

    def body(ins, outs, scratch):
        offs_hbm, gain_hbm, wq_hbm, wo_hbm, down_hbm, up_hbm = ins
        (a_ref,), (b_ref,), gain_ref, wq_ref, wo_ref, mask_ref, out, saved = outs
        offs_ref, sems = scratch
        odd = is_odd()

        def pick(source, target, sem):
            return pltpu.make_async_copy(source, target, sems.at[sem])

        a_start, a_wait = by_place(odd, pick(down_hbm.at[0], a_ref, 0), pick(up_hbm.at[0], a_ref, 0))
        b_start, b_wait = by_place(odd, pick(up_hbm.at[0], b_ref, 1), pick(down_hbm.at[0], b_ref, 1))
        offs_copy = pick(offs_hbm, offs_ref, 2)
        gain_copy = pick(gain_hbm, gain_ref, 3)
        wo_copy = pick(wo_hbm.at[0], wo_ref, 4)
        cols = [pl.ds(n * hd, hd) for n in range(3)]
        wq_copies = [pick(wq_hbm.at[0, :, cols[n]], wq_ref.at[:, cols[n]], 5 + n) for n in range(3)]
        a_start()
        gain_copy.start()
        offs_copy.start()
        for copy in wq_copies:
            copy.start()
        wo_copy.start()
        b_start()
        offs_copy.wait()
        mask_ref[...] = mask_body(odd, offs_ref, rows)
        a_wait()
        gain_copy.wait()
        forward_body([a_ref], gain_ref, wq_ref, wo_ref, mask_ref, out, *saved, waits=wq_copies + [wo_copy])
        b_wait()

    return call(
        "first", body, [Far(x) for x in (offs, gain, wq, wo, down, up)],
        [
            stream(rows, width, 1), stream(rows, width, 1), Mem(gain.shape, BF16), Mem(wq.shape[1:], BF16),
            Mem(wo.shape[1:], BF16), Mem((rows, rows), F32), stream(rows, width, parts), saved_outs(rows, width),
        ],
        [pltpu.SMEM(offs.shape, jnp.int32), pltpu.SemaphoreType.DMA((8,))],
    )


def forward_kernel(h, fixed, mask, parts, us=0.002):
    rows, width = h[0].shape[0] * len(h), h[0].shape[1]

    def body(ins, outs, scratch):
        h, fixed, mask_ref = ins
        out, saved = outs
        forward_body(h, *fixed, mask_ref, out, *saved)

    return call("forward", body, [h, fixed, mask], [stream(rows, width, parts), saved_outs(rows, width)], us=us)


def prepare_kernel(gain, wq, wo, tie, down, up):
    _, rows, width = down.shape
    hd = HEADS_DEV * HEAD_DIM

    def body(ins, outs, scratch):
        gain_ref, wq_ref, wo_ref, _, down_hbm, up_hbm = ins
        wqt_ref, wot_ref, wg_ref, (a_ref,), (b_ref,) = outs
        (sems,) = scratch
        odd = is_odd()

        def pick(source, target, sem):
            return pltpu.make_async_copy(source.at[0], target, sems.at[sem])

        a_start, a_wait = by_place(odd, pick(down_hbm, a_ref, 0), pick(up_hbm, a_ref, 0))
        b_start, b_wait = by_place(odd, pick(up_hbm, b_ref, 1), pick(down_hbm, b_ref, 1))
        a_start()
        b_start()
        for at in range(0, width, 256):
            wqt_ref[:, at:at + 256] = wq_ref[at:at + 256, :].T
            wot_ref[at:at + 256, :] = wo_ref[:, at:at + 256].T
        wg_ref[...] = dot(gain_ref[...], wq_ref[...])
        a_wait()
        b_wait()

    return call(
        "prepare", body, [gain, wq, wo, tie, Far(down), Far(up)],
        [Mem((3 * hd, width), BF16), Mem((width, hd), BF16), Mem((1, 3 * hd), F32),
         stream(rows, width, 1), stream(rows, width, 1)],
        [pltpu.SemaphoreType.DMA((2,))],
    )


def turn_kernel(h, g, fixed, mask, turned, parts):
    rows, width = h[0].shape[0] * len(h), h[0].shape[1]
    hd = HEADS_DEV * HEAD_DIM

    def body(ins, outs, scratch):
        h, g, fixed, mask_ref, turned = ins
        out, e, (u_ref, dqkv_ref, att_ref, dg_ref) = outs
        qkv_ref, p_ref, st_ref = scratch
        forward_body(h, *fixed, mask_ref, out, u_ref, qkv_ref, p_ref, att_ref, st_ref)
        backward_body(g, h, fixed[0], *turned, qkv_ref, p_ref, st_ref, e, dqkv_ref, dg_ref)

    out, e, (u, dqkv, att, dgain) = call(
        "turn", body, [h, g, fixed, mask, turned],
        [
            stream(rows, width, 1),
            stream(rows, width, parts),
            [Mem((rows, width), BF16), Mem((rows, 3 * hd), BF16), Mem((rows, hd), BF16), Mem((8, width), F32)],
        ],
        [
            pltpu.VMEM((rows, 3 * hd), BF16),
            pltpu.VMEM((HEADS_DEV, rows, rows), F32),
            pltpu.VMEM((rows, 256), F32),
        ],
    )
    return out, e, (u, dqkv, att, g, dgain)


def backward_kernel(g, h, gain, turned, saved, parts):
    rows, width = saved[0].shape
    u, qkv, probs, att, stats = saved

    def body(ins, outs, scratch):
        g, h, gain_ref, turned, (qkv_ref, p_ref, st_ref) = ins
        e, dqkv_ref, dg_ref = outs
        backward_body(g, h, gain_ref, *turned, qkv_ref, p_ref, st_ref, e, dqkv_ref, dg_ref)

    e, dqkv, dgain = call(
        "backward", body, [g, h, gain, turned, [qkv, probs, stats]],
        [stream(rows, width, parts), Mem(qkv.shape, BF16), Mem((8, width), F32)],
    )
    return e, (u, dqkv, att, g, dgain)


def out_weights(uses, width, put):
    att = jnp.concatenate([use[2][...] for use in uses], axis=0)
    for n in range(0, width, 512):
        cols = pl.ds(n, 512)
        put(cols, dot(att, jnp.concatenate([whole(use[3], cols) for use in uses], axis=0), TN))


def in_weights(uses, width, put):
    dqkv = jnp.concatenate([use[1][...] for use in uses], axis=0)
    for m in range(0, width, 256):
        put(pl.ds(m, 256), dot(jnp.concatenate([use[0][:, m:m + 256] for use in uses], axis=0), dqkv, TN))


def gain_sum(uses):
    total = uses[0][4][...]
    for use in uses[1:]:
        total = total + use[4][...]
    return total


class Copies:
    def __init__(self, sems, odd):
        self.sems, self.odd, self.waits = sems, odd, []

    def push(self, source, target, other=None):
        sem = self.sems.at[len(self.waits)]
        copy = pltpu.make_async_copy(source, target, sem)
        if other is None:
            copy.start()
        else:
            by_place(self.odd, copy, pltpu.make_async_copy(source, other, sem))[0]()
        self.waits.append(copy.wait)

    def wait(self):
        for wait in self.waits:
            wait()


def early_weights(uses, out_a, out_b):
    rows, width = uses[0][0].shape
    hd = HEADS_DEV * HEAD_DIM

    def body(ins, outs, scratch):
        uses, (a_ref,), (b_ref,) = ins
        (down, up), gain_out, wo_out, wq_out = outs
        copies = Copies(scratch[0], is_odd())
        copies.push(a_ref, down.at[0], up.at[0])
        copies.push(b_ref, up.at[0], down.at[0])
        gain_out[...] = gain_sum(uses)

        def put_wo(cols, value):
            wo_out[:, cols] = value

        def put_wq(at, value):
            wq_out[at, :] = value

        out_weights(uses, width, put_wo)
        in_weights(uses, width, put_wq)
        copies.wait()

    outs, *sums = call(
        "early_weights", body, [list(uses), out_a, out_b],
        [[jax.ShapeDtypeStruct((1, rows, width), BF16)] * 2,
         Mem((8, width), F32), Mem((hd, width), F32), Mem((width, 3 * hd), F32)],
        [pltpu.SemaphoreType.DMA((2,))],
    )
    return outs, sums


def finish_kernel(g, h, gain, turned, saved, back_b, uses, sums):
    rows, width = saved[0].shape
    hd = HEADS_DEV * HEAD_DIM
    u, qkv, probs, att, stats = saved

    def body(ins, outs, scratch):
        g, h, gain_ref, (wqt_ref, wot_ref, wg_ref), (u_ref, qkv_ref, p_ref, att_ref, st_ref), (b_ref,), uses, sums = ins
        gain_total, wo_sum, wq_sum = sums
        (down, up), gain_hbm, wo_hbm, wq_hbm = outs
        e_ref, dqkv_ref, dg_ref, wo_buf, wq_buf, gain_buf, sems = scratch
        copies = Copies(sems, is_odd())
        copies.push(b_ref, up.at[0], down.at[0])
        uses = [*uses, (u_ref, dqkv_ref, att_ref, g, dg_ref)]

        def put_wo(cols, value):
            wo_buf[:, cols] = (wo_sum[:, cols] + value).astype(BF16)
            copies.push(wo_buf.at[:, cols], wo_hbm.at[0, :, cols])

        def put_wq(at, value):
            wq_buf[at, :] = (wq_sum[at, :] + value).astype(BF16)
            copies.push(wq_buf.at[at], wq_hbm.at[0, at])

        def done(cols):
            copies.push(e_ref.at[:, cols], down.at[0, :, cols], up.at[0, :, cols])

        attention_reverse(g, wot_ref, qkv_ref, p_ref, dqkv_ref)
        out_weights(uses, width, put_wo)
        in_weights(uses, width, put_wq)
        norm_reverse(g, h, gain_ref, wqt_ref, wg_ref, qkv_ref, st_ref, [e_ref], dqkv_ref, dg_ref, done)
        gain_buf[...] = jnp.sum(gain_total[...] + gain_sum(uses), axis=0, keepdims=True).astype(BF16)
        copies.push(gain_buf, gain_hbm)
        copies.wait()

    return call(
        "finish", body, [g, h, gain, turned, list(saved), back_b, list(uses), list(sums)],
        [
            [jax.ShapeDtypeStruct((1, rows, width), BF16)] * 2,
            jax.ShapeDtypeStruct((1, width), BF16),
            jax.ShapeDtypeStruct((1, hd, width), BF16),
            jax.ShapeDtypeStruct((1, width, 3 * hd), BF16),
        ],
        [
            pltpu.VMEM((rows, width), BF16),
            pltpu.VMEM(qkv.shape, BF16),
            pltpu.VMEM((8, width), F32),
            pltpu.VMEM((hd, width), BF16),
            pltpu.VMEM((width, 3 * hd), BF16),
            pltpu.VMEM((1, width), BF16),
            pltpu.SemaphoreType.DMA((2 + width // 512 * 2 + width // 256,)),
        ],
    )


def shards(acts_down, acts_up, cotangent_down, cotangent_up, ln_gain, w_qkv, w_out, band_offsets):
    sections = lax.axis_size("section")
    near = [(i, i ^ 1) for i in range(sections)]
    far = [(i, (i + (1 if i % 2 else -1)) % sections) for i in range(sections)]

    def swap_near(x):
        return [lax.ppermute(part, "section", near) for part in x]

    def swap_far(x):
        return [lax.ppermute(part, "section", far) for part in x]

    def after(x, other):
        return lax.optimization_barrier((x, other))[0]

    a0, b0, gain, wq, wo, mask, a1_out, a0_saved = first_kernel(
        band_offsets.T, ln_gain, w_qkv, w_out, acts_down, acts_up, 1)
    fixed = [gain, wq, wo]
    a1 = swap_far(a1_out)
    b1_out, b0_saved = forward_kernel(after(b0, a0_saved[4]), fixed, mask, NEAR_PARTS)
    b1 = swap_near(b1_out)
    b2_out, b1_saved = forward_kernel(after(b1, b0_saved[4]), fixed, mask, 1)
    b2 = swap_far(b2_out)
    *turned, cot_a, cot_b = prepare_kernel(gain, wq, wo, b1_saved[4], cotangent_down, cotangent_up)
    a2_out, a1_saved = forward_kernel(after(a1, turned[2]), fixed, mask, NEAR_PARTS, us=8)
    a2 = swap_near(a2_out)
    out_b, eb2, use_b2 = turn_kernel(after(b2, a1_saved[4]), cot_b, fixed, mask, turned, 1)
    cb1 = swap_far(eb2)
    out_a, ea2, use_a2 = turn_kernel(after(a2, use_b2[4]), cot_a, fixed, mask, turned, NEAR_PARTS)
    ca1 = swap_near(ea2)
    ea1, use_a1 = backward_kernel(after(ca1, use_a2[4]), a1, gain, turned, a1_saved, 1)
    ca0 = swap_far(ea1)
    eb1, use_b1 = backward_kernel(after(cb1, use_a1[4]), b1, gain, turned, b1_saved, NEAR_PARTS)
    cb0 = swap_near(eb1)
    (out_down, out_up), sums = early_weights([use_b2, use_a2, use_a1, after(use_b1, use_b1[4])], out_a, out_b)
    back_b, use_b0 = backward_kernel(after(cb0, sums[0]), b0, gain, turned, b0_saved, 1)
    (back_down, back_up), d_gain, d_wo, d_wq = finish_kernel(
        after(ca0, use_b0[4]), a0, gain, turned, a0_saved, back_b, [use_b0], sums)
    return out_down, out_up, back_down, back_up, d_gain, d_wq, d_wo


def solution(mesh):
    both = ("groups", "section")
    in_specs = (
        P(both, None, None), P(both, None, None), P(both, None, None), P(both, None, None),
        P("section", None), P("section", None, None), P("section", None, None), P(),
    )
    out_specs = (
        P(both, None, None), P(both, None, None), P(both, None, None), P(both, None, None),
        P(both, None), P(both, None, None), P(both, None, None),
    )
    return jax.shard_map(shards, mesh=mesh, in_specs=in_specs, out_specs=out_specs, check_vma=False)
```

time: 68.4 us -> 64 us (0.936)
  the two profiles are of different devices: /device:TPU:1 before, /device:TPU:29 now
where the time goes in v3:
time: 64 us; the launch traced here: 63.9 us
  starting transfers between devices  31.1 us (49%)
  Pallas kernels  28.7 us (45%)
  waiting for transfers between devices  3.17 us (5%)
  between operations  0.93 us (1%)
    pallas_call x12, Pallas kernels, call(): pl.pallas_call(kernel, in_specs=[far if isinstance(x, Far) else VM for x...  28.7 us
    ppermute x8, starting transfers between devices, swap_near(): return [lax.ppermute(part, 'section', near) for part in x]  25.3 us
    ppermute x4, starting transfers between devices, swap_far(): return [lax.ppermute(part, 'section', far) for part in x]  5.76 us
    ppermute x8, waiting for transfers between devices, swap_near(): return [lax.ppermute(part, 'section', near) for part in x]  2.93 us
  transfers between devices with their start and end apart: 12, of which 5 were waited for; matrix products, arithmetic and copies ran while one was open for 0% of the time, Pallas kernels for 33%

profile of v3, /device:TPU:29, one launch (start us, length us, event | category | flops | bytes accessed | tf_op | source)
XLA Modules:
  0.0 63.9 jit_solution(2478627631155561441)
XLA Ops:
  0.6 3.4 %first.1 = (bf16[128,2048]{1,0:T(8,128)(2,1)S(1)}, bf16[128,2048]{1,0:T(8,128)(2,1)S(1)}, bf16[1,2048]{1,0:T(2,128)(2,1)S(1)}, bf16[2048,768]{1,0:T(8,128)(2,1)S...) custom-call(s32[2,4]{1,0:T(2,128)} %bitcast.1, ...), custom_call_target="tpu_custom_call" | custom-call | flops 2000000 | bytes 200 | tf_op jit(solution)/shard_map/first/pallas_call | solution.py:174
  4.1 1.6 %forward.3 = (bf16[64,2048]{1,0:T(8,128)(2,1)S(1)}, bf16[64,2048]{1,0:T(8,128)(2,1)S(1)}, bf16[128,2048]{1,0:T(8,128)(2,1)S(1)}, bf16[128,768]{1,0:T(8,128)(2,1)...) custom-call(bf16[128,2048]{1,0:T(8,128)(2,1)S(1)} %get-tuple-element.97.refs_0_.refs_2_, ...), custom_call_target="tpu_custom_call" | custom-call | flops 2000000 | bytes 200 | tf_op jit(solution)/shard_map/forward/pallas_call | solution.py:174
  5.7 0.7 %collective-permute-start = (bf16[64,2048]{1,0:T(8,128)(2,1)S(1)}, bf16[64,2048]{1,0:T(8,128)(2,1)S(1)}, u32[]{:S(2)}, u32[]{:S(2)}) collective-permute-start(bf16[64,2048]{1,0:T(8,128)(2,1)S(1)} %get-tuple-element.102), channel_id=1, source_target_pairs={{0,1},{1,0},{2,3},{3,2},{4,5},{5,4},{6,7},{7,6},{8,9},{9,8},{10,11... | collective-permute-start | bytes 786440 | tf_op jit(solution)/shard_map/ppermute | solution.py:471
  6.5 1.1 %collective-permute-done.refs_0_.refs_1_ = bf16[64,2048]{1,0:T(8,128)(2,1)S(1)} collective-permute-done((bf16[64,2048]{1,0:T(8,128)(2,1)S(1)}, bf16[64,2048]{1,0:T(8,128)(2,1)S(1)}, u32[]{:S(2)}, u32[]{:S(2)}) %collective-permute-start) | collective-permute-done | bytes 262176 | tf_op jit(solution)/shard_map/ppermute | solution.py:471
  7.6 0.4 collective-permute-done.1.refs_1_.refs_2_
  7.9 1.6 %forward.4 = (bf16[128,2048]{1,0:T(8,128)(2,1)S(1)}, bf16[128,2048]{1,0:T(8,128)(2,1)S(1)}, bf16[128,768]{1,0:T(8,128)(2,1)S(1)}, f32[2,128,128]{2,1,0:T(8,128)S...) custom-call(bf16[64,2048]{1,0:T(8,128)(2,1)S(1)} %collective-permute-done.refs_0_.refs_1_, ...), custom_call_target="tpu_custom_call" | custom-call | flops 2000000 | bytes 200 | tf_op jit(solution)/shard_map/forward/pallas_call | solution.py:174
  9.5 4.2 %collective-permute-start.2 = (bf16[128,2048]{1,0:T(8,128)(2,1)S(1)}, bf16[128,2048]{1,0:T(8,128)(2,1)S(1)}, u32[]{:S(2)}, u32[]{:S(2)}) collective-permute-start(bf16[128,2048]{1,0:T(8,128)(2,1)S(1)} %get-tuple-element.107), channel_id=1, source_target_pairs={{0,15},{1,2},{2,1},{3,4},{4,3},{5,6},{6,5},{7,8},{8,7},{9,10},{10,... | collective-permute-start | bytes 1572872 | tf_op jit(solution)/shard_map/ppermute | solution.py:474
  13.7 1.5 %prepare.1 = (bf16[768,2048]{1,0:T(8,128)(2,1)S(1)}, bf16[2048,256]{1,0:T(8,128)(2,1)S(1)}, f32[1,768]{1,0:T(1,128)S(1)}, bf16[128,2048]{1,0:T(8,128)(2,1)S(1)}, bf16[128,2048]{1,0:T(8,128)(2,1)S(1)}) custom-call(bf16[1,2048]{1,0:T(2,128)(2,1)S(1)} %get-tuple-element.98.refs_1_.refs_2_.refs_0_.refs_3_, ...), custom_call_target="tpu_custom_call" | custom-call | flops 2000000 | bytes 200 | tf_op jit(solution)/shard_map/prepare/pallas_call | solution.py:174
  15.2 0.2 collective-permute-done.3.refs_0_.refs_2_
  15.5 1.6 %forward.5 = (bf16[64,2048]{1,0:T(8,128)(2,1)S(1)}, bf16[64,2048]{1,0:T(8,128)(2,1)S(1)}, bf16[128,2048]{1,0:T(8,128)(2,1)S(1)}, bf16[128,768]{1,0:T(8,128)(2,1)...) custom-call(bf16[128,2048]{1,0:T(8,128)(2,1)S(1)} %collective-permute-done.3.refs_0_.refs_2_,, ...), custom_call_target="tpu_custom_call" | custom-call | flops 8000000000 | bytes 800000 | tf_op jit(solution)/shard_map/forward/pallas_call | solution.py:174
  17.0 9.2 %collective-permute-start.4 = (bf16[64,2048]{1,0:T(8,128)(2,1)S(1)}, bf16[64,2048]{1,0:T(8,128)(2,1)S(1)}, u32[]{:S(2)}, u32[]{:S(2)}) collective-permute-start(bf16[64,2048]{1,0:T(8,128)(2,1)S(1)} %get-tuple-element.121), channel_id=1, source_target_pairs={{0,1},{1,0},{2,3},{3,2},{4,5},{5,4},{6,7},{7,6},{8,9},{9,8},{10,11... | collective-permute-start | bytes 786440 | tf_op jit(solution)/shard_map/ppermute | solution.py:471
  26.3 3.2 %turn.2 = (bf16[128,2048]{1,0:T(8,128)(2,1)S(1)}, bf16[128,2048]{1,0:T(8,128)(2,1)S(1)}, bf16[128,2048]{1,0:T(8,128)(2,1)S(1)}, bf16[128,768]{1,0:T(8,128)(2,1)S...) custom-call(bf16[128,2048]{1,0:T(8,128)(2,1)S(1)} %collective-permute-done.2.refs_0_, ...), custom_call_target="tpu_custom_call" | custom-call | flops 2000000 | bytes 200 | tf_op jit(solution)/shard_map/turn/pallas_call | solution.py:174
  29.6 3.4 %turn.3 = (bf16[128,2048]{1,0:T(8,128)(2,1)S(1)}, bf16[64,2048]{1,0:T(8,128)(2,1)S(1)}, bf16[64,2048]{1,0:T(8,128)(2,1)S(1)}, bf16[128,2048]{1,0:T(8,128)(2,1)S(...) custom-call(bf16[64,2048]{1,0:T(8,128)(2,1)S(1)} %collective-permute-done.4.refs_0_, ...), custom_call_target="tpu_custom_call" | custom-call | flops 2000000 | bytes 200 | tf_op jit(solution)/shard_map/turn/pallas_call | solution.py:174
  33.0 4.0 %collective-permute-start.6 = (bf16[64,2048]{1,0:T(8,128)(2,1)S(1)}, bf16[64,2048]{1,0:T(8,128)(2,1)S(1)}, u32[]{:S(2)}, u32[]{:S(2)}) collective-permute-start(bf16[64,2048]{1,0:T(8,128)(2,1)S(1)} %get-tuple-element.131), channel_id=1, source_target_pairs={{0,1},{1,0},{2,3},{3,2},{4,5},{5,4},{6,7},{7,6},{8,9},{9,8},{10,11... | collective-permute-start | bytes 786440 | tf_op jit(solution)/shard_map/ppermute | solution.py:471
  37.0 0.1 collective-permute-start.7
  37.1 1.1 %collective-permute-done.6.refs_0_.refs_13_ = bf16[64,2048]{1,0:T(8,128)(2,1)S(1)} collective-permute-done((bf16[64,2048]{1,0:T(8,128)(2,1)S(1)}, bf16[64,2048]{1,0:T(8,128)(2,1)S(1)}, u32[]{:S(2)}, u32[]{:S(2)}) %collective-permute-start.6) | collective-permute-done | bytes 262176 | tf_op jit(solution)/shard_map/ppermute | solution.py:471
  38.2 0.4 collective-permute-done.7.refs_1_.refs_14_
  38.5 1.8 %backward.3 = (bf16[128,2048]{1,0:T(8,128)(2,1)S(1)}, bf16[128,768]{1,0:T(8,128)(2,1)S(1)}, f32[8,2048]{1,0:T(8,128)S(1)}) custom-call(bf16[64,2048]{1,0:T(8,128)(2,1)S(1)} %collective-permute-done.6.refs_0_.refs_13_, bf16[64,2048]{1,0:T(8,128)(2,1)S(1)} %collective-permute-done.7.refs_1_.refs_14_, ...), custom_call_target="tpu_custom_call" | custom-call | flops 2000000 | bytes 200 | tf_op jit(solution)/shard_map/backward/pallas_call | solution.py:174
  40.3 1.4 %collective-permute-start.9 = (bf16[128,2048]{1,0:T(8,128)(2,1)S(1)}, bf16[128,2048]{1,0:T(8,128)(2,1)S(1)}, u32[]{:S(2)}, u32[]{:S(2)}) collective-permute-start(bf16[128,2048]{1,0:T(8,128)(2,1)S(1)} %get-tuple-element.157), channel_id=1, source_target_pairs={{0,15},{1,2},{2,1},{3,4},{4,3},{5,6},{6,5},{7,8},{8,7},{9,10},{10,... | collective-permute-start | bytes 1572872 | tf_op jit(solution)/shard_map/ppermute | solution.py:474
  41.7 1.7 %backward.4 = (bf16[64,2048]{1,0:T(8,128)(2,1)S(1)}, bf16[64,2048]{1,0:T(8,128)(2,1)S(1)}, bf16[128,768]{1,0:T(8,128)(2,1)S(1)}, f32[8,2048]{1,0:T(8,128)S(1)}) custom-call(bf16[128,2048]{1,0:T(8,128)(2,1)S(1)} %collective-permute-done.8.refs_0_.refs_19_, bf16[64,2048]{1,0:T(8,128)(2,1)S(1)} %collective-permute-done.refs_0_.refs_1_, ...), custom_call_target="tpu_custom_call" | custom-call | flops 2000000 | bytes 200 | tf_op jit(solution)/shard_map/backward/pallas_call | solution.py:174
  43.5 11.1 %collective-permute-start.10 = (bf16[64,2048]{1,0:T(8,128)(2,1)S(1)}, bf16[64,2048]{1,0:T(8,128)(2,1)S(1)}, u32[]{:S(2)}, u32[]{:S(2)}) collective-permute-start(bf16[64,2048]{1,0:T(8,128)(2,1)S(1)} %get-tuple-element.158), channel_id=1, source_target_pairs={{0,1},{1,0},{2,3},{3,2},{4,5},{5,4},{6,7},{7,6},{8,9},{9,8},{10,11... | collective-permute-start | bytes 786440 | tf_op jit(solution)/shard_map/ppermute | solution.py:471
  54.7 3.2 %early_weights.1 = (bf16[1,128,2048]{2,1,0:T(8,128)(2,1)}, bf16[1,128,2048]{2,1,0:T(8,128)(2,1)}, f32[8,2048]{1,0:T(8,128)S(1)}, f32[256,2048]{1,0:T(8,128)S(1)}, f32[2048,768]{1,0:T(8,128)S(1)}) custom-call(bf16[128,2048]{1,0:T(8,128)(2,1)S(1)} %get-tuple-element.117.refs_0_, bf16[128,768]{1,0:T(8,128)(2,1)S(1)} %get-tuple-element.118.refs_1_, ...), custom_call_target="tpu_custom_call" | custom-call | flops 2000000 | bytes 200 | tf_op jit(solution)/shard_map/early_weights/pallas_call | solution.py:174
  57.9 1.8 %backward.5 = (bf16[128,2048]{1,0:T(8,128)(2,1)S(1)}, bf16[128,768]{1,0:T(8,128)(2,1)S(1)}, f32[8,2048]{1,0:T(8,128)S(1)}) custom-call(bf16[64,2048]{1,0:T(8,128)(2,1)S(1)} %collective-permute-done.10.refs_0_.refs_15_, bf16[64,2048]{1,0:T(8,128)(2,1)S(1)} %collective-permute-done.11.refs_1_.refs_16_, ...), custom_call_target="tpu_custom_call" | custom-call | flops 2000000 | bytes 200 | tf_op jit(solution)/shard_map/backward/pallas_call | solution.py:174
  59.7 4.0 %finish.1 = (bf16[1,128,2048]{2,1,0:T(8,128)(2,1)}, bf16[1,128,2048]{2,1,0:T(8,128)(2,1)}, bf16[1,2048]{1,0:T(2,128)(2,1)}, bf16[1,256,2048]{2,1,0:T(8,128)(2,1)}, bf16[1,2048,768]{2,1,0:T(8,128)(2,1)}) custom-call(bf16[128,2048]{1,0:T(8,128)(2,1)S(1)} %collective-permute-done.9.refs_0_, bf16[128,2048]{1,0:T(8,128)(2,1)S(1)} %get-tuple-element.167.refs_1_, ...), custom_call_target="tpu_custom_call" | custom-call | flops 2000000 | bytes 200 | tf_op jit(solution)/shard_map/finish/pallas_call | solution.py:174
  (12 shorter events, 0.4 us)
Async XLA Ops:
  4.0 11.5 %collective-permute-start.3 = (bf16[128,2048]{1,0:T(8,128)(2,1)S(1)}, bf16[128,2048]{1,0:T(8,128)(2,1)S(1)}, u32[]{:S(2)}, u32[]{:S(2)}) collective-permute-start(bf16[128,2048]{1,0:T(8,128)(2,1)S(1)} %get-tuple-element.108), channel_id=1, source_target_pairs={{0,15},{1,2},{2,1},{3,4},{4,3},{5,6},{6,5},{7,8},{8,7},{9,10},{10,... | collective-permute-start | bytes 1572872 | tf_op jit(solution)/shard_map/ppermute | solution.py:474
  5.7 1.9 %collective-permute-start = (bf16[64,2048]{1,0:T(8,128)(2,1)S(1)}, bf16[64,2048]{1,0:T(8,128)(2,1)S(1)}, u32[]{:S(2)}, u32[]{:S(2)}) collective-permute-start(bf16[64,2048]{1,0:T(8,128)(2,1)S(1)} %get-tuple-element.102), channel_id=1, source_target_pairs={{0,1},{1,0},{2,3},{3,2},{4,5},{5,4},{6,7},{7,6},{8,9},{9,8},{10,11... | collective-permute-start | bytes 786440 | tf_op jit(solution)/shard_map/ppermute | solution.py:471
  6.4 1.5 %collective-permute-start.1 = (bf16[64,2048]{1,0:T(8,128)(2,1)S(1)}, bf16[64,2048]{1,0:T(8,128)(2,1)S(1)}, u32[]{:S(2)}, u32[]{:S(2)}) collective-permute-start(bf16[64,2048]{1,0:T(8,128)(2,1)S(1)} %get-tuple-element.103), channel_id=1, source_target_pairs={{0,1},{1,0},{2,3},{3,2},{4,5},{5,4},{6,7},{7,6},{8,9},{9,8},{10,11... | collective-permute-start | bytes 786440 | tf_op jit(solution)/shard_map/ppermute | solution.py:471
  9.5 16.8 %collective-permute-start.2 = (bf16[128,2048]{1,0:T(8,128)(2,1)S(1)}, bf16[128,2048]{1,0:T(8,128)(2,1)S(1)}, u32[]{:S(2)}, u32[]{:S(2)}) collective-permute-start(bf16[128,2048]{1,0:T(8,128)(2,1)S(1)} %get-tuple-element.107), channel_id=1, source_target_pairs={{0,15},{1,2},{2,1},{3,4},{4,3},{5,6},{6,5},{7,8},{8,7},{9,10},{10,... | collective-permute-start | bytes 1572872 | tf_op jit(solution)/shard_map/ppermute | solution.py:474
  17.0 12.6 %collective-permute-start.4 = (bf16[64,2048]{1,0:T(8,128)(2,1)S(1)}, bf16[64,2048]{1,0:T(8,128)(2,1)S(1)}, u32[]{:S(2)}, u32[]{:S(2)}) collective-permute-start(bf16[64,2048]{1,0:T(8,128)(2,1)S(1)} %get-tuple-element.121), channel_id=1, source_target_pairs={{0,1},{1,0},{2,3},{3,2},{4,5},{5,4},{6,7},{7,6},{8,9},{9,8},{10,11... | collective-permute-start | bytes 786440 | tf_op jit(solution)/shard_map/ppermute | solution.py:471
  26.2 3.4 %collective-permute-start.5 = (bf16[64,2048]{1,0:T(8,128)(2,1)S(1)}, bf16[64,2048]{1,0:T(8,128)(2,1)S(1)}, u32[]{:S(2)}, u32[]{:S(2)}) collective-permute-start(bf16[64,2048]{1,0:T(8,128)(2,1)S(1)} %get-tuple-element.122), channel_id=1, source_target_pairs={{0,1},{1,0},{2,3},{3,2},{4,5},{5,4},{6,7},{7,6},{8,9},{9,8},{10,11... | collective-permute-start | bytes 786440 | tf_op jit(solution)/shard_map/ppermute | solution.py:471
  29.5 12.2 %collective-permute-start.8 = (bf16[128,2048]{1,0:T(8,128)(2,1)S(1)}, bf16[128,2048]{1,0:T(8,128)(2,1)S(1)}, u32[]{:S(2)}, u32[]{:S(2)}) collective-permute-start(bf16[128,2048]{1,0:T(8,128)(2,1)S(1)} %get-tuple-element.141), channel_id=1, source_target_pairs={{0,15},{1,2},{2,1},{3,4},{4,3},{5,6},{6,5},{7,8},{8,7},{9,10},{10,... | collective-permute-start | bytes 1572872 | tf_op jit(solution)/shard_map/ppermute | solution.py:474
  33.0 5.1 %collective-permute-start.6 = (bf16[64,2048]{1,0:T(8,128)(2,1)S(1)}, bf16[64,2048]{1,0:T(8,128)(2,1)S(1)}, u32[]{:S(2)}, u32[]{:S(2)}) collective-permute-start(bf16[64,2048]{1,0:T(8,128)(2,1)S(1)} %get-tuple-element.131), channel_id=1, source_target_pairs={{0,1},{1,0},{2,3},{3,2},{4,5},{5,4},{6,7},{7,6},{8,9},{9,8},{10,11... | collective-permute-start | bytes 786440 | tf_op jit(solution)/shard_map/ppermute | solution.py:471
  37.0 1.5 %collective-permute-start.7 = (bf16[64,2048]{1,0:T(8,128)(2,1)S(1)}, bf16[64,2048]{1,0:T(8,128)(2,1)S(1)}, u32[]{:S(2)}, u32[]{:S(2)}) collective-permute-start(bf16[64,2048]{1,0:T(8,128)(2,1)S(1)} %get-tuple-element.132), channel_id=1, source_target_pairs={{0,1},{1,0},{2,3},{3,2},{4,5},{5,4},{6,7},{7,6},{8,9},{9,8},{10,11... | collective-permute-start | bytes 786440 | tf_op jit(solution)/shard_map/ppermute | solution.py:471
  40.3 19.4 %collective-permute-start.9 = (bf16[128,2048]{1,0:T(8,128)(2,1)S(1)}, bf16[128,2048]{1,0:T(8,128)(2,1)S(1)}, u32[]{:S(2)}, u32[]{:S(2)}) collective-permute-start(bf16[128,2048]{1,0:T(8,128)(2,1)S(1)} %get-tuple-element.157), channel_id=1, source_target_pairs={{0,15},{1,2},{2,1},{3,4},{4,3},{5,6},{6,5},{7,8},{8,7},{9,10},{10,... | collective-permute-start | bytes 1572872 | tf_op jit(solution)/shard_map/ppermute | solution.py:474
  43.5 14.4 %collective-permute-start.10 = (bf16[64,2048]{1,0:T(8,128)(2,1)S(1)}, bf16[64,2048]{1,0:T(8,128)(2,1)S(1)}, u32[]{:S(2)}, u32[]{:S(2)}) collective-permute-start(bf16[64,2048]{1,0:T(8,128)(2,1)S(1)} %get-tuple-element.158), channel_id=1, source_target_pairs={{0,1},{1,0},{2,3},{3,2},{4,5},{5,4},{6,7},{7,6},{8,9},{9,8},{10,11... | collective-permute-start | bytes 786440 | tf_op jit(solution)/shard_map/ppermute | solution.py:471
  54.6 3.3 %collective-permute-start.11 = (bf16[64,2048]{1,0:T(8,128)(2,1)S(1)}, bf16[64,2048]{1,0:T(8,128)(2,1)S(1)}, u32[]{:S(2)}, u32[]{:S(2)}) collective-permute-start(bf16[64,2048]{1,0:T(8,128)(2,1)S(1)} %get-tuple-element.159), channel_id=1, source_target_pairs={{0,1},{1,0},{2,3},{3,2},{4,5},{5,4},{6,7},{7,6},{8,9},{9,8},{10,11... | collective-permute-start | bytes 786440 | tf_op jit(solution)/shard_map/ppermute | solution.py:471

commit v4 on v3

--- a/solution.py
+++ b/solution.py
@@ -18,6 +18,7 @@
 SCALE = 1.0 / math.sqrt(HEAD_DIM)
 VM = pl.BlockSpec(memory_space=pltpu.VMEM)
 NEAR_PARTS = 2
+FAR_SHARES = (3, 5)
 
 
 def dot(a, b, dims=(((1,), (0,)), ((), ()))):
@@ -37,14 +38,32 @@
     return jnp.where(keep, 1.0, 0.0).astype(F32)
 
 
+def held(refs, at):
+    for ref in refs:
+        if at < ref.shape[0]:
+            return ref, at
+        at -= ref.shape[0]
+
+
 def read(refs, at, size, cols=slice(None)):
-    held = refs[0].shape[0]
-    return refs[at // held][pl.ds(at % held, size), cols]
+    ref, at = held(refs, at)
+    return ref[pl.ds(at, size), cols]
 
 
 def write(refs, at, size, value, cols=slice(None)):
-    held = refs[0].shape[0]
-    refs[at // held][pl.ds(at % held, size), cols] = value
+    ref, at = held(refs, at)
+    ref[pl.ds(at, size), cols] = value
+
+
+def pieces(*arrays):
+    cuts = {0}
+    for refs in arrays:
+        at = 0
+        for ref in refs:
+            at += ref.shape[0]
+            cuts.add(at)
+    cuts = sorted(cuts)
+    return list(zip(cuts[:-1], cuts[1:]))
 
 
 def whole(refs, cols=slice(None)):
@@ -72,22 +91,21 @@
     heads = [pl.ds(head * HEAD_DIM, HEAD_DIM) for head in range(HEADS_DEV)]
     scores = [dot(qkv_ref[:, cols], qkv_ref[:, pl.ds(hd + cols.start, HEAD_DIM)], NT) for cols in heads]
     weighted = [jnp.where(keep > 0.0, jnp.exp(score * SCALE), 0.0) for score in scores]
+    mixed = [
+        dot(value.astype(BF16), qkv_ref[:, pl.ds(2 * hd + cols.start, HEAD_DIM)]) for value, cols in zip(weighted, heads)
+    ]
     inverse = [1.0 / jnp.sum(value, axis=-1, keepdims=True) for value in weighted]
-    probs = [value * scale for value, scale in zip(weighted, inverse)]
-    mixed = [
-        dot(value.astype(BF16), qkv_ref[:, pl.ds(2 * hd + cols.start, HEAD_DIM)]) for value, cols in zip(probs, heads)
-    ]
     for head, cols in enumerate(heads):
-        p_ref[head] = probs[head]
-        att_ref[:, cols] = mixed[head].astype(BF16)
+        att_ref[:, cols] = (mixed[head] * inverse[head]).astype(BF16)
+        p_ref[head] = weighted[head] * inverse[head]
     if waits:
         waits[3].wait()
     for n in range(0, width, 512):
         cols = pl.ds(n, 512)
         value = dot(att_ref[...], wo_ref[:, cols])
-        size = min(out[0].shape[0], h[0].shape[0])
-        for at in range(0, rows, size):
-            write(out, at, size, (read(h, at, size, cols).astype(F32) + value[at:at + size]).astype(BF16), cols)
+        for at, end in pieces(out, h):
+            size = end - at
+            write(out, at, size, (read(h, at, size, cols).astype(F32) + value[at:end]).astype(BF16), cols)
 
 
 def attention_reverse(g, wot_ref, qkv_ref, p_ref, dqkv_ref):
@@ -130,9 +148,8 @@
             dg_ref[:, cols] = jnp.sum((du * xhat).reshape(rows // 8, 8, 128), axis=0)
             gain = gain_ref[:, cols].astype(F32)
             value = (du * gain) * rstd - first - xhat * second + whole(g, cols).astype(F32)
-            size = e[0].shape[0]
-            for part in range(len(e)):
-                e[part][:, cols] = value[part * size:(part + 1) * size].astype(BF16)
+            for at, end in pieces(e):
+                write(e, at, end - at, value[at:end].astype(BF16), cols)
         if done:
             done(pl.ds(block, 512))
 
@@ -195,8 +212,9 @@
         self.shape, self.dtype = shape, dtype
 
 
-def stream(rows, width, parts):
-    return [Mem((rows // parts, width), BF16) for _ in range(parts)]
+def stream(rows, width, parts=1):
+    shares = parts if isinstance(parts, tuple) else (1,) * parts
+    return [Mem((rows * share // sum(shares), width), BF16) for share in shares]
 
 
 def saved_outs(rows, width):
@@ -255,7 +273,7 @@
 
 
 def forward_kernel(h, fixed, mask, parts, us=0.002):
-    rows, width = h[0].shape[0] * len(h), h[0].shape[1]
+    rows, width = sum(x.shape[0] for x in h), h[0].shape[1]
 
     def body(ins, outs, scratch):
         h, fixed, mask_ref = ins
@@ -298,7 +316,7 @@
 
 
 def turn_kernel(h, g, fixed, mask, turned, parts):
-    rows, width = h[0].shape[0] * len(h), h[0].shape[1]
+    rows, width = sum(x.shape[0] for x in h), h[0].shape[1]
     hd = HEADS_DEV * HEAD_DIM
 
     def body(ins, outs, scratch):
@@ -378,7 +396,7 @@
             wait()
 
 
-def early_weights(uses, out_a, out_b):
+def early_weights(uses, out_a, out_b, us):
     rows, width = uses[0][0].shape
     hd = HEADS_DEV * HEAD_DIM
 
@@ -404,9 +422,29 @@
         "early_weights", body, [list(uses), out_a, out_b],
         [[jax.ShapeDtypeStruct((1, rows, width), BF16)] * 2,
          Mem((8, width), F32), Mem((hd, width), F32), Mem((width, 3 * hd), F32)],
-        [pltpu.SemaphoreType.DMA((2,))],
+        [pltpu.SemaphoreType.DMA((2,))], us=us,
     )
     return outs, sums
+
+
+def more_weights(uses, sums):
+    width = uses[0][0].shape[1]
+
+    def body(ins, outs, scratch):
+        uses, (gain_in, wo_in, wq_in) = ins
+        gain_out, wo_out, wq_out = outs
+        gain_out[...] = gain_in[...] + gain_sum(uses)
+
+        def put_wo(cols, value):
+            wo_out[:, cols] = wo_in[:, cols] + value
+
+        def put_wq(at, value):
+            wq_out[at, :] = wq_in[at, :] + value
+
+        out_weights(uses, width, put_wo)
+        in_weights(uses, width, put_wq)
+
+    return call("more_weights", body, [list(uses), list(sums)], [Mem(x.shape, F32) for x in sums])
 
 
 def finish_kernel(g, h, gain, turned, saved, back_b, uses, sums):
@@ -483,20 +521,25 @@
     b1_out, b0_saved = forward_kernel(after(b0, a0_saved[4]), fixed, mask, NEAR_PARTS)
     b1 = swap_near(b1_out)
     b2_out, b1_saved = forward_kernel(after(b1, b0_saved[4]), fixed, mask, 1)
-    b2 = swap_far(b2_out)
     *turned, cot_a, cot_b = prepare_kernel(gain, wq, wo, b1_saved[4], cotangent_down, cotangent_up)
-    a2_out, a1_saved = forward_kernel(after(a1, turned[2]), fixed, mask, NEAR_PARTS, us=8)
+    b2 = swap_far(after(b2_out, turned[2]))
+    a2_out, a1_saved = forward_kernel(after(a1, turned[2]), fixed, mask, NEAR_PARTS)
     a2 = swap_near(a2_out)
-    out_b, eb2, use_b2 = turn_kernel(after(b2, a1_saved[4]), cot_b, fixed, mask, turned, 1)
+    out_a, ea2, use_a2 = turn_kernel(after(a2, a1_saved[4]), cot_a, fixed, mask, turned, NEAR_PARTS)
+    ca1 = swap_near(ea2)
+    (ea1_fore, ea1_rest), use_a1 = backward_kernel(after(ca1, use_a2[4]), a1, gain, turned, a1_saved, FAR_SHARES)
+    (ca0_fore,) = swap_far([ea1_fore])
+    out_b, eb2, use_b2 = turn_kernel(after(b2, use_a1[4]), cot_b, fixed, mask, turned, 2)
     cb1 = swap_far(eb2)
-    out_a, ea2, use_a2 = turn_kernel(after(a2, use_b2[4]), cot_a, fixed, mask, turned, NEAR_PARTS)
-    ca1 = swap_near(ea2)
-    ea1, use_a1 = backward_kernel(after(ca1, use_a2[4]), a1, gain, turned, a1_saved, 1)
-    ca0 = swap_far(ea1)
-    eb1, use_b1 = backward_kernel(after(cb1, use_a1[4]), b1, gain, turned, b1_saved, NEAR_PARTS)
+    use_b2, ca0_fore = lax.optimization_barrier((use_b2, ca0_fore))
+    (out_down, out_up), sums = early_weights([use_b2, use_a2, use_a1], out_a, out_b, us=8)
+    cb1_fore, ea1_rest, sums = lax.optimization_barrier((cb1[0], ea1_rest, sums))
+    (ca0_rest,) = swap_far([ea1_rest])
+    eb1, use_b1 = backward_kernel([cb1_fore, cb1[1]], b1, gain, turned, b1_saved, NEAR_PARTS)
     cb0 = swap_near(eb1)
-    (out_down, out_up), sums = early_weights([use_b2, use_a2, use_a1, after(use_b1, use_b1[4])], out_a, out_b)
+    sums = more_weights([after(use_b1, use_b1[4])], sums)
     back_b, use_b0 = backward_kernel(after(cb0, sums[0]), b0, gain, turned, b0_saved, 1)
+    ca0 = [ca0_fore, ca0_rest]
     (back_down, back_up), d_gain, d_wo, d_wq = finish_kernel(
         after(ca0, use_b0[4]), a0, gain, turned, a0_saved, back_b, [use_b0], sums)
     return out_down, out_up, back_down, back_up, d_gain, d_wq, d_wo

time: 64 us -> 67.5 us (1.055)
  the two profiles are of different devices: /device:TPU:29 before, /device:TPU:1 now
where the time goes in v4:
time: 67.5 us; the launch traced here: 67.3 us
  Pallas kernels  29.5 us (44%)
  waiting for transfers between devices  20.3 us (30%)
  starting transfers between devices  16.5 us (24%)
  between operations  0.92 us (1%)
    pallas_call x13, Pallas kernels, call(): pl.pallas_call(kernel, in_specs=[far if isinstance(x, Far) else VM for x...  29.5 us
    ppermute x6, waiting for transfers between devices, swap_far(): return [lax.ppermute(part, 'section', far) for part in x]  17.3 us
    ppermute x6, starting transfers between devices, swap_far(): return [lax.ppermute(part, 'section', far) for part in x]  9.12 us
    ppermute x8, starting transfers between devices, swap_near(): return [lax.ppermute(part, 'section', near) for part in x]  7.43 us
    ppermute x8, waiting for transfers between devices, swap_near(): return [lax.ppermute(part, 'section', near) for part in x]  2.99 us
  transfers between devices with their start and end apart: 14, of which 10 were waited for; matrix products, arithmetic and copies ran while one was open for 0% of the time, Pallas kernels for 31%

profile of v4, /device:TPU:1, one launch (start us, length us, event | category | flops | bytes accessed | tf_op | source)
XLA Modules:
  0.0 67.3 jit_solution(6165634494387322227)
XLA Ops:
  0.6 3.3 %first.1 = (bf16[128,2048]{1,0:T(8,128)(2,1)S(1)}, bf16[128,2048]{1,0:T(8,128)(2,1)S(1)}, bf16[1,2048]{1,0:T(2,128)(2,1)S(1)}, bf16[2048,768]{1,0:T(8,128)(2,1)S...) custom-call(s32[2,4]{1,0:T(2,128)} %bitcast.1, ...), custom_call_target="tpu_custom_call" | custom-call | flops 2000000 | bytes 200 | tf_op jit(solution)/shard_map/first/pallas_call | solution.py:191
  4.0 2.7 %collective-permute-start.3 = (bf16[128,2048]{1,0:T(8,128)(2,1)S(1)}, bf16[128,2048]{1,0:T(8,128)(2,1)S(1)}, u32[]{:S(2)}, u32[]{:S(2)}) collective-permute-start(bf16[128,2048]{1,0:T(8,128)(2,1)S(1)} %get-tuple-element.129), channel_id=1, source_target_pairs={{0,15},{1,2},{2,1},{3,4},{4,3},{5,6},{6,5},{7,8},{8,7},{9,10},{10,... | collective-permute-start | bytes 1572872 | tf_op jit(solution)/shard_map/ppermute | solution.py:512
  6.7 1.6 %forward.3 = (bf16[64,2048]{1,0:T(8,128)(2,1)S(1)}, bf16[64,2048]{1,0:T(8,128)(2,1)S(1)}, bf16[128,2048]{1,0:T(8,128)(2,1)S(1)}, bf16[128,768]{1,0:T(8,128)(2,1)...) custom-call(bf16[128,2048]{1,0:T(8,128)(2,1)S(1)} %get-tuple-element.115.refs_0_.refs_2_, ...), custom_call_target="tpu_custom_call" | custom-call | flops 2000000 | bytes 200 | tf_op jit(solution)/shard_map/forward/pallas_call | solution.py:191
  8.2 2.9 %collective-permute-start = (bf16[64,2048]{1,0:T(8,128)(2,1)S(1)}, bf16[64,2048]{1,0:T(8,128)(2,1)S(1)}, u32[]{:S(2)}, u32[]{:S(2)}) collective-permute-start(bf16[64,2048]{1,0:T(8,128)(2,1)S(1)} %get-tuple-element.120), channel_id=1, source_target_pairs={{0,1},{1,0},{2,3},{3,2},{4,5},{5,4},{6,7},{7,6},{8,9},{9,8},{10,11... | collective-permute-start | bytes 786440 | tf_op jit(solution)/shard_map/ppermute | solution.py:509
  12.7 1.6 %forward.4 = (bf16[128,2048]{1,0:T(8,128)(2,1)S(1)}, bf16[128,2048]{1,0:T(8,128)(2,1)S(1)}, bf16[128,768]{1,0:T(8,128)(2,1)S(1)}, f32[2,128,128]{2,1,0:T(8,128)S...) custom-call(bf16[64,2048]{1,0:T(8,128)(2,1)S(1)} %collective-permute-done.refs_0_.refs_2_, ...), custom_call_target="tpu_custom_call" | custom-call | flops 2000000 | bytes 200 | tf_op jit(solution)/shard_map/forward/pallas_call | solution.py:191
  14.3 1.5 %prepare.1 = (bf16[768,2048]{1,0:T(8,128)(2,1)S(1)}, bf16[2048,256]{1,0:T(8,128)(2,1)S(1)}, f32[1,768]{1,0:T(1,128)S(1)}, bf16[128,2048]{1,0:T(8,128)(2,1)S(1)}, bf16[128,2048]{1,0:T(8,128)(2,1)S(1)}) custom-call(bf16[1,2048]{1,0:T(2,128)(2,1)S(1)} %get-tuple-element.116.refs_1_.refs_2_.refs_0_.refs_3_.refs_4_, ...), custom_call_target="tpu_custom_call" | custom-call | flops 2000000 | bytes 200 | tf_op jit(solution)/shard_map/prepare/pallas_call | solution.py:191
  15.8 3.3 %collective-permute-done.3.refs_0_.refs_2_ = bf16[128,2048]{1,0:T(8,128)(2,1)S(1)} collective-permute-done((bf16[128,2048]{1,0:T(8,128)(2,1)S(1)}, bf16[128,2048]{1,0:T(8,128)(2,1)S(1)}, u32[]{:S(2)}, u32[]{:S(2)}) %collective-permute-start.3) | collective-permute-done | bytes 524320 | tf_op jit(solution)/shard_map/ppermute | solution.py:512
  19.1 1.6 %forward.5 = (bf16[64,2048]{1,0:T(8,128)(2,1)S(1)}, bf16[64,2048]{1,0:T(8,128)(2,1)S(1)}, bf16[128,2048]{1,0:T(8,128)(2,1)S(1)}, bf16[128,768]{1,0:T(8,128)(2,1)...) custom-call(bf16[128,2048]{1,0:T(8,128)(2,1)S(1)} %collective-permute-done.3.refs_0_.refs_2_,, ...), custom_call_target="tpu_custom_call" | custom-call | flops 2000000 | bytes 200 | tf_op jit(solution)/shard_map/forward/pallas_call | solution.py:191
  21.3 1.7 %collective-permute-start.2 = (bf16[128,2048]{1,0:T(8,128)(2,1)S(1)}, bf16[128,2048]{1,0:T(8,128)(2,1)S(1)}, u32[]{:S(2)}, u32[]{:S(2)}) collective-permute-start(bf16[128,2048]{1,0:T(8,128)(2,1)S(1)} %get-tuple-element.128), channel_id=1, source_target_pairs={{0,15},{1,2},{2,1},{3,4},{4,3},{5,6},{6,5},{7,8},{8,7},{9,10},{10,... | collective-permute-start | bytes 1572872 | tf_op jit(solution)/shard_map/ppermute | solution.py:512
  23.1 3.2 %turn.2 = (bf16[128,2048]{1,0:T(8,128)(2,1)S(1)}, bf16[64,2048]{1,0:T(8,128)(2,1)S(1)}, bf16[64,2048]{1,0:T(8,128)(2,1)S(1)}, bf16[128,2048]{1,0:T(8,128)(2,1)S(...) custom-call(bf16[64,2048]{1,0:T(8,128)(2,1)S(1)} %collective-permute-done.4.refs_0_, ...), custom_call_target="tpu_custom_call" | custom-call | flops 2000000 | bytes 200 | tf_op jit(solution)/shard_map/turn/pallas_call | solution.py:191
  26.2 3.2 %collective-permute-start.6 = (bf16[64,2048]{1,0:T(8,128)(2,1)S(1)}, bf16[64,2048]{1,0:T(8,128)(2,1)S(1)}, u32[]{:S(2)}, u32[]{:S(2)}) collective-permute-start(bf16[64,2048]{1,0:T(8,128)(2,1)S(1)} %get-tuple-element.139), channel_id=1, source_target_pairs={{0,1},{1,0},{2,3},{3,2},{4,5},{5,4},{6,7},{7,6},{8,9},{9,8},{10,11... | collective-permute-start | bytes 786440 | tf_op jit(solution)/shard_map/ppermute | solution.py:509
  31.0 1.8 %backward.3 = (bf16[48,2048]{1,0:T(8,128)(2,1)S(1)}, bf16[80,2048]{1,0:T(8,128)(2,1)S(1)}, bf16[128,768]{1,0:T(8,128)(2,1)S(1)}, f32[8,2048]{1,0:T(8,128)S(1)}) custom-call(bf16[64,2048]{1,0:T(8,128)(2,1)S(1)} %collective-permute-done.6.refs_0_.refs_13_, bf16[64,2048]{1,0:T(8,128)(2,1)S(1)} %collective-permute-done.7.refs_1_.refs_14_, ...), custom_call_target="tpu_custom_call" | custom-call | flops 2000000 | bytes 200 | tf_op jit(solution)/shard_map/backward/pallas_call | solution.py:191
  32.8 4.1 %collective-permute-done.2.refs_0_ = bf16[128,2048]{1,0:T(8,128)(2,1)S(1)} collective-permute-done((bf16[128,2048]{1,0:T(8,128)(2,1)S(1)}, bf16[128,2048]{1,0:T(8,128)(2,1)S(1)}, u32[]{:S(2)}, u32[]{:S(2)}) %collective-permute-start.2) | collective-permute-done | bytes 524320 | tf_op jit(solution)/shard_map/ppermute | solution.py:512
  36.9 3.3 %turn.3 = (bf16[128,2048]{1,0:T(8,128)(2,1)S(1)}, bf16[64,2048]{1,0:T(8,128)(2,1)S(1)}, bf16[64,2048]{1,0:T(8,128)(2,1)S(1)}, bf16[128,2048]{1,0:T(8,128)(2,1)S(...) custom-call(bf16[128,2048]{1,0:T(8,128)(2,1)S(1)} %collective-permute-done.2.refs_0_, ...), custom_call_target="tpu_custom_call" | custom-call | flops 2000000 | bytes 200 | tf_op jit(solution)/shard_map/turn/pallas_call | solution.py:191
  40.2 2.5 %collective-permute-start.9 = (bf16[64,2048]{1,0:T(8,128)(2,1)S(1)}, bf16[64,2048]{1,0:T(8,128)(2,1)S(1)}, u32[]{:S(2)}, u32[]{:S(2)}) collective-permute-start(bf16[64,2048]{1,0:T(8,128)(2,1)S(1)} %get-tuple-element.170), channel_id=1, source_target_pairs={{0,15},{1,2},{2,1},{3,4},{4,3},{5,6},{6,5},{7,8},{8,7},{9,10},{10,... | collective-permute-start | bytes 786440 | tf_op jit(solution)/shard_map/ppermute | solution.py:512
  42.9 1.8 %collective-permute-done.8.refs_0_ = bf16[48,2048]{1,0:T(8,128)(2,1)S(1)} collective-permute-done((bf16[48,2048]{1,0:T(8,128)(2,1)S(1)}, bf16[48,2048]{1,0:T(8,128)(2,1)S(1)}, u32[]{:S(2)}, u32[]{:S(2)}) %collective-permute-start.8) | collective-permute-done | bytes 196640 | tf_op jit(solution)/shard_map/ppermute | solution.py:512
  44.6 3.0 %early_weights.1 = (bf16[1,128,2048]{2,1,0:T(8,128)(2,1)}, bf16[1,128,2048]{2,1,0:T(8,128)(2,1)}, f32[8,2048]{1,0:T(8,128)S(1)}, f32[256,2048]{1,0:T(8,128)S(1)}, f32[2048,768]{1,0:T(8,128)S(1)}) custom-call(bf16[128,2048]{1,0:T(8,128)(2,1)S(1)} %get-tuple-element.154.refs_0_, bf16[128,768]{1,0:T(8,128)(2,1)S(1)} %get-tuple-element.155.refs_1_, ...), custom_call_target="tpu_custom_call" | custom-call | flops 8000000000 | bytes 800000 | tf_op jit(solution)/shard_map/early_weights/pallas_call | solution.py:191
  47.6 3.8 %collective-permute-done.9.refs_0_.refs_3_ = bf16[64,2048]{1,0:T(8,128)(2,1)S(1)} collective-permute-done((bf16[64,2048]{1,0:T(8,128)(2,1)S(1)}, bf16[64,2048]{1,0:T(8,128)(2,1)S(1)}, u32[]{:S(2)}, u32[]{:S(2)}) %collective-permute-start.9) | collective-permute-done | bytes 262176 | tf_op jit(solution)/shard_map/ppermute | solution.py:512
  51.4 2.0 %collective-permute-start.10 = (bf16[80,2048]{1,0:T(8,128)(2,1)S(1)}, bf16[80,2048]{1,0:T(8,128)(2,1)S(1)}, u32[]{:S(2)}, u32[]{:S(2)}) collective-permute-start(bf16[80,2048]{1,0:T(8,128)(2,1)S(1)} %get-tuple-element.175), channel_id=1, source_target_pairs={{0,15},{1,2},{2,1},{3,4},{4,3},{5,6},{6,5},{7,8},{8,7},{9,10},{10,... | collective-permute-start | bytes 983048 | tf_op jit(solution)/shard_map/ppermute | solution.py:512
  53.4 4.3 %collective-permute-done.11.refs_1_.refs_4_ = bf16[64,2048]{1,0:T(8,128)(2,1)S(1)} collective-permute-done((bf16[64,2048]{1,0:T(8,128)(2,1)S(1)}, bf16[64,2048]{1,0:T(8,128)(2,1)S(1)}, u32[]{:S(2)}, u32[]{:S(2)}) %collective-permute-start.11) | collective-permute-done | bytes 262176 | tf_op jit(solution)/shard_map/ppermute | solution.py:512
  57.8 1.8 %backward.4 = (bf16[64,2048]{1,0:T(8,128)(2,1)S(1)}, bf16[64,2048]{1,0:T(8,128)(2,1)S(1)}, bf16[128,768]{1,0:T(8,128)(2,1)S(1)}, f32[8,2048]{1,0:T(8,128)S(1)}) custom-call(bf16[64,2048]{1,0:T(8,128)(2,1)S(1)} %collective-permute-done.9.refs_0_.refs_3_, bf16[64,2048]{1,0:T(8,128)(2,1)S(1)} %collective-permute-done.11.refs_1_.refs_4_, ...), custom_call_target="tpu_custom_call" | custom-call | flops 2000000 | bytes 200 | tf_op jit(solution)/shard_map/backward/pallas_call | solution.py:191
  60.1 1.3 %more_weights.1 = (f32[8,2048]{1,0:T(8,128)S(1)}, f32[256,2048]{1,0:T(8,128)S(1)}, f32[2048,768]{1,0:T(8,128)S(1)}) custom-call(bf16[128,2048]{1,0:T(8,128)(2,1)S(1)} %get-tuple-element.186.refs_0_, bf16[128,768]{1,0:T(8,128)(2,1)S(1)} %get-tuple-element.187.refs_1_, bf16[128,256]{1,0:T(8,128)(2,1)S(1)} %get-tuple-element.188.refs_2_, ...), custom_call_target="tpu_custom_call" | custom-call | flops 2000000 | bytes 200 | tf_op jit(solution)/shard_map/more_weights/pallas_call | solution.py:191
  61.5 1.8 %backward.5 = (bf16[128,2048]{1,0:T(8,128)(2,1)S(1)}, bf16[128,768]{1,0:T(8,128)(2,1)S(1)}, f32[8,2048]{1,0:T(8,128)S(1)}) custom-call(bf16[64,2048]{1,0:T(8,128)(2,1)S(1)} %collective-permute-done.12.refs_0_.refs_16_, bf16[64,2048]{1,0:T(8,128)(2,1)S(1)} %collective-permute-done.13.refs_1_.refs_17_, ...), custom_call_target="tpu_custom_call" | custom-call | flops 2000000 | bytes 200 | tf_op jit(solution)/shard_map/backward/pallas_call | solution.py:191
  63.3 3.9 %finish.1 = (bf16[1,128,2048]{2,1,0:T(8,128)(2,1)}, bf16[1,128,2048]{2,1,0:T(8,128)(2,1)}, bf16[1,2048]{1,0:T(2,128)(2,1)}, bf16[1,256,2048]{2,1,0:T(8,128)(2,1)}, bf16[1,2048,768]{2,1,0:T(8,128)(2,1)}) custom-call(bf16[48,2048]{1,0:T(8,128)(2,1)S(1)} %collective-permute-done.8.refs_0_, bf16[80,2048]{1,0:T(8,128)(2,1)S(1)} %collective-permute-done.10.refs_1_, ...), custom_call_target="tpu_custom_call" | custom-call | flops 2000000 | bytes 200 | tf_op jit(solution)/shard_map/finish/pallas_call | solution.py:191
  (17 shorter events, 4.4 us)
Async XLA Ops:
  4.0 15.2 %collective-permute-start.3 = (bf16[128,2048]{1,0:T(8,128)(2,1)S(1)}, bf16[128,2048]{1,0:T(8,128)(2,1)S(1)}, u32[]{:S(2)}, u32[]{:S(2)}) collective-permute-start(bf16[128,2048]{1,0:T(8,128)(2,1)S(1)} %get-tuple-element.129), channel_id=1, source_target_pairs={{0,15},{1,2},{2,1},{3,4},{4,3},{5,6},{6,5},{7,8},{8,7},{9,10},{10,... | collective-permute-start | bytes 1572872 | tf_op jit(solution)/shard_map/ppermute | solution.py:512
  8.2 4.1 %collective-permute-start = (bf16[64,2048]{1,0:T(8,128)(2,1)S(1)}, bf16[64,2048]{1,0:T(8,128)(2,1)S(1)}, u32[]{:S(2)}, u32[]{:S(2)}) collective-permute-start(bf16[64,2048]{1,0:T(8,128)(2,1)S(1)} %get-tuple-element.120), channel_id=1, source_target_pairs={{0,1},{1,0},{2,3},{3,2},{4,5},{5,4},{6,7},{7,6},{8,9},{9,8},{10,11... | collective-permute-start | bytes 786440 | tf_op jit(solution)/shard_map/ppermute | solution.py:509
  11.2 1.5 %collective-permute-start.1 = (bf16[64,2048]{1,0:T(8,128)(2,1)S(1)}, bf16[64,2048]{1,0:T(8,128)(2,1)S(1)}, u32[]{:S(2)}, u32[]{:S(2)}) collective-permute-start(bf16[64,2048]{1,0:T(8,128)(2,1)S(1)} %get-tuple-element.121), channel_id=1, source_target_pairs={{0,1},{1,0},{2,3},{3,2},{4,5},{5,4},{6,7},{7,6},{8,9},{9,8},{10,11... | collective-permute-start | bytes 786440 | tf_op jit(solution)/shard_map/ppermute | solution.py:509
  20.7 2.3 %collective-permute-start.4 = (bf16[64,2048]{1,0:T(8,128)(2,1)S(1)}, bf16[64,2048]{1,0:T(8,128)(2,1)S(1)}, u32[]{:S(2)}, u32[]{:S(2)}) collective-permute-start(bf16[64,2048]{1,0:T(8,128)(2,1)S(1)} %get-tuple-element.131), channel_id=1, source_target_pairs={{0,1},{1,0},{2,3},{3,2},{4,5},{5,4},{6,7},{7,6},{8,9},{9,8},{10,11... | collective-permute-start | bytes 786440 | tf_op jit(solution)/shard_map/ppermute | solution.py:509
  20.8 2.2 %collective-permute-start.5 = (bf16[64,2048]{1,0:T(8,128)(2,1)S(1)}, bf16[64,2048]{1,0:T(8,128)(2,1)S(1)}, u32[]{:S(2)}, u32[]{:S(2)}) collective-permute-start(bf16[64,2048]{1,0:T(8,128)(2,1)S(1)} %get-tuple-element.132), channel_id=1, source_target_pairs={{0,1},{1,0},{2,3},{3,2},{4,5},{5,4},{6,7},{7,6},{8,9},{9,8},{10,11... | collective-permute-start | bytes 786440 | tf_op jit(solution)/shard_map/ppermute | solution.py:509
  21.3 15.6 %collective-permute-start.2 = (bf16[128,2048]{1,0:T(8,128)(2,1)S(1)}, bf16[128,2048]{1,0:T(8,128)(2,1)S(1)}, u32[]{:S(2)}, u32[]{:S(2)}) collective-permute-start(bf16[128,2048]{1,0:T(8,128)(2,1)S(1)} %get-tuple-element.128), channel_id=1, source_target_pairs={{0,15},{1,2},{2,1},{3,4},{4,3},{5,6},{6,5},{7,8},{8,7},{9,10},{10,... | collective-permute-start | bytes 1572872 | tf_op jit(solution)/shard_map/ppermute | solution.py:512
  26.2 4.4 %collective-permute-start.6 = (bf16[64,2048]{1,0:T(8,128)(2,1)S(1)}, bf16[64,2048]{1,0:T(8,128)(2,1)S(1)}, u32[]{:S(2)}, u32[]{:S(2)}) collective-permute-start(bf16[64,2048]{1,0:T(8,128)(2,1)S(1)} %get-tuple-element.139), channel_id=1, source_target_pairs={{0,1},{1,0},{2,3},{3,2},{4,5},{5,4},{6,7},{7,6},{8,9},{9,8},{10,11... | collective-permute-start | bytes 786440 | tf_op jit(solution)/shard_map/ppermute | solution.py:509
  29.4 1.5 %collective-permute-start.7 = (bf16[64,2048]{1,0:T(8,128)(2,1)S(1)}, bf16[64,2048]{1,0:T(8,128)(2,1)S(1)}, u32[]{:S(2)}, u32[]{:S(2)}) collective-permute-start(bf16[64,2048]{1,0:T(8,128)(2,1)S(1)} %get-tuple-element.140), channel_id=1, source_target_pairs={{0,1},{1,0},{2,3},{3,2},{4,5},{5,4},{6,7},{7,6},{8,9},{9,8},{10,11... | collective-permute-start | bytes 786440 | tf_op jit(solution)/shard_map/ppermute | solution.py:509
  32.7 11.9 %collective-permute-start.8 = (bf16[48,2048]{1,0:T(8,128)(2,1)S(1)}, bf16[48,2048]{1,0:T(8,128)(2,1)S(1)}, u32[]{:S(2)}, u32[]{:S(2)}) collective-permute-start(bf16[48,2048]{1,0:T(8,128)(2,1)S(1)} %get-tuple-element.153), channel_id=1, source_target_pairs={{0,15},{1,2},{2,1},{3,4},{4,3},{5,6},{6,5},{7,8},{8,7},{9,10},{10,... | collective-permute-start | bytes 589832 | tf_op jit(solution)/shard_map/ppermute | solution.py:512
  40.2 11.2 %collective-permute-start.9 = (bf16[64,2048]{1,0:T(8,128)(2,1)S(1)}, bf16[64,2048]{1,0:T(8,128)(2,1)S(1)}, u32[]{:S(2)}, u32[]{:S(2)}) collective-permute-start(bf16[64,2048]{1,0:T(8,128)(2,1)S(1)} %get-tuple-element.170), channel_id=1, source_target_pairs={{0,15},{1,2},{2,1},{3,4},{4,3},{5,6},{6,5},{7,8},{8,7},{9,10},{10,... | collective-permute-start | bytes 786440 | tf_op jit(solution)/shard_map/ppermute | solution.py:512
  42.8 15.0 %collective-permute-start.11 = (bf16[64,2048]{1,0:T(8,128)(2,1)S(1)}, bf16[64,2048]{1,0:T(8,128)(2,1)S(1)}, u32[]{:S(2)}, u32[]{:S(2)}) collective-permute-start(bf16[64,2048]{1,0:T(8,128)(2,1)S(1)} %get-tuple-element.177), channel_id=1, source_target_pairs={{0,15},{1,2},{2,1},{3,4},{4,3},{5,6},{6,5},{7,8},{8,7},{9,10},{10,... | collective-permute-start | bytes 786440 | tf_op jit(solution)/shard_map/ppermute | solution.py:512
  51.4 11.8 %collective-permute-start.10 = (bf16[80,2048]{1,0:T(8,128)(2,1)S(1)}, bf16[80,2048]{1,0:T(8,128)(2,1)S(1)}, u32[]{:S(2)}, u32[]{:S(2)}) collective-permute-start(bf16[80,2048]{1,0:T(8,128)(2,1)S(1)} %get-tuple-element.175), channel_id=1, source_target_pairs={{0,15},{1,2},{2,1},{3,4},{4,3},{5,6},{6,5},{7,8},{8,7},{9,10},{10,... | collective-permute-start | bytes 983048 | tf_op jit(solution)/shard_map/ppermute | solution.py:512
  59.5 1.9 %collective-permute-start.12 = (bf16[64,2048]{1,0:T(8,128)(2,1)S(1)}, bf16[64,2048]{1,0:T(8,128)(2,1)S(1)}, u32[]{:S(2)}, u32[]{:S(2)}) collective-permute-start(bf16[64,2048]{1,0:T(8,128)(2,1)S(1)} %get-tuple-element.180), channel_id=1, source_target_pairs={{0,1},{1,0},{2,3},{3,2},{4,5},{5,4},{6,7},{7,6},{8,9},{9,8},{10,11... | collective-permute-start | bytes 786440 | tf_op jit(solution)/shard_map/ppermute | solution.py:509
  59.6 1.9 %collective-permute-start.13 = (bf16[64,2048]{1,0:T(8,128)(2,1)S(1)}, bf16[64,2048]{1,0:T(8,128)(2,1)S(1)}, u32[]{:S(2)}, u32[]{:S(2)}) collective-permute-start(bf16[64,2048]{1,0:T(8,128)(2,1)S(1)} %get-tuple-element.181), channel_id=1, source_target_pairs={{0,1},{1,0},{2,3},{3,2},{4,5},{5,4},{6,7},{7,6},{8,9},{9,8},{10,11... | collective-permute-start | bytes 786440 | tf_op jit(solution)/shard_map/ppermute | solution.py:509

commit v5 on v4

--- a/solution.py
+++ b/solution.py
@@ -18,6 +18,7 @@
 SCALE = 1.0 / math.sqrt(HEAD_DIM)
 VM = pl.BlockSpec(memory_space=pltpu.VMEM)
 NEAR_PARTS = 2
+NEAR_SMALL = 4
 FAR_SHARES = (3, 5)
 
 
@@ -523,9 +524,9 @@
     b2_out, b1_saved = forward_kernel(after(b1, b0_saved[4]), fixed, mask, 1)
     *turned, cot_a, cot_b = prepare_kernel(gain, wq, wo, b1_saved[4], cotangent_down, cotangent_up)
     b2 = swap_far(after(b2_out, turned[2]))
-    a2_out, a1_saved = forward_kernel(after(a1, turned[2]), fixed, mask, NEAR_PARTS)
+    a2_out, a1_saved = forward_kernel(after(a1, turned[2]), fixed, mask, NEAR_SMALL)
     a2 = swap_near(a2_out)
-    out_a, ea2, use_a2 = turn_kernel(after(a2, a1_saved[4]), cot_a, fixed, mask, turned, NEAR_PARTS)
+    out_a, ea2, use_a2 = turn_kernel(after(a2, a1_saved[4]), cot_a, fixed, mask, turned, NEAR_SMALL)
     ca1 = swap_near(ea2)
     (ea1_fore, ea1_rest), use_a1 = backward_kernel(after(ca1, use_a2[4]), a1, gain, turned, a1_saved, FAR_SHARES)
     (ca0_fore,) = swap_far([ea1_fore])

time: 67.5 us -> 68.9 us (1.021)
  starting transfers between devices: 16.5 us -> 18.9 us
  waiting for transfers between devices: 20.3 us -> 19.4 us
    ppermute x6, starting transfers between devices: 9.12 us -> 13.1 us  [swap_far(): return [lax.ppermute(part, 'section', far) for part in x]]
    ppermute x6, waiting for transfers between devices: 17.3 us -> 15.7 us  [swap_far(): return [lax.ppermute(part, 'section', far) for part in x]]
    ppermute x8 -> x12, starting transfers between devices: 7.43 us -> 5.75 us  [swap_near(): return [lax.ppermute(part, 'section', near) for part in x]]
    ppermute x8 -> x12, waiting for transfers between devices: 2.99 us -> 3.7 us  [swap_near(): return [lax.ppermute(part, 'section', near) for part in x]]
  transfers between devices with their start and end apart: 14 -> 18, of which waited for: 10 -> 15; matrix products, arithmetic and copies ran while one was open for 0% -> 0% of each run, Pallas kernels for 31% -> 33%
where the time goes in v5:
time: 68.9 us; the launch traced here: 68.7 us
  Pallas kernels  29.6 us (43%)
  waiting for transfers between devices  19.4 us (28%)
  starting transfers between devices  18.9 us (27%)
  between operations  0.92 us (1%)
    pallas_call x13, Pallas kernels, call(): pl.pallas_call(kernel, in_specs=[far if isinstance(x, Far) else VM for x...  29.6 us
    ppermute x6, waiting for transfers between devices, swap_far(): return [lax.ppermute(part, 'section', far) for part in x]  15.7 us
    ppermute x6, starting transfers between devices, swap_far(): return [lax.ppermute(part, 'section', far) for part in x]  13.1 us
    ppermute x12, starting transfers between devices, swap_near(): return [lax.ppermute(part, 'section', near) for part in x]  5.75 us
    ppermute x12, waiting for transfers between devices, swap_near(): return [lax.ppermute(part, 'section', near) for part in x]  3.7 us
  transfers between devices with their start and end apart: 18, of which 15 were waited for; matrix products, arithmetic and copies ran while one was open for 0% of the time, Pallas kernels for 33%

profile of v5, /device:TPU:1, one launch (start us, length us, event | category | flops | bytes accessed | tf_op | source)
XLA Modules:
  0.0 68.7 jit_solution(8594241989799049647)
XLA Ops:
  0.6 3.3 %first.1 = (bf16[128,2048]{1,0:T(8,128)(2,1)S(1)}, bf16[128,2048]{1,0:T(8,128)(2,1)S(1)}, bf16[1,2048]{1,0:T(2,128)(2,1)S(1)}, bf16[2048,768]{1,0:T(8,128)(2,1)S...) custom-call(s32[2,4]{1,0:T(2,128)} %bitcast.1, ...), custom_call_target="tpu_custom_call" | custom-call | flops 2000000 | bytes 200 | tf_op jit(solution)/shard_map/first/pallas_call | solution.py:192
  4.0 2.7 %collective-permute-start.3 = (bf16[128,2048]{1,0:T(8,128)(2,1)S(1)}, bf16[128,2048]{1,0:T(8,128)(2,1)S(1)}, u32[]{:S(2)}, u32[]{:S(2)}) collective-permute-start(bf16[128,2048]{1,0:T(8,128)(2,1)S(1)} %get-tuple-element.137), channel_id=1, source_target_pairs={{0,15},{1,2},{2,1},{3,4},{4,3},{5,6},{6,5},{7,8},{8,7},{9,10},{10,... | collective-permute-start | bytes 1572872 | tf_op jit(solution)/shard_map/ppermute | solution.py:513
  6.7 1.6 %forward.3 = (bf16[64,2048]{1,0:T(8,128)(2,1)S(1)}, bf16[64,2048]{1,0:T(8,128)(2,1)S(1)}, bf16[128,2048]{1,0:T(8,128)(2,1)S(1)}, bf16[128,768]{1,0:T(8,128)(2,1)...) custom-call(bf16[128,2048]{1,0:T(8,128)(2,1)S(1)} %get-tuple-element.123.refs_0_.refs_2_, ...), custom_call_target="tpu_custom_call" | custom-call | flops 2000000 | bytes 200 | tf_op jit(solution)/shard_map/forward/pallas_call | solution.py:192
  8.2 2.9 %collective-permute-start = (bf16[64,2048]{1,0:T(8,128)(2,1)S(1)}, bf16[64,2048]{1,0:T(8,128)(2,1)S(1)}, u32[]{:S(2)}, u32[]{:S(2)}) collective-permute-start(bf16[64,2048]{1,0:T(8,128)(2,1)S(1)} %get-tuple-element.128), channel_id=1, source_target_pairs={{0,1},{1,0},{2,3},{3,2},{4,5},{5,4},{6,7},{7,6},{8,9},{9,8},{10,11... | collective-permute-start | bytes 786440 | tf_op jit(solution)/shard_map/ppermute | solution.py:510
  11.3 1.1 %collective-permute-done.refs_0_.refs_2_ = bf16[64,2048]{1,0:T(8,128)(2,1)S(1)} collective-permute-done((bf16[64,2048]{1,0:T(8,128)(2,1)S(1)}, bf16[64,2048]{1,0:T(8,128)(2,1)S(1)}, u32[]{:S(2)}, u32[]{:S(2)}) %collective-permute-start) | collective-permute-done | bytes 262176 | tf_op jit(solution)/shard_map/ppermute | solution.py:510
  12.7 1.6 %forward.4 = (bf16[128,2048]{1,0:T(8,128)(2,1)S(1)}, bf16[128,2048]{1,0:T(8,128)(2,1)S(1)}, bf16[128,768]{1,0:T(8,128)(2,1)S(1)}, f32[2,128,128]{2,1,0:T(8,128)S...) custom-call(bf16[64,2048]{1,0:T(8,128)(2,1)S(1)} %collective-permute-done.refs_0_.refs_2_, ...), custom_call_target="tpu_custom_call" | custom-call | flops 2000000 | bytes 200 | tf_op jit(solution)/shard_map/forward/pallas_call | solution.py:192
  14.3 1.5 %prepare.1 = (bf16[768,2048]{1,0:T(8,128)(2,1)S(1)}, bf16[2048,256]{1,0:T(8,128)(2,1)S(1)}, f32[1,768]{1,0:T(1,128)S(1)}, bf16[128,2048]{1,0:T(8,128)(2,1)S(1)}, bf16[128,2048]{1,0:T(8,128)(2,1)S(1)}) custom-call(bf16[1,2048]{1,0:T(2,128)(2,1)S(1)} %get-tuple-element.124.refs_1_.refs_2_.refs_0_.refs_5_.refs_4_.refs_3_, ...), custom_call_target="tpu_custom_call" | custom-call | flops 2000000 | bytes 200 | tf_op jit(solution)/shard_map/prepare/pallas_call | solution.py:192
  15.9 8.1 %collective-permute-done.3.refs_0_.refs_4_ = bf16[128,2048]{1,0:T(8,128)(2,1)S(1)} collective-permute-done((bf16[128,2048]{1,0:T(8,128)(2,1)S(1)}, bf16[128,2048]{1,0:T(8,128)(2,1)S(1)}, u32[]{:S(2)}, u32[]{:S(2)}) %collective-permute-start.3) | collective-permute-done | bytes 524320 | tf_op jit(solution)/shard_map/ppermute | solution.py:513
  24.0 1.6 %forward.5 = (bf16[32,2048]{1,0:T(8,128)(2,1)S(1)}, bf16[32,2048]{1,0:T(8,128)(2,1)S(1)}, bf16[32,2048]{1,0:T(8,128)(2,1)S(1)}, bf16[32,2048]{1,0:T(8,128)(2,1)S...) custom-call(bf16[128,2048]{1,0:T(8,128)(2,1)S(1)} %collective-permut, ...), custom_call_target="tpu_custom_call" | custom-call | flops 2000000 | bytes 200 | tf_op jit(solution)/shard_map/forward/pallas_call | solution.py:192
  25.7 0.5 collective-permute-start.5
  27.7 3.2 %turn.2 = (bf16[128,2048]{1,0:T(8,128)(2,1)S(1)}, bf16[32,2048]{1,0:T(8,128)(2,1)S(1)}, bf16[32,2048]{1,0:T(8,128)(2,1)S(1)}, bf16[32,2048]{1,0:T(8,128)(2,1)S(1...) custom-call(bf16[32,2048]{1,0:T(8,128)(2,1)S(1)} %collective-permute, ...), custom_call_target="tpu_custom_call" | custom-call | flops 2000000 | bytes 200 | tf_op jit(solution)/shard_map/turn/pallas_call | solution.py:192
  33.2 1.7 %backward.3 = (bf16[48,2048]{1,0:T(8,128)(2,1)S(1)}, bf16[80,2048]{1,0:T(8,128)(2,1)S(1)}, bf16[128,768]{1,0:T(8,128)(2,1)S(1)}, f32[8,2048]{1,0:T(8,128)S(1)}) custom-call(bf16[32,2048]{1,0:T(8,128)(2,1)S(1)} %collective-permute-done.8.refs_0_.refs_13_, bf16[32,2048]{1,0:T(8,128)(2,1)S(1)} %collective-permute-done.9.refs_1_.refs_14_, ...), custom_call_target="tpu_custom_call" | custom-call | flops 2000000 | bytes 200 | tf_op jit(solution)/shard_map/backward/pallas_call | solution.py:192
  34.9 2.5 %collective-permute-start.12 = (bf16[48,2048]{1,0:T(8,128)(2,1)S(1)}, bf16[48,2048]{1,0:T(8,128)(2,1)S(1)}, u32[]{:S(2)}, u32[]{:S(2)}) collective-permute-start(bf16[48,2048]{1,0:T(8,128)(2,1)S(1)} %get-tuple-element.169), channel_id=1, source_target_pairs={{0,15},{1,2},{2,1},{3,4},{4,3},{5,6},{6,5},{7,8},{8,7},{9,10},{10,... | collective-permute-start | bytes 589832 | tf_op jit(solution)/shard_map/ppermute | solution.py:513
  37.4 3.3 %turn.3 = (bf16[128,2048]{1,0:T(8,128)(2,1)S(1)}, bf16[64,2048]{1,0:T(8,128)(2,1)S(1)}, bf16[64,2048]{1,0:T(8,128)(2,1)S(1)}, bf16[128,2048]{1,0:T(8,128)(2,1)S(...) custom-call(bf16[128,2048]{1,0:T(8,128)(2,1)S(1)} %collective-permute-done.2.refs_0_, ...), custom_call_target="tpu_custom_call" | custom-call | flops 2000000 | bytes 200 | tf_op jit(solution)/shard_map/turn/pallas_call | solution.py:192
  40.9 1.7 %collective-permute-start.15 = (bf16[64,2048]{1,0:T(8,128)(2,1)S(1)}, bf16[64,2048]{1,0:T(8,128)(2,1)S(1)}, u32[]{:S(2)}, u32[]{:S(2)}) collective-permute-start(bf16[64,2048]{1,0:T(8,128)(2,1)S(1)} %get-tuple-element.193), channel_id=1, source_target_pairs={{0,15},{1,2},{2,1},{3,4},{4,3},{5,6},{6,5},{7,8},{8,7},{9,10},{10,... | collective-permute-start | bytes 786440 | tf_op jit(solution)/shard_map/ppermute | solution.py:513
  42.6 3.1 %early_weights.1 = (bf16[1,128,2048]{2,1,0:T(8,128)(2,1)}, bf16[1,128,2048]{2,1,0:T(8,128)(2,1)}, f32[8,2048]{1,0:T(8,128)S(1)}, f32[256,2048]{1,0:T(8,128)S(1)}, f32[2048,768]{1,0:T(8,128)S(1)}) custom-call(bf16[128,2048]{1,0:T(8,128)(2,1)S(1)} %get-tuple-element.170.refs_0_, bf16[128,768]{1,0:T(8,128)(2,1)S(1)} %get-tuple-element.171.refs_1_, ...), custom_call_target="tpu_custom_call" | custom-call | flops 8000000000 | bytes 800000 | tf_op jit(solution)/shard_map/early_weights/pallas_call | solution.py:192
  45.7 4.9 %collective-permute-done.13.refs_0_.refs_3_ = bf16[64,2048]{1,0:T(8,128)(2,1)S(1)} collective-permute-done((bf16[64,2048]{1,0:T(8,128)(2,1)S(1)}, bf16[64,2048]{1,0:T(8,128)(2,1)S(1)}, u32[]{:S(2)}, u32[]{:S(2)}) %collective-permute-start.13) | collective-permute-done | bytes 262176 | tf_op jit(solution)/shard_map/ppermute | solution.py:513
  50.6 6.0 %collective-permute-start.14 = (bf16[80,2048]{1,0:T(8,128)(2,1)S(1)}, bf16[80,2048]{1,0:T(8,128)(2,1)S(1)}, u32[]{:S(2)}, u32[]{:S(2)}) collective-permute-start(bf16[80,2048]{1,0:T(8,128)(2,1)S(1)} %get-tuple-element.191), channel_id=1, source_target_pairs={{0,15},{1,2},{2,1},{3,4},{4,3},{5,6},{6,5},{7,8},{8,7},{9,10},{10,... | collective-permute-start | bytes 983048 | tf_op jit(solution)/shard_map/ppermute | solution.py:513
  56.9 1.7 %backward.4 = (bf16[64,2048]{1,0:T(8,128)(2,1)S(1)}, bf16[64,2048]{1,0:T(8,128)(2,1)S(1)}, bf16[128,768]{1,0:T(8,128)(2,1)S(1)}, f32[8,2048]{1,0:T(8,128)S(1)}) custom-call(bf16[64,2048]{1,0:T(8,128)(2,1)S(1)} %collective-permute-done.13.refs_0_.refs_3_, bf16[64,2048]{1,0:T(8,128)(2,1)S(1)} %collective-permute-done.15.refs_1_.refs_4_, ...), custom_call_target="tpu_custom_call" | custom-call | flops 2000000 | bytes 200 | tf_op jit(solution)/shard_map/backward/pallas_call | solution.py:192
  58.7 0.5 collective-permute-start.17
  59.2 1.3 %more_weights.1 = (f32[8,2048]{1,0:T(8,128)S(1)}, f32[256,2048]{1,0:T(8,128)S(1)}, f32[2048,768]{1,0:T(8,128)S(1)}) custom-call(bf16[128,2048]{1,0:T(8,128)(2,1)S(1)} %get-tuple-element.202.refs_0_, bf16[128,768]{1,0:T(8,128)(2,1)S(1)} %get-tuple-element.203.refs_1_, bf16[128,256]{1,0:T(8,128)(2,1)S(1)} %get-tuple-element.204.refs_2_, ...), custom_call_target="tpu_custom_call" | custom-call | flops 2000000 | bytes 200 | tf_op jit(solution)/shard_map/more_weights/pallas_call | solution.py:192
  60.6 1.8 %backward.5 = (bf16[128,2048]{1,0:T(8,128)(2,1)S(1)}, bf16[128,768]{1,0:T(8,128)(2,1)S(1)}, f32[8,2048]{1,0:T(8,128)S(1)}) custom-call(bf16[64,2048]{1,0:T(8,128)(2,1)S(1)} %collective-permute-done.16.refs_0_.refs_16_, bf16[64,2048]{1,0:T(8,128)(2,1)S(1)} %collective-permute-done.17.refs_1_.refs_17_, ...), custom_call_target="tpu_custom_call" | custom-call | flops 2000000 | bytes 200 | tf_op jit(solution)/shard_map/backward/pallas_call | solution.py:192
  62.4 2.3 %collective-permute-done.14.refs_1_ = bf16[80,2048]{1,0:T(8,128)(2,1)S(1)} collective-permute-done((bf16[80,2048]{1,0:T(8,128)(2,1)S(1)}, bf16[80,2048]{1,0:T(8,128)(2,1)S(1)}, u32[]{:S(2)}, u32[]{:S(2)}) %collective-permute-start.14) | collective-permute-done | bytes 327712 | tf_op jit(solution)/shard_map/ppermute | solution.py:513
  64.7 3.9 %finish.1 = (bf16[1,128,2048]{2,1,0:T(8,128)(2,1)}, bf16[1,128,2048]{2,1,0:T(8,128)(2,1)}, bf16[1,2048]{1,0:T(2,128)(2,1)}, bf16[1,256,2048]{2,1,0:T(8,128)(2,1)}, bf16[1,2048,768]{2,1,0:T(8,128)(2,1)}) custom-call(bf16[48,2048]{1,0:T(8,128)(2,1)S(1)} %collective-permute-done.12.refs_0_, bf16[80,2048]{1,0:T(8,128)(2,1)S(1)} %collective-permute-done.14.refs_1_, ...), custom_call_target="tpu_custom_call" | custom-call | flops 2000000 | bytes 200 | tf_op jit(solution)/shard_map/finish/pallas_call | solution.py:192
  (25 shorter events, 4.9 us)
Async XLA Ops:
  4.0 20.1 %collective-permute-start.3 = (bf16[128,2048]{1,0:T(8,128)(2,1)S(1)}, bf16[128,2048]{1,0:T(8,128)(2,1)S(1)}, u32[]{:S(2)}, u32[]{:S(2)}) collective-permute-start(bf16[128,2048]{1,0:T(8,128)(2,1)S(1)} %get-tuple-element.137), channel_id=1, source_target_pairs={{0,15},{1,2},{2,1},{3,4},{4,3},{5,6},{6,5},{7,8},{8,7},{9,10},{10,... | collective-permute-start | bytes 1572872 | tf_op jit(solution)/shard_map/ppermute | solution.py:513
  8.2 4.1 %collective-permute-start = (bf16[64,2048]{1,0:T(8,128)(2,1)S(1)}, bf16[64,2048]{1,0:T(8,128)(2,1)S(1)}, u32[]{:S(2)}, u32[]{:S(2)}) collective-permute-start(bf16[64,2048]{1,0:T(8,128)(2,1)S(1)} %get-tuple-element.128), channel_id=1, source_target_pairs={{0,1},{1,0},{2,3},{3,2},{4,5},{5,4},{6,7},{7,6},{8,9},{9,8},{10,11... | collective-permute-start | bytes 786440 | tf_op jit(solution)/shard_map/ppermute | solution.py:510
  11.2 1.5 %collective-permute-start.1 = (bf16[64,2048]{1,0:T(8,128)(2,1)S(1)}, bf16[64,2048]{1,0:T(8,128)(2,1)S(1)}, u32[]{:S(2)}, u32[]{:S(2)}) collective-permute-start(bf16[64,2048]{1,0:T(8,128)(2,1)S(1)} %get-tuple-element.129), channel_id=1, source_target_pairs={{0,1},{1,0},{2,3},{3,2},{4,5},{5,4},{6,7},{7,6},{8,9},{9,8},{10,11... | collective-permute-start | bytes 786440 | tf_op jit(solution)/shard_map/ppermute | solution.py:510
  15.8 21.6 %collective-permute-start.2 = (bf16[128,2048]{1,0:T(8,128)(2,1)S(1)}, bf16[128,2048]{1,0:T(8,128)(2,1)S(1)}, u32[]{:S(2)}, u32[]{:S(2)}) collective-permute-start(bf16[128,2048]{1,0:T(8,128)(2,1)S(1)} %get-tuple-element.136), channel_id=1, source_target_pairs={{0,15},{1,2},{2,1},{3,4},{4,3},{5,6},{6,5},{7,8},{8,7},{9,10},{10,... | collective-permute-start | bytes 1572872 | tf_op jit(solution)/shard_map/ppermute | solution.py:513
  25.6 1.4 %collective-permute-start.4 = (bf16[32,2048]{1,0:T(8,128)(2,1)S(1)}, bf16[32,2048]{1,0:T(8,128)(2,1)S(1)}, u32[]{:S(2)}, u32[]{:S(2)}) collective-permute-start(bf16[32,2048]{1,0:T(8,128)(2,1)S(1)} %get-tuple-element.139), channel_id=1, source_target_pairs={{0,1},{1,0},{2,3},{3,2},{4,5},{5,4},{6,7},{7,6},{8,9},{9,8},{10,11... | collective-permute-start | bytes 393224 | tf_op jit(solution)/shard_map/ppermute | solution.py:510
  25.7 1.5 %collective-permute-start.5 = (bf16[32,2048]{1,0:T(8,128)(2,1)S(1)}, bf16[32,2048]{1,0:T(8,128)(2,1)S(1)}, u32[]{:S(2)}, u32[]{:S(2)}) collective-permute-start(bf16[32,2048]{1,0:T(8,128)(2,1)S(1)} %get-tuple-element.140), channel_id=1, source_target_pairs={{0,1},{1,0},{2,3},{3,2},{4,5},{5,4},{6,7},{7,6},{8,9},{9,8},{10,11... | collective-permute-start | bytes 393224 | tf_op jit(solution)/shard_map/ppermute | solution.py:510
  26.2 1.3 %collective-permute-start.6 = (bf16[32,2048]{1,0:T(8,128)(2,1)S(1)}, bf16[32,2048]{1,0:T(8,128)(2,1)S(1)}, u32[]{:S(2)}, u32[]{:S(2)}) collective-permute-start(bf16[32,2048]{1,0:T(8,128)(2,1)S(1)} %get-tuple-element.141), channel_id=1, source_target_pairs={{0,1},{1,0},{2,3},{3,2},{4,5},{5,4},{6,7},{7,6},{8,9},{9,8},{10,11... | collective-permute-start | bytes 393224 | tf_op jit(solution)/shard_map/ppermute | solution.py:510
  26.3 1.5 %collective-permute-start.7 = (bf16[32,2048]{1,0:T(8,128)(2,1)S(1)}, bf16[32,2048]{1,0:T(8,128)(2,1)S(1)}, u32[]{:S(2)}, u32[]{:S(2)}) collective-permute-start(bf16[32,2048]{1,0:T(8,128)(2,1)S(1)} %get-tuple-element.142), channel_id=1, source_target_pairs={{0,1},{1,0},{2,3},{3,2},{4,5},{5,4},{6,7},{7,6},{8,9},{9,8},{10,11... | collective-permute-start | bytes 393224 | tf_op jit(solution)/shard_map/ppermute | solution.py:510
  30.9 1.4 %collective-permute-start.8 = (bf16[32,2048]{1,0:T(8,128)(2,1)S(1)}, bf16[32,2048]{1,0:T(8,128)(2,1)S(1)}, u32[]{:S(2)}, u32[]{:S(2)}) collective-permute-start(bf16[32,2048]{1,0:T(8,128)(2,1)S(1)} %get-tuple-element.151), channel_id=1, source_target_pairs={{0,1},{1,0},{2,3},{3,2},{4,5},{5,4},{6,7},{7,6},{8,9},{9,8},{10,11... | collective-permute-start | bytes 393224 | tf_op jit(solution)/shard_map/ppermute | solution.py:510
  31.3 1.3 %collective-permute-start.9 = (bf16[32,2048]{1,0:T(8,128)(2,1)S(1)}, bf16[32,2048]{1,0:T(8,128)(2,1)S(1)}, u32[]{:S(2)}, u32[]{:S(2)}) collective-permute-start(bf16[32,2048]{1,0:T(8,128)(2,1)S(1)} %get-tuple-element.152), channel_id=1, source_target_pairs={{0,1},{1,0},{2,3},{3,2},{4,5},{5,4},{6,7},{7,6},{8,9},{9,8},{10,11... | collective-permute-start | bytes 393224 | tf_op jit(solution)/shard_map/ppermute | solution.py:510
  31.5 1.3 %collective-permute-start.10 = (bf16[32,2048]{1,0:T(8,128)(2,1)S(1)}, bf16[32,2048]{1,0:T(8,128)(2,1)S(1)}, u32[]{:S(2)}, u32[]{:S(2)}) collective-permute-start(bf16[32,2048]{1,0:T(8,128)(2,1)S(1)} %get-tuple-element.153), channel_id=1, source_target_pairs={{0,1},{1,0},{2,3},{3,2},{4,5},{5,4},{6,7},{7,6},{8,9},{9,8},{10,11... | collective-permute-start | bytes 393224 | tf_op jit(solution)/shard_map/ppermute | solution.py:510
  31.8 1.3 %collective-permute-start.11 = (bf16[32,2048]{1,0:T(8,128)(2,1)S(1)}, bf16[32,2048]{1,0:T(8,128)(2,1)S(1)}, u32[]{:S(2)}, u32[]{:S(2)}) collective-permute-start(bf16[32,2048]{1,0:T(8,128)(2,1)S(1)} %get-tuple-element.154), channel_id=1, source_target_pairs={{0,1},{1,0},{2,3},{3,2},{4,5},{5,4},{6,7},{7,6},{8,9},{9,8},{10,11... | collective-permute-start | bytes 393224 | tf_op jit(solution)/shard_map/ppermute | solution.py:510
  34.9 7.7 %collective-permute-start.12 = (bf16[48,2048]{1,0:T(8,128)(2,1)S(1)}, bf16[48,2048]{1,0:T(8,128)(2,1)S(1)}, u32[]{:S(2)}, u32[]{:S(2)}) collective-permute-start(bf16[48,2048]{1,0:T(8,128)(2,1)S(1)} %get-tuple-element.169), channel_id=1, source_target_pairs={{0,15},{1,2},{2,1},{3,4},{4,3},{5,6},{6,5},{7,8},{8,7},{9,10},{10,... | collective-permute-start | bytes 589832 | tf_op jit(solution)/shard_map/ppermute | solution.py:513
  40.8 9.8 %collective-permute-start.13 = (bf16[64,2048]{1,0:T(8,128)(2,1)S(1)}, bf16[64,2048]{1,0:T(8,128)(2,1)S(1)}, u32[]{:S(2)}, u32[]{:S(2)}) collective-permute-start(bf16[64,2048]{1,0:T(8,128)(2,1)S(1)} %get-tuple-element.186), channel_id=1, source_target_pairs={{0,15},{1,2},{2,1},{3,4},{4,3},{5,6},{6,5},{7,8},{8,7},{9,10},{10,... | collective-permute-start | bytes 786440 | tf_op jit(solution)/shard_map/ppermute | solution.py:513
  40.9 16.0 %collective-permute-start.15 = (bf16[64,2048]{1,0:T(8,128)(2,1)S(1)}, bf16[64,2048]{1,0:T(8,128)(2,1)S(1)}, u32[]{:S(2)}, u32[]{:S(2)}) collective-permute-start(bf16[64,2048]{1,0:T(8,128)(2,1)S(1)} %get-tuple-element.193), channel_id=1, source_target_pairs={{0,15},{1,2},{2,1},{3,4},{4,3},{5,6},{6,5},{7,8},{8,7},{9,10},{10,... | collective-permute-start | bytes 786440 | tf_op jit(solution)/shard_map/ppermute | solution.py:513
  50.6 14.1 %collective-permute-start.14 = (bf16[80,2048]{1,0:T(8,128)(2,1)S(1)}, bf16[80,2048]{1,0:T(8,128)(2,1)S(1)}, u32[]{:S(2)}, u32[]{:S(2)}) collective-permute-start(bf16[80,2048]{1,0:T(8,128)(2,1)S(1)} %get-tuple-element.191), channel_id=1, source_target_pairs={{0,15},{1,2},{2,1},{3,4},{4,3},{5,6},{6,5},{7,8},{8,7},{9,10},{10,... | collective-permute-start | bytes 983048 | tf_op jit(solution)/shard_map/ppermute | solution.py:513
  58.7 1.9 %collective-permute-start.16 = (bf16[64,2048]{1,0:T(8,128)(2,1)S(1)}, bf16[64,2048]{1,0:T(8,128)(2,1)S(1)}, u32[]{:S(2)}, u32[]{:S(2)}) collective-permute-start(bf16[64,2048]{1,0:T(8,128)(2,1)S(1)} %get-tuple-element.196), channel_id=1, source_target_pairs={{0,1},{1,0},{2,3},{3,2},{4,5},{5,4},{6,7},{7,6},{8,9},{9,8},{10,11... | collective-permute-start | bytes 786440 | tf_op jit(solution)/shard_map/ppermute | solution.py:510
  58.7 1.9 %collective-permute-start.17 = (bf16[64,2048]{1,0:T(8,128)(2,1)S(1)}, bf16[64,2048]{1,0:T(8,128)(2,1)S(1)}, u32[]{:S(2)}, u32[]{:S(2)}) collective-permute-start(bf16[64,2048]{1,0:T(8,128)(2,1)S(1)} %get-tuple-element.197), channel_id=1, source_target_pairs={{0,1},{1,0},{2,3},{3,2},{4,5},{5,4},{6,7},{7,6},{8,9},{9,8},{10,11... | collective-permute-start | bytes 786440 | tf_op jit(solution)/shard_map/ppermute | solution.py:510

commit v6 on v3

--- a/solution.py
+++ b/solution.py
@@ -51,7 +51,7 @@
     return jnp.concatenate([ref[:, cols] for ref in refs], axis=0)
 
 
-def forward_body(h, gain_ref, wq_ref, wo_ref, mask_ref, out, u_ref, qkv_ref, p_ref, att_ref, st_ref, waits=None):
+def attend(h, gain_ref, wq_ref, mask_ref, u_ref, qkv_ref, p_ref, att_ref, st_ref, waits=None):
     rows, width = u_ref.shape
     hd = HEADS_DEV * HEAD_DIM
     gain = gain_ref[...].astype(F32)
@@ -80,8 +80,10 @@
     for head, cols in enumerate(heads):
         p_ref[head] = probs[head]
         att_ref[:, cols] = mixed[head].astype(BF16)
-    if waits:
-        waits[3].wait()
+
+
+def project_out(h, att_ref, wo_ref, out):
+    rows, width = att_ref.shape[0], wo_ref.shape[1]
     for n in range(0, width, 512):
         cols = pl.ds(n, 512)
         value = dot(att_ref[...], wo_ref[:, cols])
@@ -90,9 +92,15 @@
             write(out, at, size, (read(h, at, size, cols).astype(F32) + value[at:at + size]).astype(BF16), cols)
 
 
-def attention_reverse(g, wot_ref, qkv_ref, p_ref, dqkv_ref):
-    hd = HEADS_DEV * HEAD_DIM
-    datt = dot(whole(g), wot_ref[...]).astype(BF16)
+def forward_body(h, gain_ref, wq_ref, wo_ref, mask_ref, out, u_ref, qkv_ref, p_ref, att_ref, st_ref, waits=None):
+    attend(h, gain_ref, wq_ref, mask_ref, u_ref, qkv_ref, p_ref, att_ref, st_ref, waits)
+    if waits:
+        waits[3].wait()
+    project_out(h, att_ref, wo_ref, out)
+
+
+def attention_reverse(datt, qkv_ref, p_ref, dqkv_ref):
+    hd = HEADS_DEV * HEAD_DIM
     heads = [pl.ds(head * HEAD_DIM, HEAD_DIM) for head in range(HEADS_DEV)]
     keys = [pl.ds(hd + cols.start, HEAD_DIM) for cols in heads]
     values = [pl.ds(2 * hd + cols.start, HEAD_DIM) for cols in heads]
@@ -138,7 +146,7 @@
 
 
 def backward_body(g, h, gain_ref, wqt_ref, wot_ref, wg_ref, qkv_ref, p_ref, st_ref, e, dqkv_ref, dg_ref):
-    attention_reverse(g, wot_ref, qkv_ref, p_ref, dqkv_ref)
+    attention_reverse(dot(whole(g), wot_ref[...]).astype(BF16), qkv_ref, p_ref, dqkv_ref)
     norm_reverse(g, h, gain_ref, wqt_ref, wg_ref, qkv_ref, st_ref, e, dqkv_ref, dg_ref)
 
 
@@ -271,7 +279,7 @@
 
     def body(ins, outs, scratch):
         gain_ref, wq_ref, wo_ref, _, down_hbm, up_hbm = ins
-        wqt_ref, wot_ref, wg_ref, (a_ref,), (b_ref,) = outs
+        wqt_ref, wot_ref, wg_ref, (a_ref,), (b_ref,), da_ref, db_ref = outs
         (sems,) = scratch
         odd = is_odd()
 
@@ -288,30 +296,33 @@
         wg_ref[...] = dot(gain_ref[...], wq_ref[...])
         a_wait()
         b_wait()
+        both = dot(jnp.concatenate([a_ref[...], b_ref[...]], axis=0), wot_ref[...]).astype(BF16)
+        da_ref[...] = both[:rows]
+        db_ref[...] = both[rows:]
 
     return call(
         "prepare", body, [gain, wq, wo, tie, Far(down), Far(up)],
         [Mem((3 * hd, width), BF16), Mem((width, hd), BF16), Mem((1, 3 * hd), F32),
-         stream(rows, width, 1), stream(rows, width, 1)],
+         stream(rows, width, 1), stream(rows, width, 1), Mem((rows, hd), BF16), Mem((rows, hd), BF16)],
         [pltpu.SemaphoreType.DMA((2,))],
     )
 
 
-def turn_kernel(h, g, fixed, mask, turned, parts):
+def turn_kernel(h, g, datt, fixed, mask, turned, parts):
     rows, width = h[0].shape[0] * len(h), h[0].shape[1]
     hd = HEADS_DEV * HEAD_DIM
 
     def body(ins, outs, scratch):
-        h, g, fixed, mask_ref, turned = ins
-        out, e, (u_ref, dqkv_ref, att_ref, dg_ref) = outs
+        h, g, datt_ref, (gain_ref, wq_ref), mask_ref, (wqt_ref, wg_ref) = ins
+        e, (u_ref, dqkv_ref, att_ref, dg_ref) = outs
         qkv_ref, p_ref, st_ref = scratch
-        forward_body(h, *fixed, mask_ref, out, u_ref, qkv_ref, p_ref, att_ref, st_ref)
-        backward_body(g, h, fixed[0], *turned, qkv_ref, p_ref, st_ref, e, dqkv_ref, dg_ref)
-
-    out, e, (u, dqkv, att, dgain) = call(
-        "turn", body, [h, g, fixed, mask, turned],
+        attend(h, gain_ref, wq_ref, mask_ref, u_ref, qkv_ref, p_ref, att_ref, st_ref)
+        attention_reverse(datt_ref[...], qkv_ref, p_ref, dqkv_ref)
+        norm_reverse(g, h, gain_ref, wqt_ref, wg_ref, qkv_ref, st_ref, e, dqkv_ref, dg_ref)
+
+    e, (u, dqkv, att, dgain) = call(
+        "turn", body, [h, g, datt, fixed[:2], mask, [turned[0], turned[2]]],
         [
-            stream(rows, width, 1),
             stream(rows, width, parts),
             [Mem((rows, width), BF16), Mem((rows, 3 * hd), BF16), Mem((rows, hd), BF16), Mem((8, width), F32)],
         ],
@@ -321,7 +332,7 @@
             pltpu.VMEM((rows, 256), F32),
         ],
     )
-    return out, e, (u, dqkv, att, g, dgain)
+    return e, (u, dqkv, att, g, dgain)
 
 
 def backward_kernel(g, h, gain, turned, saved, parts):
@@ -378,15 +389,18 @@
             wait()
 
 
-def early_weights(uses, out_a, out_b):
+def early_weights(uses, h_a, att_a, h_b, att_b, wo):
     rows, width = uses[0][0].shape
     hd = HEADS_DEV * HEAD_DIM
 
     def body(ins, outs, scratch):
-        uses, (a_ref,), (b_ref,) = ins
+        uses, h_a, att_a_ref, h_b, att_b_ref, wo_ref = ins
         (down, up), gain_out, wo_out, wq_out = outs
-        copies = Copies(scratch[0], is_odd())
+        a_ref, b_ref, sems = scratch
+        copies = Copies(sems, is_odd())
+        project_out(h_a, att_a_ref, wo_ref, [a_ref])
         copies.push(a_ref, down.at[0], up.at[0])
+        project_out(h_b, att_b_ref, wo_ref, [b_ref])
         copies.push(b_ref, up.at[0], down.at[0])
         gain_out[...] = gain_sum(uses)
 
@@ -401,12 +415,32 @@
         copies.wait()
 
     outs, *sums = call(
-        "early_weights", body, [list(uses), out_a, out_b],
+        "early_weights", body, [list(uses), h_a, att_a, h_b, att_b, wo],
         [[jax.ShapeDtypeStruct((1, rows, width), BF16)] * 2,
          Mem((8, width), F32), Mem((hd, width), F32), Mem((width, 3 * hd), F32)],
-        [pltpu.SemaphoreType.DMA((2,))],
+        [pltpu.VMEM((rows, width), BF16), pltpu.VMEM((rows, width), BF16), pltpu.SemaphoreType.DMA((2,))],
     )
     return outs, sums
+
+
+def more_weights(uses, sums):
+    width = uses[0][0].shape[1]
+
+    def body(ins, outs, scratch):
+        uses, (gain_in, wo_in, wq_in) = ins
+        gain_out, wo_out, wq_out = outs
+        gain_out[...] = gain_in[...] + gain_sum(uses)
+
+        def put_wo(cols, value):
+            wo_out[:, cols] = wo_in[:, cols] + value
+
+        def put_wq(at, value):
+            wq_out[at, :] = wq_in[at, :] + value
+
+        out_weights(uses, width, put_wo)
+        in_weights(uses, width, put_wq)
+
+    return call("more_weights", body, [list(uses), list(sums)], [Mem(x.shape, F32) for x in sums])
 
 
 def finish_kernel(g, h, gain, turned, saved, back_b, uses, sums):
@@ -434,8 +468,8 @@
         def done(cols):
             copies.push(e_ref.at[:, cols], down.at[0, :, cols], up.at[0, :, cols])
 
-        attention_reverse(g, wot_ref, qkv_ref, p_ref, dqkv_ref)
         out_weights(uses, width, put_wo)
+        attention_reverse(dot(whole(g), wot_ref[...]).astype(BF16), qkv_ref, p_ref, dqkv_ref)
         in_weights(uses, width, put_wq)
         norm_reverse(g, h, gain_ref, wqt_ref, wg_ref, qkv_ref, st_ref, [e_ref], dqkv_ref, dg_ref, done)
         gain_buf[...] = jnp.sum(gain_total[...] + gain_sum(uses), axis=0, keepdims=True).astype(BF16)
@@ -484,18 +518,20 @@
     b1 = swap_near(b1_out)
     b2_out, b1_saved = forward_kernel(after(b1, b0_saved[4]), fixed, mask, 1)
     b2 = swap_far(b2_out)
-    *turned, cot_a, cot_b = prepare_kernel(gain, wq, wo, b1_saved[4], cotangent_down, cotangent_up)
+    *turned, cot_a, cot_b, datt_a, datt_b = prepare_kernel(gain, wq, wo, b1_saved[4], cotangent_down, cotangent_up)
     a2_out, a1_saved = forward_kernel(after(a1, turned[2]), fixed, mask, NEAR_PARTS, us=8)
     a2 = swap_near(a2_out)
-    out_b, eb2, use_b2 = turn_kernel(after(b2, a1_saved[4]), cot_b, fixed, mask, turned, 1)
+    eb2, use_b2 = turn_kernel(after(b2, a1_saved[4]), cot_b, datt_b, fixed, mask, turned, 1)
     cb1 = swap_far(eb2)
-    out_a, ea2, use_a2 = turn_kernel(after(a2, use_b2[4]), cot_a, fixed, mask, turned, NEAR_PARTS)
+    ea2, use_a2 = turn_kernel(after(a2, use_b2[4]), cot_a, datt_a, fixed, mask, turned, NEAR_PARTS)
     ca1 = swap_near(ea2)
     ea1, use_a1 = backward_kernel(after(ca1, use_a2[4]), a1, gain, turned, a1_saved, 1)
     ca0 = swap_far(ea1)
-    eb1, use_b1 = backward_kernel(after(cb1, use_a1[4]), b1, gain, turned, b1_saved, NEAR_PARTS)
+    (out_down, out_up), sums = early_weights(
+        [use_b2, use_a2, after(use_a1, use_a1[4])], a2, use_a2[2], b2, use_b2[2], wo)
+    eb1, use_b1 = backward_kernel(after(cb1, sums[0]), b1, gain, turned, b1_saved, NEAR_PARTS)
     cb0 = swap_near(eb1)
-    (out_down, out_up), sums = early_weights([use_b2, use_a2, use_a1, after(use_b1, use_b1[4])], out_a, out_b)
+    sums = more_weights([after(use_b1, use_b1[4])], sums)
     back_b, use_b0 = backward_kernel(after(cb0, sums[0]), b0, gain, turned, b0_saved, 1)
     (back_down, back_up), d_gain, d_wo, d_wq = finish_kernel(
         after(ca0, use_b0[4]), a0, gain, turned, a0_saved, back_b, [use_b0], sums)

time: 64 us -> 61.5 us (0.961)
  the two profiles are of different devices: /device:TPU:29 before, /device:TPU:1 now
where the time goes in v6:
time: 61.5 us; the launch traced here: 61.3 us
  Pallas kernels  29.8 us (48%)
  waiting for transfers between devices  21.2 us (34%)
  starting transfers between devices  9.39 us (15%)
  between operations  0.94 us (2%)
    pallas_call x13, Pallas kernels, call(): pl.pallas_call(kernel, in_specs=[far if isinstance(x, Far) else VM for x...  29.8 us
    ppermute x4, waiting for transfers between devices, swap_far(): return [lax.ppermute(part, 'section', far) for part in x]  18.3 us
    ppermute x8, starting transfers between devices, swap_near(): return [lax.ppermute(part, 'section', near) for part in x]  4.72 us
    ppermute x4, starting transfers between devices, swap_far(): return [lax.ppermute(part, 'section', far) for part in x]  4.67 us
    ppermute x8, waiting for transfers between devices, swap_near(): return [lax.ppermute(part, 'section', near) for part in x]  2.93 us
  transfers between devices with their start and end apart: 12, of which 9 were waited for; matrix products, arithmetic and copies ran while one was open for 0% of the time, Pallas kernels for 37%

profile of v6, /device:TPU:1, one launch (start us, length us, event | category | flops | bytes accessed | tf_op | source)
XLA Modules:
  0.0 61.3 jit_solution(9469226428155072658)
XLA Ops:
  0.6 3.3 %first.1 = (bf16[128,2048]{1,0:T(8,128)(2,1)S(1)}, bf16[128,2048]{1,0:T(8,128)(2,1)S(1)}, bf16[1,2048]{1,0:T(2,128)(2,1)S(1)}, bf16[2048,768]{1,0:T(8,128)(2,1)S...) custom-call(s32[2,4]{1,0:T(2,128)} %bitcast.1, ...), custom_call_target="tpu_custom_call" | custom-call | flops 2000000 | bytes 200 | tf_op jit(solution)/shard_map/first/pallas_call | solution.py:182
  4.0 2.7 %collective-permute-start.3 = (bf16[128,2048]{1,0:T(8,128)(2,1)S(1)}, bf16[128,2048]{1,0:T(8,128)(2,1)S(1)}, u32[]{:S(2)}, u32[]{:S(2)}) collective-permute-start(bf16[128,2048]{1,0:T(8,128)(2,1)S(1)} %get-tuple-element.117), channel_id=1, source_target_pairs={{0,15},{1,2},{2,1},{3,4},{4,3},{5,6},{6,5},{7,8},{8,7},{9,10},{10,... | collective-permute-start | bytes 1572872 | tf_op jit(solution)/shard_map/ppermute | solution.py:508
  6.7 1.6 %forward.3 = (bf16[64,2048]{1,0:T(8,128)(2,1)S(1)}, bf16[64,2048]{1,0:T(8,128)(2,1)S(1)}, bf16[128,2048]{1,0:T(8,128)(2,1)S(1)}, bf16[128,768]{1,0:T(8,128)(2,1)...) custom-call(bf16[128,2048]{1,0:T(8,128)(2,1)S(1)} %get-tuple-element.106.refs_0_.refs_2_, ...), custom_call_target="tpu_custom_call" | custom-call | flops 2000000 | bytes 200 | tf_op jit(solution)/shard_map/forward/pallas_call | solution.py:182
  8.3 2.9 %collective-permute-start = (bf16[64,2048]{1,0:T(8,128)(2,1)S(1)}, bf16[64,2048]{1,0:T(8,128)(2,1)S(1)}, u32[]{:S(2)}, u32[]{:S(2)}) collective-permute-start(bf16[64,2048]{1,0:T(8,128)(2,1)S(1)} %get-tuple-element.111), channel_id=1, source_target_pairs={{0,1},{1,0},{2,3},{3,2},{4,5},{5,4},{6,7},{7,6},{8,9},{9,8},{10,11... | collective-permute-start | bytes 786440 | tf_op jit(solution)/shard_map/ppermute | solution.py:505
  11.3 1.1 %collective-permute-done.refs_0_.refs_1_ = bf16[64,2048]{1,0:T(8,128)(2,1)S(1)} collective-permute-done((bf16[64,2048]{1,0:T(8,128)(2,1)S(1)}, bf16[64,2048]{1,0:T(8,128)(2,1)S(1)}, u32[]{:S(2)}, u32[]{:S(2)}) %collective-permute-start) | collective-permute-done | bytes 262176 | tf_op jit(solution)/shard_map/ppermute | solution.py:505
  12.7 1.6 %forward.4 = (bf16[128,2048]{1,0:T(8,128)(2,1)S(1)}, bf16[128,2048]{1,0:T(8,128)(2,1)S(1)}, bf16[128,768]{1,0:T(8,128)(2,1)S(1)}, f32[2,128,128]{2,1,0:T(8,128)S...) custom-call(bf16[64,2048]{1,0:T(8,128)(2,1)S(1)} %collective-permute-done.refs_0_.refs_1_, ...), custom_call_target="tpu_custom_call" | custom-call | flops 2000000 | bytes 200 | tf_op jit(solution)/shard_map/forward/pallas_call | solution.py:182
  14.4 2.9 %prepare.1 = (bf16[768,2048]{1,0:T(8,128)(2,1)S(1)}, bf16[2048,256]{1,0:T(8,128)(2,1)S(1)}, f32[1,768]{1,0:T(1,128)S(1)}, bf16[128,2048]{1,0:T(8,128)(2,1)S(1)},...) custom-call(bf16[1,2048]{1,0:T(2,128)(2,1)S(1)} %get-tuple-element.107.refs_1_.refs_2_.ref, ...), custom_call_target="tpu_custom_call" | custom-call | flops 2000000 | bytes 200 | tf_op jit(solution)/shard_map/prepare/pallas_call | solution.py:182
  17.4 6.7 %collective-permute-done.3.refs_0_.refs_2_ = bf16[128,2048]{1,0:T(8,128)(2,1)S(1)} collective-permute-done((bf16[128,2048]{1,0:T(8,128)(2,1)S(1)}, bf16[128,2048]{1,0:T(8,128)(2,1)S(1)}, u32[]{:S(2)}, u32[]{:S(2)}) %collective-permute-start.3) | collective-permute-done | bytes 524320 | tf_op jit(solution)/shard_map/ppermute | solution.py:508
  24.0 1.6 %forward.5 = (bf16[64,2048]{1,0:T(8,128)(2,1)S(1)}, bf16[64,2048]{1,0:T(8,128)(2,1)S(1)}, bf16[128,2048]{1,0:T(8,128)(2,1)S(1)}, bf16[128,768]{1,0:T(8,128)(2,1)...) custom-call(bf16[128,2048]{1,0:T(8,128)(2,1)S(1)} %collective-permute-done.3.refs_0_.refs_2_,, ...), custom_call_target="tpu_custom_call" | custom-call | flops 8000000000 | bytes 800000 | tf_op jit(solution)/shard_map/forward/pallas_call | solution.py:182
  25.7 0.5 collective-permute-start.5
  26.2 4.2 %collective-permute-done.2.refs_0_.refs_19_ = bf16[128,2048]{1,0:T(8,128)(2,1)S(1)} collective-permute-done((bf16[128,2048]{1,0:T(8,128)(2,1)S(1)}, bf16[128,2048]{1,0:T(8,128)(2,1)S(1)}, u32[]{:S(2)}, u32[]{:S(2)}) %collective-permute-start.2) | collective-permute-done | bytes 524320 | tf_op jit(solution)/shard_map/ppermute | solution.py:508
  30.4 2.4 %turn.2 = (bf16[128,2048]{1,0:T(8,128)(2,1)S(1)}, bf16[128,2048]{1,0:T(8,128)(2,1)S(1)}, bf16[128,768]{1,0:T(8,128)(2,1)S(1)}, bf16[128,256]{1,0:T(8,128)(2,1)S(1)}, f32[8,2048]{1,0:T(8,128)S(1)}) custom-call(bf16[128,2048]{1,0:T(8,128)(2,1)S(1)} %collective-permute-done.2.refs_0_.refs_19_, bf16[128,2048]{1,0:T(8,128)(2,1)S(1)} %get-tuple-element.123.refs_1_.refs_3_, ...), custom_call_target="tpu_custom_call" | custom-call | flops 2000000 | bytes 200 | tf_op jit(solution)/shard_map/turn/pallas_call | solution.py:182
  32.9 1.8 %collective-permute-start.9 = (bf16[128,2048]{1,0:T(8,128)(2,1)S(1)}, bf16[128,2048]{1,0:T(8,128)(2,1)S(1)}, u32[]{:S(2)}, u32[]{:S(2)}) collective-permute-start(bf16[128,2048]{1,0:T(8,128)(2,1)S(1)} %get-tuple-element.160), channel_id=1, source_target_pairs={{0,15},{1,2},{2,1},{3,4},{4,3},{5,6},{6,5},{7,8},{8,7},{9,10},{10,... | collective-permute-start | bytes 1572872 | tf_op jit(solution)/shard_map/ppermute | solution.py:508
  34.7 2.5 %turn.3 = (bf16[64,2048]{1,0:T(8,128)(2,1)S(1)}, bf16[64,2048]{1,0:T(8,128)(2,1)S(1)}, bf16[128,2048]{1,0:T(8,128)(2,1)S(1)}, bf16[128,768]{1,0:T(8,128)(2,1)S(1...) custom-call(bf16[64,2048]{1,0:T(8,128)(2,1)S(1)} %collective-permute-done.4.refs_0_.refs_16_, ...), custom_call_target="tpu_custom_call" | custom-call | flops 2000000 | bytes 200 | tf_op jit(solution)/shard_map/turn/pallas_call | solution.py:182
  37.7 1.0 %collective-permute-done.6.refs_0_.refs_13_ = bf16[64,2048]{1,0:T(8,128)(2,1)S(1)} collective-permute-done((bf16[64,2048]{1,0:T(8,128)(2,1)S(1)}, bf16[64,2048]{1,0:T(8,128)(2,1)S(1)}, u32[]{:S(2)}, u32[]{:S(2)}) %collective-permute-start.6) | collective-permute-done | bytes 262176 | tf_op jit(solution)/shard_map/ppermute | solution.py:505
  39.1 1.9 %backward.3 = (bf16[128,2048]{1,0:T(8,128)(2,1)S(1)}, bf16[128,768]{1,0:T(8,128)(2,1)S(1)}, f32[8,2048]{1,0:T(8,128)S(1)}) custom-call(bf16[64,2048]{1,0:T(8,128)(2,1)S(1)} %collective-permute-done.6.refs_0_.refs_13_, bf16[64,2048]{1,0:T(8,128)(2,1)S(1)} %collective-permute-done.7.refs_1_.refs_14_, ...), custom_call_target="tpu_custom_call" | custom-call | flops 2000000 | bytes 200 | tf_op jit(solution)/shard_map/backward/pallas_call | solution.py:182
  41.2 3.4 %early_weights.1 = (bf16[1,128,2048]{2,1,0:T(8,128)(2,1)}, bf16[1,128,2048]{2,1,0:T(8,128)(2,1)}, f32[8,2048]{1,0:T(8,128)S(1)}, f32[256,2048]{1,0:T(8,128)S(1)}, f32[2048,768]{1,0:T(8,128)S(1)}) custom-call(bf16[128,2048]{1,0:T(8,128)(2,1)S(1)} %get-tuple-element.126.refs_0_, bf16[128,768]{1,0:T(8,128)(2,1)S(1)} %get-tuple-element.127.refs_1_, ...), custom_call_target="tpu_custom_call" | custom-call | flops 2000000 | bytes 200 | tf_op jit(solution)/shard_map/early_weights/pallas_call | solution.py:182
  44.6 5.1 %collective-permute-done.9.refs_0_.refs_3_ = bf16[128,2048]{1,0:T(8,128)(2,1)S(1)} collective-permute-done((bf16[128,2048]{1,0:T(8,128)(2,1)S(1)}, bf16[128,2048]{1,0:T(8,128)(2,1)S(1)}, u32[]{:S(2)}, u32[]{:S(2)}) %collective-permute-start.9) | collective-permute-done | bytes 524320 | tf_op jit(solution)/shard_map/ppermute | solution.py:508
  49.7 1.7 %backward.4 = (bf16[64,2048]{1,0:T(8,128)(2,1)S(1)}, bf16[64,2048]{1,0:T(8,128)(2,1)S(1)}, bf16[128,768]{1,0:T(8,128)(2,1)S(1)}, f32[8,2048]{1,0:T(8,128)S(1)}) custom-call(bf16[128,2048]{1,0:T(8,128)(2,1)S(1)} %collective-permute-done.9.refs_0_.refs_3_, bf16[64,2048]{1,0:T(8,128)(2,1)S(1)} %collective-permute-done.refs_0_.refs_1_, ...), custom_call_target="tpu_custom_call" | custom-call | flops 2000000 | bytes 200 | tf_op jit(solution)/shard_map/backward/pallas_call | solution.py:182
  51.5 0.5 collective-permute-start.11
  52.0 1.3 %more_weights.1 = (f32[8,2048]{1,0:T(8,128)S(1)}, f32[256,2048]{1,0:T(8,128)S(1)}, f32[2048,768]{1,0:T(8,128)S(1)}) custom-call(bf16[128,2048]{1,0:T(8,128)(2,1)S(1)} %get-tuple-element.171.refs_0_, bf16[128,768]{1,0:T(8,128)(2,1)S(1)} %get-tuple-element.172.refs_1_, bf16[128,256]{1,0:T(8,128)(2,1)S(1)} %get-tuple-element.173.refs_2_, ...), custom_call_target="tpu_custom_call" | custom-call | flops 2000000 | bytes 200 | tf_op jit(solution)/shard_map/more_weights/pallas_call | solution.py:182
  53.4 1.7 %backward.5 = (bf16[128,2048]{1,0:T(8,128)(2,1)S(1)}, bf16[128,768]{1,0:T(8,128)(2,1)S(1)}, f32[8,2048]{1,0:T(8,128)S(1)}) custom-call(bf16[64,2048]{1,0:T(8,128)(2,1)S(1)} %collective-permute-done.10.refs_0_.refs_15_, bf16[64,2048]{1,0:T(8,128)(2,1)S(1)} %collective-permute-done.11.refs_1_.refs_16_, ...), custom_call_target="tpu_custom_call" | custom-call | flops 2000000 | bytes 200 | tf_op jit(solution)/shard_map/backward/pallas_call | solution.py:182
  55.1 2.2 %collective-permute-done.8.refs_0_ = bf16[128,2048]{1,0:T(8,128)(2,1)S(1)} collective-permute-done((bf16[128,2048]{1,0:T(8,128)(2,1)S(1)}, bf16[128,2048]{1,0:T(8,128)(2,1)S(1)}, u32[]{:S(2)}, u32[]{:S(2)}) %collective-permute-start.8) | collective-permute-done | bytes 524320 | tf_op jit(solution)/shard_map/ppermute | solution.py:508
  57.4 3.8 %finish.1 = (bf16[1,128,2048]{2,1,0:T(8,128)(2,1)}, bf16[1,128,2048]{2,1,0:T(8,128)(2,1)}, bf16[1,2048]{1,0:T(2,128)(2,1)}, bf16[1,256,2048]{2,1,0:T(8,128)(2,1)}, bf16[1,2048,768]{2,1,0:T(8,128)(2,1)}) custom-call(bf16[128,2048]{1,0:T(8,128)(2,1)S(1)} %collective-permute-done.8.refs_0_, bf16[128,2048]{1,0:T(8,128)(2,1)S(1)} %get-tuple-element.185.refs_1_, ...), custom_call_target="tpu_custom_call" | custom-call | flops 2000000 | bytes 200 | tf_op jit(solution)/shard_map/finish/pallas_call | solution.py:182
  (13 shorter events, 1.8 us)
Async XLA Ops:
  4.0 20.1 %collective-permute-start.3 = (bf16[128,2048]{1,0:T(8,128)(2,1)S(1)}, bf16[128,2048]{1,0:T(8,128)(2,1)S(1)}, u32[]{:S(2)}, u32[]{:S(2)}) collective-permute-start(bf16[128,2048]{1,0:T(8,128)(2,1)S(1)} %get-tuple-element.117), channel_id=1, source_target_pairs={{0,15},{1,2},{2,1},{3,4},{4,3},{5,6},{6,5},{7,8},{8,7},{9,10},{10,... | collective-permute-start | bytes 1572872 | tf_op jit(solution)/shard_map/ppermute | solution.py:508
  8.3 4.1 %collective-permute-start = (bf16[64,2048]{1,0:T(8,128)(2,1)S(1)}, bf16[64,2048]{1,0:T(8,128)(2,1)S(1)}, u32[]{:S(2)}, u32[]{:S(2)}) collective-permute-start(bf16[64,2048]{1,0:T(8,128)(2,1)S(1)} %get-tuple-element.111), channel_id=1, source_target_pairs={{0,1},{1,0},{2,3},{3,2},{4,5},{5,4},{6,7},{7,6},{8,9},{9,8},{10,11... | collective-permute-start | bytes 786440 | tf_op jit(solution)/shard_map/ppermute | solution.py:505
  11.2 1.5 %collective-permute-start.1 = (bf16[64,2048]{1,0:T(8,128)(2,1)S(1)}, bf16[64,2048]{1,0:T(8,128)(2,1)S(1)}, u32[]{:S(2)}, u32[]{:S(2)}) collective-permute-start(bf16[64,2048]{1,0:T(8,128)(2,1)S(1)} %get-tuple-element.112), channel_id=1, source_target_pairs={{0,1},{1,0},{2,3},{3,2},{4,5},{5,4},{6,7},{7,6},{8,9},{9,8},{10,11... | collective-permute-start | bytes 786440 | tf_op jit(solution)/shard_map/ppermute | solution.py:505
  14.3 16.1 %collective-permute-start.2 = (bf16[128,2048]{1,0:T(8,128)(2,1)S(1)}, bf16[128,2048]{1,0:T(8,128)(2,1)S(1)}, u32[]{:S(2)}, u32[]{:S(2)}) collective-permute-start(bf16[128,2048]{1,0:T(8,128)(2,1)S(1)} %get-tuple-element.116), channel_id=1, source_target_pairs={{0,15},{1,2},{2,1},{3,4},{4,3},{5,6},{6,5},{7,8},{8,7},{9,10},{10,... | collective-permute-start | bytes 1572872 | tf_op jit(solution)/shard_map/ppermute | solution.py:508
  25.6 7.2 %collective-permute-start.4 = (bf16[64,2048]{1,0:T(8,128)(2,1)S(1)}, bf16[64,2048]{1,0:T(8,128)(2,1)S(1)}, u32[]{:S(2)}, u32[]{:S(2)}) collective-permute-start(bf16[64,2048]{1,0:T(8,128)(2,1)S(1)} %get-tuple-element.130), channel_id=1, source_target_pairs={{0,1},{1,0},{2,3},{3,2},{4,5},{5,4},{6,7},{7,6},{8,9},{9,8},{10,11... | collective-permute-start | bytes 786440 | tf_op jit(solution)/shard_map/ppermute | solution.py:505
  25.7 7.2 %collective-permute-start.5 = (bf16[64,2048]{1,0:T(8,128)(2,1)S(1)}, bf16[64,2048]{1,0:T(8,128)(2,1)S(1)}, u32[]{:S(2)}, u32[]{:S(2)}) collective-permute-start(bf16[64,2048]{1,0:T(8,128)(2,1)S(1)} %get-tuple-element.131), channel_id=1, source_target_pairs={{0,1},{1,0},{2,3},{3,2},{4,5},{5,4},{6,7},{7,6},{8,9},{9,8},{10,11... | collective-permute-start | bytes 786440 | tf_op jit(solution)/shard_map/ppermute | solution.py:505
  32.9 16.9 %collective-permute-start.9 = (bf16[128,2048]{1,0:T(8,128)(2,1)S(1)}, bf16[128,2048]{1,0:T(8,128)(2,1)S(1)}, u32[]{:S(2)}, u32[]{:S(2)}) collective-permute-start(bf16[128,2048]{1,0:T(8,128)(2,1)S(1)} %get-tuple-element.160), channel_id=1, source_target_pairs={{0,15},{1,2},{2,1},{3,4},{4,3},{5,6},{6,5},{7,8},{8,7},{9,10},{10,... | collective-permute-start | bytes 1572872 | tf_op jit(solution)/shard_map/ppermute | solution.py:508
  37.2 1.6 %collective-permute-start.6 = (bf16[64,2048]{1,0:T(8,128)(2,1)S(1)}, bf16[64,2048]{1,0:T(8,128)(2,1)S(1)}, u32[]{:S(2)}, u32[]{:S(2)}) collective-permute-start(bf16[64,2048]{1,0:T(8,128)(2,1)S(1)} %get-tuple-element.141), channel_id=1, source_target_pairs={{0,1},{1,0},{2,3},{3,2},{4,5},{5,4},{6,7},{7,6},{8,9},{9,8},{10,11... | collective-permute-start | bytes 786440 | tf_op jit(solution)/shard_map/ppermute | solution.py:505
  37.2 1.9 %collective-permute-start.7 = (bf16[64,2048]{1,0:T(8,128)(2,1)S(1)}, bf16[64,2048]{1,0:T(8,128)(2,1)S(1)}, u32[]{:S(2)}, u32[]{:S(2)}) collective-permute-start(bf16[64,2048]{1,0:T(8,128)(2,1)S(1)} %get-tuple-element.142), channel_id=1, source_target_pairs={{0,1},{1,0},{2,3},{3,2},{4,5},{5,4},{6,7},{7,6},{8,9},{9,8},{10,11... | collective-permute-start | bytes 786440 | tf_op jit(solution)/shard_map/ppermute | solution.py:505
  41.1 16.3 %collective-permute-start.8 = (bf16[128,2048]{1,0:T(8,128)(2,1)S(1)}, bf16[128,2048]{1,0:T(8,128)(2,1)S(1)}, u32[]{:S(2)}, u32[]{:S(2)}) collective-permute-start(bf16[128,2048]{1,0:T(8,128)(2,1)S(1)} %get-tuple-element.159), channel_id=1, source_target_pairs={{0,15},{1,2},{2,1},{3,4},{4,3},{5,6},{6,5},{7,8},{8,7},{9,10},{10,... | collective-permute-start | bytes 1572872 | tf_op jit(solution)/shard_map/ppermute | solution.py:508
  51.4 1.9 %collective-permute-start.10 = (bf16[64,2048]{1,0:T(8,128)(2,1)S(1)}, bf16[64,2048]{1,0:T(8,128)(2,1)S(1)}, u32[]{:S(2)}, u32[]{:S(2)}) collective-permute-start(bf16[64,2048]{1,0:T(8,128)(2,1)S(1)} %get-tuple-element.165), channel_id=1, source_target_pairs={{0,1},{1,0},{2,3},{3,2},{4,5},{5,4},{6,7},{7,6},{8,9},{9,8},{10,11... | collective-permute-start | bytes 786440 | tf_op jit(solution)/shard_map/ppermute | solution.py:505
  51.5 1.9 %collective-permute-start.11 = (bf16[64,2048]{1,0:T(8,128)(2,1)S(1)}, bf16[64,2048]{1,0:T(8,128)(2,1)S(1)}, u32[]{:S(2)}, u32[]{:S(2)}) collective-permute-start(bf16[64,2048]{1,0:T(8,128)(2,1)S(1)} %get-tuple-element.166), channel_id=1, source_target_pairs={{0,1},{1,0},{2,3},{3,2},{4,5},{5,4},{6,7},{7,6},{8,9},{9,8},{10,11... | collective-permute-start | bytes 786440 | tf_op jit(solution)/shard_map/ppermute | solution.py:505

commit v7 on v6

--- a/solution.py
+++ b/solution.py
@@ -64,16 +64,23 @@
         u_ref[part, :] = (centred * rstd * gain).astype(BF16)
         st_ref[part, :] = jnp.concatenate(
             [jnp.broadcast_to(mean, (CHUNK, 128)), jnp.broadcast_to(rstd, (CHUNK, 128))], axis=1)
-    for n in range(3):
-        if waits:
+    if waits:
+        total = None
+        depth = width // (len(waits) - 1)
+        for n in range(len(waits) - 1):
             waits[n].wait()
-        qkv_ref[:, n * hd:(n + 1) * hd] = dot(u_ref[...], wq_ref[:, n * hd:(n + 1) * hd]).astype(BF16)
+            at = n * depth
+            part = dot(u_ref[:, at:at + depth], wq_ref[at:at + depth, :])
+            total = part if total is None else total + part
+        qkv_ref[...] = total.astype(BF16)
+    else:
+        for n in range(3):
+            qkv_ref[:, n * hd:(n + 1) * hd] = dot(u_ref[...], wq_ref[:, n * hd:(n + 1) * hd]).astype(BF16)
     keep = mask_ref[...]
     heads = [pl.ds(head * HEAD_DIM, HEAD_DIM) for head in range(HEADS_DEV)]
     scores = [dot(qkv_ref[:, cols], qkv_ref[:, pl.ds(hd + cols.start, HEAD_DIM)], NT) for cols in heads]
     weighted = [jnp.where(keep > 0.0, jnp.exp(score * SCALE), 0.0) for score in scores]
-    inverse = [1.0 / jnp.sum(value, axis=-1, keepdims=True) for value in weighted]
-    probs = [value * scale for value, scale in zip(weighted, inverse)]
+    probs = [value / jnp.sum(value, axis=-1, keepdims=True) for value in weighted]
     mixed = [
         dot(value.astype(BF16), qkv_ref[:, pl.ds(2 * hd + cols.start, HEAD_DIM)]) for value, cols in zip(probs, heads)
     ]
@@ -95,7 +102,7 @@
 def forward_body(h, gain_ref, wq_ref, wo_ref, mask_ref, out, u_ref, qkv_ref, p_ref, att_ref, st_ref, waits=None):
     attend(h, gain_ref, wq_ref, mask_ref, u_ref, qkv_ref, p_ref, att_ref, st_ref, waits)
     if waits:
-        waits[3].wait()
+        waits[-1].wait()
     project_out(h, att_ref, wo_ref, out)
 
 
@@ -236,8 +243,8 @@
         offs_copy = pick(offs_hbm, offs_ref, 2)
         gain_copy = pick(gain_hbm, gain_ref, 3)
         wo_copy = pick(wo_hbm.at[0], wo_ref, 4)
-        cols = [pl.ds(n * hd, hd) for n in range(3)]
-        wq_copies = [pick(wq_hbm.at[0, :, cols[n]], wq_ref.at[:, cols[n]], 5 + n) for n in range(3)]
+        spans = [pl.ds(n * (width // 4), width // 4) for n in range(4)]
+        wq_copies = [pick(wq_hbm.at[0, span], wq_ref.at[span], 5 + n) for n, span in enumerate(spans)]
         a_start()
         gain_copy.start()
         offs_copy.start()
@@ -258,7 +265,7 @@
             stream(rows, width, 1), stream(rows, width, 1), Mem(gain.shape, BF16), Mem(wq.shape[1:], BF16),
             Mem(wo.shape[1:], BF16), Mem((rows, rows), F32), stream(rows, width, parts), saved_outs(rows, width),
         ],
-        [pltpu.SMEM(offs.shape, jnp.int32), pltpu.SemaphoreType.DMA((8,))],
+        [pltpu.SMEM(offs.shape, jnp.int32), pltpu.SemaphoreType.DMA((9,))],
     )
 
 
@@ -519,7 +526,7 @@
     b2_out, b1_saved = forward_kernel(after(b1, b0_saved[4]), fixed, mask, 1)
     b2 = swap_far(b2_out)
     *turned, cot_a, cot_b, datt_a, datt_b = prepare_kernel(gain, wq, wo, b1_saved[4], cotangent_down, cotangent_up)
-    a2_out, a1_saved = forward_kernel(after(a1, turned[2]), fixed, mask, NEAR_PARTS, us=8)
+    a2_out, a1_saved = forward_kernel(after(a1, turned[2]), fixed, mask, 1, us=8)
     a2 = swap_near(a2_out)
     eb2, use_b2 = turn_kernel(after(b2, a1_saved[4]), cot_b, datt_b, fixed, mask, turned, 1)
     cb1 = swap_far(eb2)

time: 61.5 us -> 61.2 us (level)
    ppermute x8 -> x7, starting transfers between devices: 4.72 us -> 4.22 us  [swap_near(): return [lax.ppermute(part, 'section', near) for part in x]]
    ppermute x8 -> x7, waiting for transfers between devices: 2.93 us -> 2.93 us  [swap_near(): return [lax.ppermute(part, 'section', near) for part in x]]
  transfers between devices with their start and end apart: 12 -> 11, of which waited for: 9 -> 9; matrix products, arithmetic and copies ran while one was open for 0% -> 0% of each run, Pallas kernels for 37% -> 37%
where the time goes in v7:
time: 61.2 us; the launch traced here: 61.1 us
  Pallas kernels  29.6 us (48%)
  waiting for transfers between devices  21.7 us (35%)
  starting transfers between devices  8.88 us (15%)
  between operations  0.92 us (2%)
    pallas_call x13, Pallas kernels, call(): pl.pallas_call(kernel, in_specs=[far if isinstance(x, Far) else VM for x...  29.6 us
    ppermute x4, waiting for transfers between devices, swap_far(): return [lax.ppermute(part, 'section', far) for part in x]  18.8 us
    ppermute x4, starting transfers between devices, swap_far(): return [lax.ppermute(part, 'section', far) for part in x]  4.67 us
    ppermute x7, starting transfers between devices, swap_near(): return [lax.ppermute(part, 'section', near) for part in x]  4.22 us
    ppermute x7, waiting for transfers between devices, swap_near(): return [lax.ppermute(part, 'section', near) for part in x]  2.93 us
  transfers between devices with their start and end apart: 11, of which 9 were waited for; matrix products, arithmetic and copies ran while one was open for 0% of the time, Pallas kernels for 37%

profile of v7, /device:TPU:1, one launch (start us, length us, event | category | flops | bytes accessed | tf_op | source)
XLA Modules:
  0.0 61.1 jit_solution(3747524893105283876)
XLA Ops:
  0.6 3.2 %first.1 = (bf16[128,2048]{1,0:T(8,128)(2,1)S(1)}, bf16[128,2048]{1,0:T(8,128)(2,1)S(1)}, bf16[1,2048]{1,0:T(2,128)(2,1)S(1)}, bf16[2048,768]{1,0:T(8,128)(2,1)S...) custom-call(s32[2,4]{1,0:T(2,128)} %bitcast.1, ...), custom_call_target="tpu_custom_call" | custom-call | flops 2000000 | bytes 200 | tf_op jit(solution)/shard_map/first/pallas_call | solution.py:189
  3.8 2.7 %collective-permute-start.3 = (bf16[128,2048]{1,0:T(8,128)(2,1)S(1)}, bf16[128,2048]{1,0:T(8,128)(2,1)S(1)}, u32[]{:S(2)}, u32[]{:S(2)}) collective-permute-start(bf16[128,2048]{1,0:T(8,128)(2,1)S(1)} %get-tuple-element.115), channel_id=1, source_target_pairs={{0,15},{1,2},{2,1},{3,4},{4,3},{5,6},{6,5},{7,8},{8,7},{9,10},{10,... | collective-permute-start | bytes 1572872 | tf_op jit(solution)/shard_map/ppermute | solution.py:515
  6.5 1.6 %forward.3 = (bf16[64,2048]{1,0:T(8,128)(2,1)S(1)}, bf16[64,2048]{1,0:T(8,128)(2,1)S(1)}, bf16[128,2048]{1,0:T(8,128)(2,1)S(1)}, bf16[128,768]{1,0:T(8,128)(2,1)...) custom-call(bf16[128,2048]{1,0:T(8,128)(2,1)S(1)} %get-tuple-element.104.refs_0_.refs_2_, ...), custom_call_target="tpu_custom_call" | custom-call | flops 2000000 | bytes 200 | tf_op jit(solution)/shard_map/forward/pallas_call | solution.py:189
  8.1 2.9 %collective-permute-start = (bf16[64,2048]{1,0:T(8,128)(2,1)S(1)}, bf16[64,2048]{1,0:T(8,128)(2,1)S(1)}, u32[]{:S(2)}, u32[]{:S(2)}) collective-permute-start(bf16[64,2048]{1,0:T(8,128)(2,1)S(1)} %get-tuple-element.109), channel_id=1, source_target_pairs={{0,1},{1,0},{2,3},{3,2},{4,5},{5,4},{6,7},{7,6},{8,9},{9,8},{10,11... | collective-permute-start | bytes 786440 | tf_op jit(solution)/shard_map/ppermute | solution.py:512
  11.1 1.1 %collective-permute-done.refs_0_.refs_1_ = bf16[64,2048]{1,0:T(8,128)(2,1)S(1)} collective-permute-done((bf16[64,2048]{1,0:T(8,128)(2,1)S(1)}, bf16[64,2048]{1,0:T(8,128)(2,1)S(1)}, u32[]{:S(2)}, u32[]{:S(2)}) %collective-permute-start) | collective-permute-done | bytes 262176 | tf_op jit(solution)/shard_map/ppermute | solution.py:512
  12.6 1.6 %forward.4 = (bf16[128,2048]{1,0:T(8,128)(2,1)S(1)}, bf16[128,2048]{1,0:T(8,128)(2,1)S(1)}, bf16[128,768]{1,0:T(8,128)(2,1)S(1)}, f32[2,128,128]{2,1,0:T(8,128)S...) custom-call(bf16[64,2048]{1,0:T(8,128)(2,1)S(1)} %collective-permute-done.refs_0_.refs_1_, ...), custom_call_target="tpu_custom_call" | custom-call | flops 2000000 | bytes 200 | tf_op jit(solution)/shard_map/forward/pallas_call | solution.py:189
  14.2 2.9 %prepare.1 = (bf16[768,2048]{1,0:T(8,128)(2,1)S(1)}, bf16[2048,256]{1,0:T(8,128)(2,1)S(1)}, f32[1,768]{1,0:T(1,128)S(1)}, bf16[128,2048]{1,0:T(8,128)(2,1)S(1)},...) custom-call(bf16[1,2048]{1,0:T(2,128)(2,1)S(1)} %get-tuple-element.105.refs_1_.refs_2_.ref, ...), custom_call_target="tpu_custom_call" | custom-call | flops 2000000 | bytes 200 | tf_op jit(solution)/shard_map/prepare/pallas_call | solution.py:189
  17.2 6.7 %collective-permute-done.3.refs_0_.refs_2_ = bf16[128,2048]{1,0:T(8,128)(2,1)S(1)} collective-permute-done((bf16[128,2048]{1,0:T(8,128)(2,1)S(1)}, bf16[128,2048]{1,0:T(8,128)(2,1)S(1)}, u32[]{:S(2)}, u32[]{:S(2)}) %collective-permute-start.3) | collective-permute-done | bytes 524320 | tf_op jit(solution)/shard_map/ppermute | solution.py:515
  23.9 1.6 %forward.5 = (bf16[128,2048]{1,0:T(8,128)(2,1)S(1)}, bf16[128,2048]{1,0:T(8,128)(2,1)S(1)}, bf16[128,768]{1,0:T(8,128)(2,1)S(1)}, f32[2,128,128]{2,1,0:T(8,128)S...) custom-call(bf16[128,2048]{1,0:T(8,128)(2,1)S(1)} %collective-permute-done.3.refs_0_.refs_2_, ...), custom_call_target="tpu_custom_call" | custom-call | flops 8000000000 | bytes 800000 | tf_op jit(solution)/shard_map/forward/pallas_call | solution.py:189
  25.5 4.7 %collective-permute-done.2.refs_0_.refs_18_ = bf16[128,2048]{1,0:T(8,128)(2,1)S(1)} collective-permute-done((bf16[128,2048]{1,0:T(8,128)(2,1)S(1)}, bf16[128,2048]{1,0:T(8,128)(2,1)S(1)}, u32[]{:S(2)}, u32[]{:S(2)}) %collective-permute-start.2) | collective-permute-done | bytes 524320 | tf_op jit(solution)/shard_map/ppermute | solution.py:515
  30.2 2.5 %turn.2 = (bf16[128,2048]{1,0:T(8,128)(2,1)S(1)}, bf16[128,2048]{1,0:T(8,128)(2,1)S(1)}, bf16[128,768]{1,0:T(8,128)(2,1)S(1)}, bf16[128,256]{1,0:T(8,128)(2,1)S(1)}, f32[8,2048]{1,0:T(8,128)S(1)}) custom-call(bf16[128,2048]{1,0:T(8,128)(2,1)S(1)} %collective-permute-done.2.refs_0_.refs_18_, bf16[128,2048]{1,0:T(8,128)(2,1)S(1)} %get-tuple-element.121.refs_1_.refs_3_, ...), custom_call_target="tpu_custom_call" | custom-call | flops 2000000 | bytes 200 | tf_op jit(solution)/shard_map/turn/pallas_call | solution.py:189
  32.7 1.8 %collective-permute-start.8 = (bf16[128,2048]{1,0:T(8,128)(2,1)S(1)}, bf16[128,2048]{1,0:T(8,128)(2,1)S(1)}, u32[]{:S(2)}, u32[]{:S(2)}) collective-permute-start(bf16[128,2048]{1,0:T(8,128)(2,1)S(1)} %get-tuple-element.156), channel_id=1, source_target_pairs={{0,15},{1,2},{2,1},{3,4},{4,3},{5,6},{6,5},{7,8},{8,7},{9,10},{10,... | collective-permute-start | bytes 1572872 | tf_op jit(solution)/shard_map/ppermute | solution.py:515
  34.5 2.4 %turn.3 = (bf16[64,2048]{1,0:T(8,128)(2,1)S(1)}, bf16[64,2048]{1,0:T(8,128)(2,1)S(1)}, bf16[128,2048]{1,0:T(8,128)(2,1)S(1)}, bf16[128,768]{1,0:T(8,128)(2,1)S(1...) custom-call(bf16[128,2048]{1,0:T(8,128)(2,1)S(1)} %collective-permute-done.4.refs_0_.refs_16_, ...), custom_call_target="tpu_custom_call" | custom-call | flops 2000000 | bytes 200 | tf_op jit(solution)/shard_map/turn/pallas_call | solution.py:189
  37.0 0.5 collective-permute-start.6
  37.5 1.0 %collective-permute-done.5.refs_0_.refs_13_ = bf16[64,2048]{1,0:T(8,128)(2,1)S(1)} collective-permute-done((bf16[64,2048]{1,0:T(8,128)(2,1)S(1)}, bf16[64,2048]{1,0:T(8,128)(2,1)S(1)}, u32[]{:S(2)}, u32[]{:S(2)}) %collective-permute-start.5) | collective-permute-done | bytes 262176 | tf_op jit(solution)/shard_map/ppermute | solution.py:512
  38.9 1.9 %backward.3 = (bf16[128,2048]{1,0:T(8,128)(2,1)S(1)}, bf16[128,768]{1,0:T(8,128)(2,1)S(1)}, f32[8,2048]{1,0:T(8,128)S(1)}) custom-call(bf16[64,2048]{1,0:T(8,128)(2,1)S(1)} %collective-permute-done.5.refs_0_.refs_13_, bf16[64,2048]{1,0:T(8,128)(2,1)S(1)} %collective-permute-done.6.refs_1_.refs_14_, ...), custom_call_target="tpu_custom_call" | custom-call | flops 2000000 | bytes 200 | tf_op jit(solution)/shard_map/backward/pallas_call | solution.py:189
  40.9 3.4 %early_weights.1 = (bf16[1,128,2048]{2,1,0:T(8,128)(2,1)}, bf16[1,128,2048]{2,1,0:T(8,128)(2,1)}, f32[8,2048]{1,0:T(8,128)S(1)}, f32[256,2048]{1,0:T(8,128)S(1)}, f32[2048,768]{1,0:T(8,128)S(1)}) custom-call(bf16[128,2048]{1,0:T(8,128)(2,1)S(1)} %get-tuple-element.124.refs_0_, bf16[128,768]{1,0:T(8,128)(2,1)S(1)} %get-tuple-element.125.refs_1_, ...), custom_call_target="tpu_custom_call" | custom-call | flops 2000000 | bytes 200 | tf_op jit(solution)/shard_map/early_weights/pallas_call | solution.py:189
  44.4 5.1 %collective-permute-done.8.refs_0_.refs_3_ = bf16[128,2048]{1,0:T(8,128)(2,1)S(1)} collective-permute-done((bf16[128,2048]{1,0:T(8,128)(2,1)S(1)}, bf16[128,2048]{1,0:T(8,128)(2,1)S(1)}, u32[]{:S(2)}, u32[]{:S(2)}) %collective-permute-start.8) | collective-permute-done | bytes 524320 | tf_op jit(solution)/shard_map/ppermute | solution.py:515
  49.5 1.7 %backward.4 = (bf16[64,2048]{1,0:T(8,128)(2,1)S(1)}, bf16[64,2048]{1,0:T(8,128)(2,1)S(1)}, bf16[128,768]{1,0:T(8,128)(2,1)S(1)}, f32[8,2048]{1,0:T(8,128)S(1)}) custom-call(bf16[128,2048]{1,0:T(8,128)(2,1)S(1)} %collective-permute-done.8.refs_0_.refs_3_, bf16[64,2048]{1,0:T(8,128)(2,1)S(1)} %collective-permute-done.refs_0_.refs_1_, ...), custom_call_target="tpu_custom_call" | custom-call | flops 2000000 | bytes 200 | tf_op jit(solution)/shard_map/backward/pallas_call | solution.py:189
  51.3 0.5 collective-permute-start.10
  51.8 1.3 %more_weights.1 = (f32[8,2048]{1,0:T(8,128)S(1)}, f32[256,2048]{1,0:T(8,128)S(1)}, f32[2048,768]{1,0:T(8,128)S(1)}) custom-call(bf16[128,2048]{1,0:T(8,128)(2,1)S(1)} %get-tuple-element.167.refs_0_, bf16[128,768]{1,0:T(8,128)(2,1)S(1)} %get-tuple-element.168.refs_1_, bf16[128,256]{1,0:T(8,128)(2,1)S(1)} %get-tuple-element.169.refs_2_, ...), custom_call_target="tpu_custom_call" | custom-call | flops 2000000 | bytes 200 | tf_op jit(solution)/shard_map/more_weights/pallas_call | solution.py:189
  53.2 1.7 %backward.5 = (bf16[128,2048]{1,0:T(8,128)(2,1)S(1)}, bf16[128,768]{1,0:T(8,128)(2,1)S(1)}, f32[8,2048]{1,0:T(8,128)S(1)}) custom-call(bf16[64,2048]{1,0:T(8,128)(2,1)S(1)} %collective-permute-done.9.refs_0_.refs_15_, bf16[64,2048]{1,0:T(8,128)(2,1)S(1)} %collective-permute-done.10.refs_1_.refs_16_, ...), custom_call_target="tpu_custom_call" | custom-call | flops 2000000 | bytes 200 | tf_op jit(solution)/shard_map/backward/pallas_call | solution.py:189
  54.9 2.2 %collective-permute-done.7.refs_0_ = bf16[128,2048]{1,0:T(8,128)(2,1)S(1)} collective-permute-done((bf16[128,2048]{1,0:T(8,128)(2,1)S(1)}, bf16[128,2048]{1,0:T(8,128)(2,1)S(1)}, u32[]{:S(2)}, u32[]{:S(2)}) %collective-permute-start.7) | collective-permute-done | bytes 524320 | tf_op jit(solution)/shard_map/ppermute | solution.py:515
  57.1 3.8 %finish.1 = (bf16[1,128,2048]{2,1,0:T(8,128)(2,1)}, bf16[1,128,2048]{2,1,0:T(8,128)(2,1)}, bf16[1,2048]{1,0:T(2,128)(2,1)}, bf16[1,256,2048]{2,1,0:T(8,128)(2,1)}, bf16[1,2048,768]{2,1,0:T(8,128)(2,1)}) custom-call(bf16[128,2048]{1,0:T(8,128)(2,1)S(1)} %collective-permute-done.7.refs_0_, bf16[128,2048]{1,0:T(8,128)(2,1)S(1)} %get-tuple-element.181.refs_1_, ...), custom_call_target="tpu_custom_call" | custom-call | flops 2000000 | bytes 200 | tf_op jit(solution)/shard_map/finish/pallas_call | solution.py:189
  (11 shorter events, 1.3 us)
Async XLA Ops:
  3.8 20.1 %collective-permute-start.3 = (bf16[128,2048]{1,0:T(8,128)(2,1)S(1)}, bf16[128,2048]{1,0:T(8,128)(2,1)S(1)}, u32[]{:S(2)}, u32[]{:S(2)}) collective-permute-start(bf16[128,2048]{1,0:T(8,128)(2,1)S(1)} %get-tuple-element.115), channel_id=1, source_target_pairs={{0,15},{1,2},{2,1},{3,4},{4,3},{5,6},{6,5},{7,8},{8,7},{9,10},{10,... | collective-permute-start | bytes 1572872 | tf_op jit(solution)/shard_map/ppermute | solution.py:515
  8.1 4.1 %collective-permute-start = (bf16[64,2048]{1,0:T(8,128)(2,1)S(1)}, bf16[64,2048]{1,0:T(8,128)(2,1)S(1)}, u32[]{:S(2)}, u32[]{:S(2)}) collective-permute-start(bf16[64,2048]{1,0:T(8,128)(2,1)S(1)} %get-tuple-element.109), channel_id=1, source_target_pairs={{0,1},{1,0},{2,3},{3,2},{4,5},{5,4},{6,7},{7,6},{8,9},{9,8},{10,11... | collective-permute-start | bytes 786440 | tf_op jit(solution)/shard_map/ppermute | solution.py:512
  11.0 1.5 %collective-permute-start.1 = (bf16[64,2048]{1,0:T(8,128)(2,1)S(1)}, bf16[64,2048]{1,0:T(8,128)(2,1)S(1)}, u32[]{:S(2)}, u32[]{:S(2)}) collective-permute-start(bf16[64,2048]{1,0:T(8,128)(2,1)S(1)} %get-tuple-element.110), channel_id=1, source_target_pairs={{0,1},{1,0},{2,3},{3,2},{4,5},{5,4},{6,7},{7,6},{8,9},{9,8},{10,11... | collective-permute-start | bytes 786440 | tf_op jit(solution)/shard_map/ppermute | solution.py:512
  14.1 16.1 %collective-permute-start.2 = (bf16[128,2048]{1,0:T(8,128)(2,1)S(1)}, bf16[128,2048]{1,0:T(8,128)(2,1)S(1)}, u32[]{:S(2)}, u32[]{:S(2)}) collective-permute-start(bf16[128,2048]{1,0:T(8,128)(2,1)S(1)} %get-tuple-element.114), channel_id=1, source_target_pairs={{0,15},{1,2},{2,1},{3,4},{4,3},{5,6},{6,5},{7,8},{8,7},{9,10},{10,... | collective-permute-start | bytes 1572872 | tf_op jit(solution)/shard_map/ppermute | solution.py:515
  25.4 9.1 %collective-permute-start.4 = (bf16[128,2048]{1,0:T(8,128)(2,1)S(1)}, bf16[128,2048]{1,0:T(8,128)(2,1)S(1)}, u32[]{:S(2)}, u32[]{:S(2)}) collective-permute-start(bf16[128,2048]{1,0:T(8,128)(2,1)S(1)} %get-tuple-element.128), channel_id=1, source_target_pairs={{0,1},{1,0},{2,3},{3,2},{4,5},{5,4},{6,7},{7,6},{8,9},{9,8},{10,11... | collective-permute-start | bytes 1572872 | tf_op jit(solution)/shard_map/ppermute | solution.py:512
  32.7 16.8 %collective-permute-start.8 = (bf16[128,2048]{1,0:T(8,128)(2,1)S(1)}, bf16[128,2048]{1,0:T(8,128)(2,1)S(1)}, u32[]{:S(2)}, u32[]{:S(2)}) collective-permute-start(bf16[128,2048]{1,0:T(8,128)(2,1)S(1)} %get-tuple-element.156), channel_id=1, source_target_pairs={{0,15},{1,2},{2,1},{3,4},{4,3},{5,6},{6,5},{7,8},{8,7},{9,10},{10,... | collective-permute-start | bytes 1572872 | tf_op jit(solution)/shard_map/ppermute | solution.py:515
  37.0 1.6 %collective-permute-start.5 = (bf16[64,2048]{1,0:T(8,128)(2,1)S(1)}, bf16[64,2048]{1,0:T(8,128)(2,1)S(1)}, u32[]{:S(2)}, u32[]{:S(2)}) collective-permute-start(bf16[64,2048]{1,0:T(8,128)(2,1)S(1)} %get-tuple-element.137), channel_id=1, source_target_pairs={{0,1},{1,0},{2,3},{3,2},{4,5},{5,4},{6,7},{7,6},{8,9},{9,8},{10,11... | collective-permute-start | bytes 786440 | tf_op jit(solution)/shard_map/ppermute | solution.py:512
  37.0 1.9 %collective-permute-start.6 = (bf16[64,2048]{1,0:T(8,128)(2,1)S(1)}, bf16[64,2048]{1,0:T(8,128)(2,1)S(1)}, u32[]{:S(2)}, u32[]{:S(2)}) collective-permute-start(bf16[64,2048]{1,0:T(8,128)(2,1)S(1)} %get-tuple-element.138), channel_id=1, source_target_pairs={{0,1},{1,0},{2,3},{3,2},{4,5},{5,4},{6,7},{7,6},{8,9},{9,8},{10,11... | collective-permute-start | bytes 786440 | tf_op jit(solution)/shard_map/ppermute | solution.py:512
  40.8 16.3 %collective-permute-start.7 = (bf16[128,2048]{1,0:T(8,128)(2,1)S(1)}, bf16[128,2048]{1,0:T(8,128)(2,1)S(1)}, u32[]{:S(2)}, u32[]{:S(2)}) collective-permute-start(bf16[128,2048]{1,0:T(8,128)(2,1)S(1)} %get-tuple-element.155), channel_id=1, source_target_pairs={{0,15},{1,2},{2,1},{3,4},{4,3},{5,6},{6,5},{7,8},{8,7},{9,10},{10,... | collective-permute-start | bytes 1572872 | tf_op jit(solution)/shard_map/ppermute | solution.py:515
  51.2 1.9 %collective-permute-start.9 = (bf16[64,2048]{1,0:T(8,128)(2,1)S(1)}, bf16[64,2048]{1,0:T(8,128)(2,1)S(1)}, u32[]{:S(2)}, u32[]{:S(2)}) collective-permute-start(bf16[64,2048]{1,0:T(8,128)(2,1)S(1)} %get-tuple-element.161), channel_id=1, source_target_pairs={{0,1},{1,0},{2,3},{3,2},{4,5},{5,4},{6,7},{7,6},{8,9},{9,8},{10,11... | collective-permute-start | bytes 786440 | tf_op jit(solution)/shard_map/ppermute | solution.py:512
  51.3 1.9 %collective-permute-start.10 = (bf16[64,2048]{1,0:T(8,128)(2,1)S(1)}, bf16[64,2048]{1,0:T(8,128)(2,1)S(1)}, u32[]{:S(2)}, u32[]{:S(2)}) collective-permute-start(bf16[64,2048]{1,0:T(8,128)(2,1)S(1)} %get-tuple-element.162), channel_id=1, source_target_pairs={{0,1},{1,0},{2,3},{3,2},{4,5},{5,4},{6,7},{7,6},{8,9},{9,8},{10,11... | collective-permute-start | bytes 786440 | tf_op jit(solution)/shard_map/ppermute | solution.py:512

commit v8 on v7

--- a/solution.py
+++ b/solution.py
@@ -135,16 +135,18 @@
     first = jnp.sum(dqkv32 * wg_ref[...], axis=-1, keepdims=True) * (1.0 / width)
     second = jnp.sum(dqkv32 * qkv_ref[...].astype(F32), axis=-1, keepdims=True) * (1.0 / width)
     mean, rstd = st_ref[:, 0:128], st_ref[:, 128:256]
-    first, second = lanes(first) * rstd, lanes(second) * rstd
+    first, second = lanes(first) * rstd, lanes(second) * rstd * rstd
     for block in range(0, width, 512):
         wide = dot(dqkv_ref[...], wqt_ref[:, block:block + 512])
         for n in range(0, 512, 128):
             cols = pl.ds(block + n, 128)
             du = wide[:, n:n + 128]
-            xhat = (whole(h, cols).astype(F32) - mean) * rstd
-            dg_ref[:, cols] = jnp.sum((du * xhat).reshape(rows // 8, 8, 128), axis=0)
+            centred = whole(h, cols).astype(F32) - mean
+            du = du * rstd
+            if dg_ref is not None:
+                dg_ref[:, cols] = jnp.sum((du * centred).reshape(rows // 8, 8, 128), axis=0)
             gain = gain_ref[:, cols].astype(F32)
-            value = (du * gain) * rstd - first - xhat * second + whole(g, cols).astype(F32)
+            value = du * gain - centred * second - first + whole(g, cols).astype(F32)
             size = e[0].shape[0]
             for part in range(len(e)):
                 e[part][:, cols] = value[part * size:(part + 1) * size].astype(BF16)
@@ -321,25 +323,24 @@
 
     def body(ins, outs, scratch):
         h, g, datt_ref, (gain_ref, wq_ref), mask_ref, (wqt_ref, wg_ref) = ins
-        e, (u_ref, dqkv_ref, att_ref, dg_ref) = outs
-        qkv_ref, p_ref, st_ref = scratch
+        e, (u_ref, dqkv_ref, att_ref, st_ref) = outs
+        qkv_ref, p_ref = scratch
         attend(h, gain_ref, wq_ref, mask_ref, u_ref, qkv_ref, p_ref, att_ref, st_ref)
         attention_reverse(datt_ref[...], qkv_ref, p_ref, dqkv_ref)
-        norm_reverse(g, h, gain_ref, wqt_ref, wg_ref, qkv_ref, st_ref, e, dqkv_ref, dg_ref)
-
-    e, (u, dqkv, att, dgain) = call(
+        norm_reverse(g, h, gain_ref, wqt_ref, wg_ref, qkv_ref, st_ref, e, dqkv_ref, None)
+
+    e, (u, dqkv, att, stats) = call(
         "turn", body, [h, g, datt, fixed[:2], mask, [turned[0], turned[2]]],
         [
             stream(rows, width, parts),
-            [Mem((rows, width), BF16), Mem((rows, 3 * hd), BF16), Mem((rows, hd), BF16), Mem((8, width), F32)],
+            [Mem((rows, width), BF16), Mem((rows, 3 * hd), BF16), Mem((rows, hd), BF16), Mem((rows, 256), F32)],
         ],
         [
             pltpu.VMEM((rows, 3 * hd), BF16),
             pltpu.VMEM((HEADS_DEV, rows, rows), F32),
-            pltpu.VMEM((rows, 256), F32),
         ],
     )
-    return e, (u, dqkv, att, g, dgain)
+    return e, (u, dqkv, att, g, stats)
 
 
 def backward_kernel(g, h, gain, turned, saved, parts):
@@ -396,20 +397,28 @@
             wait()
 
 
-def early_weights(uses, h_a, att_a, h_b, att_b, wo):
+def early_weights(uses, h_a, h_b, wo, wqt):
     rows, width = uses[0][0].shape
     hd = HEADS_DEV * HEAD_DIM
 
     def body(ins, outs, scratch):
-        uses, h_a, att_a_ref, h_b, att_b_ref, wo_ref = ins
+        uses, h_a, h_b, wo_ref, wqt_ref = ins
         (down, up), gain_out, wo_out, wq_out = outs
         a_ref, b_ref, sems = scratch
         copies = Copies(sems, is_odd())
-        project_out(h_a, att_a_ref, wo_ref, [a_ref])
+        project_out(h_a, uses[1][2], wo_ref, [a_ref])
         copies.push(a_ref, down.at[0], up.at[0])
-        project_out(h_b, att_b_ref, wo_ref, [b_ref])
+        project_out(h_b, uses[0][2], wo_ref, [b_ref])
         copies.push(b_ref, up.at[0], down.at[0])
-        gain_out[...] = gain_sum(uses)
+        for block in range(0, width, 512):
+            wide = [dot(use[1][...], wqt_ref[:, block:block + 512]) for use in uses[:2]]
+            for n in range(0, 512, 128):
+                cols = pl.ds(block + n, 128)
+                total = uses[2][4][:, cols]
+                for use, h, du in zip(uses, (h_b, h_a), wide):
+                    xhat = (whole(h, cols).astype(F32) - use[4][:, 0:128]) * use[4][:, 128:256]
+                    total = total + jnp.sum((du[:, n:n + 128] * xhat).reshape(rows // 8, 8, 128), axis=0)
+                gain_out[:, cols] = total
 
         def put_wo(cols, value):
             wo_out[:, cols] = value
@@ -422,7 +431,7 @@
         copies.wait()
 
     outs, *sums = call(
-        "early_weights", body, [list(uses), h_a, att_a, h_b, att_b, wo],
+        "early_weights", body, [list(uses), h_a, h_b, wo, wqt],
         [[jax.ShapeDtypeStruct((1, rows, width), BF16)] * 2,
          Mem((8, width), F32), Mem((hd, width), F32), Mem((width, 3 * hd), F32)],
         [pltpu.VMEM((rows, width), BF16), pltpu.VMEM((rows, width), BF16), pltpu.SemaphoreType.DMA((2,))],
@@ -535,7 +544,7 @@
     ea1, use_a1 = backward_kernel(after(ca1, use_a2[4]), a1, gain, turned, a1_saved, 1)
     ca0 = swap_far(ea1)
     (out_down, out_up), sums = early_weights(
-        [use_b2, use_a2, after(use_a1, use_a1[4])], a2, use_a2[2], b2, use_b2[2], wo)
+        [use_b2, use_a2, after(use_a1, use_a1[4])], a2, b2, wo, turned[0])
     eb1, use_b1 = backward_kernel(after(cb1, sums[0]), b1, gain, turned, b1_saved, NEAR_PARTS)
     cb0 = swap_near(eb1)
     sums = more_weights([after(use_b1, use_b1[4])], sums)

time: 61.2 us -> 61.1 us (level)
  waiting for transfers between devices: 21.7 us -> 20.9 us
    ppermute x4, waiting for transfers between devices: 18.8 us -> 18 us  [swap_far(): return [lax.ppermute(part, 'section', far) for part in x]]
    pallas_call x13, Pallas kernels: 29.6 us -> 30.2 us  [call(): pl.pallas_call(kernel, in_specs=[far if isinstance(x, Far) else VM for x...]
  transfers between devices with their start and end apart: 11 -> 11, of which waited for: 9 -> 9; matrix products, arithmetic and copies ran while one was open for 0% -> 0% of each run, Pallas kernels for 37% -> 38%
where the time goes in v8:
time: 61.1 us; the launch traced here: 60.9 us
  Pallas kernels  30.2 us (49%)
  waiting for transfers between devices  20.9 us (34%)
  starting transfers between devices  8.89 us (15%)
  between operations  0.92 us (2%)
    pallas_call x13, Pallas kernels, call(): pl.pallas_call(kernel, in_specs=[far if isinstance(x, Far) else VM for x...  30.2 us
    ppermute x4, waiting for transfers between devices, swap_far(): return [lax.ppermute(part, 'section', far) for part in x]  18 us
    ppermute x4, starting transfers between devices, swap_far(): return [lax.ppermute(part, 'section', far) for part in x]  4.67 us
    ppermute x7, starting transfers between devices, swap_near(): return [lax.ppermute(part, 'section', near) for part in x]  4.22 us
    ppermute x7, waiting for transfers between devices, swap_near(): return [lax.ppermute(part, 'section', near) for part in x]  2.93 us
  transfers between devices with their start and end apart: 11, of which 9 were waited for; matrix products, arithmetic and copies ran while one was open for 0% of the time, Pallas kernels for 38%

profile of v8, /device:TPU:1, one launch (start us, length us, event | category | flops | bytes accessed | tf_op | source)
XLA Modules:
  0.0 60.9 jit_solution(5893026064464745337)
XLA Ops:
  0.6 3.2 %first.1 = (bf16[128,2048]{1,0:T(8,128)(2,1)S(1)}, bf16[128,2048]{1,0:T(8,128)(2,1)S(1)}, bf16[1,2048]{1,0:T(2,128)(2,1)S(1)}, bf16[2048,768]{1,0:T(8,128)(2,1)S...) custom-call(s32[2,4]{1,0:T(2,128)} %bitcast.1, ...), custom_call_target="tpu_custom_call" | custom-call | flops 2000000 | bytes 200 | tf_op jit(solution)/shard_map/first/pallas_call | solution.py:191
  3.8 2.7 %collective-permute-start.3 = (bf16[128,2048]{1,0:T(8,128)(2,1)S(1)}, bf16[128,2048]{1,0:T(8,128)(2,1)S(1)}, u32[]{:S(2)}, u32[]{:S(2)}) collective-permute-start(bf16[128,2048]{1,0:T(8,128)(2,1)S(1)} %get-tuple-element.115), channel_id=1, source_target_pairs={{0,15},{1,2},{2,1},{3,4},{4,3},{5,6},{6,5},{7,8},{8,7},{9,10},{10,... | collective-permute-start | bytes 1572872 | tf_op jit(solution)/shard_map/ppermute | solution.py:524
  6.5 1.6 %forward.3 = (bf16[64,2048]{1,0:T(8,128)(2,1)S(1)}, bf16[64,2048]{1,0:T(8,128)(2,1)S(1)}, bf16[128,2048]{1,0:T(8,128)(2,1)S(1)}, bf16[128,768]{1,0:T(8,128)(2,1)...) custom-call(bf16[128,2048]{1,0:T(8,128)(2,1)S(1)} %get-tuple-element.104.refs_0_.refs_2_, ...), custom_call_target="tpu_custom_call" | custom-call | flops 2000000 | bytes 200 | tf_op jit(solution)/shard_map/forward/pallas_call | solution.py:191
  8.1 2.9 %collective-permute-start = (bf16[64,2048]{1,0:T(8,128)(2,1)S(1)}, bf16[64,2048]{1,0:T(8,128)(2,1)S(1)}, u32[]{:S(2)}, u32[]{:S(2)}) collective-permute-start(bf16[64,2048]{1,0:T(8,128)(2,1)S(1)} %get-tuple-element.109), channel_id=1, source_target_pairs={{0,1},{1,0},{2,3},{3,2},{4,5},{5,4},{6,7},{7,6},{8,9},{9,8},{10,11... | collective-permute-start | bytes 786440 | tf_op jit(solution)/shard_map/ppermute | solution.py:521
  11.1 1.1 %collective-permute-done.refs_0_.refs_1_ = bf16[64,2048]{1,0:T(8,128)(2,1)S(1)} collective-permute-done((bf16[64,2048]{1,0:T(8,128)(2,1)S(1)}, bf16[64,2048]{1,0:T(8,128)(2,1)S(1)}, u32[]{:S(2)}, u32[]{:S(2)}) %collective-permute-start) | collective-permute-done | bytes 262176 | tf_op jit(solution)/shard_map/ppermute | solution.py:521
  12.6 1.6 %forward.4 = (bf16[128,2048]{1,0:T(8,128)(2,1)S(1)}, bf16[128,2048]{1,0:T(8,128)(2,1)S(1)}, bf16[128,768]{1,0:T(8,128)(2,1)S(1)}, f32[2,128,128]{2,1,0:T(8,128)S...) custom-call(bf16[64,2048]{1,0:T(8,128)(2,1)S(1)} %collective-permute-done.refs_0_.refs_1_, ...), custom_call_target="tpu_custom_call" | custom-call | flops 2000000 | bytes 200 | tf_op jit(solution)/shard_map/forward/pallas_call | solution.py:191
  14.2 2.9 %prepare.1 = (bf16[768,2048]{1,0:T(8,128)(2,1)S(1)}, bf16[2048,256]{1,0:T(8,128)(2,1)S(1)}, f32[1,768]{1,0:T(1,128)S(1)}, bf16[128,2048]{1,0:T(8,128)(2,1)S(1)},...) custom-call(bf16[1,2048]{1,0:T(2,128)(2,1)S(1)} %get-tuple-element.105.refs_1_.refs_2_.ref, ...), custom_call_target="tpu_custom_call" | custom-call | flops 2000000 | bytes 200 | tf_op jit(solution)/shard_map/prepare/pallas_call | solution.py:191
  17.1 6.7 %collective-permute-done.3.refs_0_.refs_2_ = bf16[128,2048]{1,0:T(8,128)(2,1)S(1)} collective-permute-done((bf16[128,2048]{1,0:T(8,128)(2,1)S(1)}, bf16[128,2048]{1,0:T(8,128)(2,1)S(1)}, u32[]{:S(2)}, u32[]{:S(2)}) %collective-permute-start.3) | collective-permute-done | bytes 524320 | tf_op jit(solution)/shard_map/ppermute | solution.py:524
  23.9 1.6 %forward.5 = (bf16[128,2048]{1,0:T(8,128)(2,1)S(1)}, bf16[128,2048]{1,0:T(8,128)(2,1)S(1)}, bf16[128,768]{1,0:T(8,128)(2,1)S(1)}, f32[2,128,128]{2,1,0:T(8,128)S...) custom-call(bf16[128,2048]{1,0:T(8,128)(2,1)S(1)} %collective-permute-done.3.refs_0_.refs_2_, ...), custom_call_target="tpu_custom_call" | custom-call | flops 8000000000 | bytes 800000 | tf_op jit(solution)/shard_map/forward/pallas_call | solution.py:191
  25.5 4.7 %collective-permute-done.2.refs_0_.refs_17_ = bf16[128,2048]{1,0:T(8,128)(2,1)S(1)} collective-permute-done((bf16[128,2048]{1,0:T(8,128)(2,1)S(1)}, bf16[128,2048]{1,0:T(8,128)(2,1)S(1)}, u32[]{:S(2)}, u32[]{:S(2)}) %collective-permute-start.2) | collective-permute-done | bytes 524320 | tf_op jit(solution)/shard_map/ppermute | solution.py:524
  30.2 2.4 %turn.2 = (bf16[128,2048]{1,0:T(8,128)(2,1)S(1)}, bf16[128,2048]{1,0:T(8,128)(2,1)S(1)}, bf16[128,768]{1,0:T(8,128)(2,1)S(1)}, bf16[128,256]{1,0:T(8,128)(2,1)S(1)}, f32[128,256]{1,0:T(8,128)S(1)}) custom-call(bf16[128,2048]{1,0:T(8,128)(2,1)S(1)} %collective-permute-done.2.refs_0_.refs_17_, bf16[128,2048]{1,0:T(8,128)(2,1)S(1)} %get-tuple-element.121.refs_1_.refs_3_, ...), custom_call_target="tpu_custom_call" | custom-call | flops 2000000 | bytes 200 | tf_op jit(solution)/shard_map/turn/pallas_call | solution.py:191
  32.6 1.8 %collective-permute-start.8 = (bf16[128,2048]{1,0:T(8,128)(2,1)S(1)}, bf16[128,2048]{1,0:T(8,128)(2,1)S(1)}, u32[]{:S(2)}, u32[]{:S(2)}) collective-permute-start(bf16[128,2048]{1,0:T(8,128)(2,1)S(1)} %get-tuple-element.156), channel_id=1, source_target_pairs={{0,15},{1,2},{2,1},{3,4},{4,3},{5,6},{6,5},{7,8},{8,7},{9,10},{10,... | collective-permute-start | bytes 1572872 | tf_op jit(solution)/shard_map/ppermute | solution.py:524
  34.4 2.3 %turn.3 = (bf16[64,2048]{1,0:T(8,128)(2,1)S(1)}, bf16[64,2048]{1,0:T(8,128)(2,1)S(1)}, bf16[128,2048]{1,0:T(8,128)(2,1)S(1)}, bf16[128,768]{1,0:T(8,128)(2,1)S(1...) custom-call(bf16[128,2048]{1,0:T(8,128)(2,1)S(1)} %collective-permute-done.4.refs_0_.refs_16_, ...), custom_call_target="tpu_custom_call" | custom-call | flops 2000000 | bytes 200 | tf_op jit(solution)/shard_map/turn/pallas_call | solution.py:191
  36.8 0.5 collective-permute-start.6
  37.3 1.0 %collective-permute-done.5.refs_0_.refs_13_ = bf16[64,2048]{1,0:T(8,128)(2,1)S(1)} collective-permute-done((bf16[64,2048]{1,0:T(8,128)(2,1)S(1)}, bf16[64,2048]{1,0:T(8,128)(2,1)S(1)}, u32[]{:S(2)}, u32[]{:S(2)}) %collective-permute-start.5) | collective-permute-done | bytes 262176 | tf_op jit(solution)/shard_map/ppermute | solution.py:521
  38.7 1.9 %backward.3 = (bf16[128,2048]{1,0:T(8,128)(2,1)S(1)}, bf16[128,768]{1,0:T(8,128)(2,1)S(1)}, f32[8,2048]{1,0:T(8,128)S(1)}) custom-call(bf16[64,2048]{1,0:T(8,128)(2,1)S(1)} %collective-permute-done.5.refs_0_.refs_13_, bf16[64,2048]{1,0:T(8,128)(2,1)S(1)} %collective-permute-done.6.refs_1_.refs_14_, ...), custom_call_target="tpu_custom_call" | custom-call | flops 2000000 | bytes 200 | tf_op jit(solution)/shard_map/backward/pallas_call | solution.py:191
  40.7 4.4 %early_weights.1 = (bf16[1,128,2048]{2,1,0:T(8,128)(2,1)}, bf16[1,128,2048]{2,1,0:T(8,128)(2,1)}, f32[8,2048]{1,0:T(8,128)S(1)}, f32[256,2048]{1,0:T(8,128)S(1)}, f32[2048,768]{1,0:T(8,128)S(1)}) custom-call(bf16[128,2048]{1,0:T(8,128)(2,1)S(1)} %get-tuple-element.124.refs_0_, bf16[128,768]{1,0:T(8,128)(2,1)S(1)} %get-tuple-element.125.refs_1_, ...), custom_call_target="tpu_custom_call" | custom-call | flops 2000000 | bytes 200 | tf_op jit(solution)/shard_map/early_weights/pallas_call | solution.py:191
  45.1 4.3 %collective-permute-done.8.refs_0_.refs_3_ = bf16[128,2048]{1,0:T(8,128)(2,1)S(1)} collective-permute-done((bf16[128,2048]{1,0:T(8,128)(2,1)S(1)}, bf16[128,2048]{1,0:T(8,128)(2,1)S(1)}, u32[]{:S(2)}, u32[]{:S(2)}) %collective-permute-start.8) | collective-permute-done | bytes 524320 | tf_op jit(solution)/shard_map/ppermute | solution.py:524
  49.4 1.7 %backward.4 = (bf16[64,2048]{1,0:T(8,128)(2,1)S(1)}, bf16[64,2048]{1,0:T(8,128)(2,1)S(1)}, bf16[128,768]{1,0:T(8,128)(2,1)S(1)}, f32[8,2048]{1,0:T(8,128)S(1)}) custom-call(bf16[128,2048]{1,0:T(8,128)(2,1)S(1)} %collective-permute-done.8.refs_0_.refs_3_, bf16[64,2048]{1,0:T(8,128)(2,1)S(1)} %collective-permute-done.refs_0_.refs_1_, ...), custom_call_target="tpu_custom_call" | custom-call | flops 2000000 | bytes 200 | tf_op jit(solution)/shard_map/backward/pallas_call | solution.py:191
  51.1 0.5 collective-permute-start.10
  51.6 1.3 %more_weights.1 = (f32[8,2048]{1,0:T(8,128)S(1)}, f32[256,2048]{1,0:T(8,128)S(1)}, f32[2048,768]{1,0:T(8,128)S(1)}) custom-call(bf16[128,2048]{1,0:T(8,128)(2,1)S(1)} %get-tuple-element.167.refs_0_, bf16[128,768]{1,0:T(8,128)(2,1)S(1)} %get-tuple-element.168.refs_1_, bf16[128,256]{1,0:T(8,128)(2,1)S(1)} %get-tuple-element.169.refs_2_, ...), custom_call_target="tpu_custom_call" | custom-call | flops 2000000 | bytes 200 | tf_op jit(solution)/shard_map/more_weights/pallas_call | solution.py:191
  53.0 1.7 %backward.5 = (bf16[128,2048]{1,0:T(8,128)(2,1)S(1)}, bf16[128,768]{1,0:T(8,128)(2,1)S(1)}, f32[8,2048]{1,0:T(8,128)S(1)}) custom-call(bf16[64,2048]{1,0:T(8,128)(2,1)S(1)} %collective-permute-done.9.refs_0_.refs_15_, bf16[64,2048]{1,0:T(8,128)(2,1)S(1)} %collective-permute-done.10.refs_1_.refs_16_, ...), custom_call_target="tpu_custom_call" | custom-call | flops 2000000 | bytes 200 | tf_op jit(solution)/shard_map/backward/pallas_call | solution.py:191
  54.8 2.2 %collective-permute-done.7.refs_0_ = bf16[128,2048]{1,0:T(8,128)(2,1)S(1)} collective-permute-done((bf16[128,2048]{1,0:T(8,128)(2,1)S(1)}, bf16[128,2048]{1,0:T(8,128)(2,1)S(1)}, u32[]{:S(2)}, u32[]{:S(2)}) %collective-permute-start.7) | collective-permute-done | bytes 524320 | tf_op jit(solution)/shard_map/ppermute | solution.py:524
  57.0 3.7 %finish.1 = (bf16[1,128,2048]{2,1,0:T(8,128)(2,1)}, bf16[1,128,2048]{2,1,0:T(8,128)(2,1)}, bf16[1,2048]{1,0:T(2,128)(2,1)}, bf16[1,256,2048]{2,1,0:T(8,128)(2,1)}, bf16[1,2048,768]{2,1,0:T(8,128)(2,1)}) custom-call(bf16[128,2048]{1,0:T(8,128)(2,1)S(1)} %collective-permute-done.7.refs_0_, bf16[128,2048]{1,0:T(8,128)(2,1)S(1)} %get-tuple-element.181.refs_1_, ...), custom_call_target="tpu_custom_call" | custom-call | flops 2000000 | bytes 200 | tf_op jit(solution)/shard_map/finish/pallas_call | solution.py:191
  (11 shorter events, 1.3 us)
Async XLA Ops:
  3.8 20.1 %collective-permute-start.3 = (bf16[128,2048]{1,0:T(8,128)(2,1)S(1)}, bf16[128,2048]{1,0:T(8,128)(2,1)S(1)}, u32[]{:S(2)}, u32[]{:S(2)}) collective-permute-start(bf16[128,2048]{1,0:T(8,128)(2,1)S(1)} %get-tuple-element.115), channel_id=1, source_target_pairs={{0,15},{1,2},{2,1},{3,4},{4,3},{5,6},{6,5},{7,8},{8,7},{9,10},{10,... | collective-permute-start | bytes 1572872 | tf_op jit(solution)/shard_map/ppermute | solution.py:524
  8.1 4.1 %collective-permute-start = (bf16[64,2048]{1,0:T(8,128)(2,1)S(1)}, bf16[64,2048]{1,0:T(8,128)(2,1)S(1)}, u32[]{:S(2)}, u32[]{:S(2)}) collective-permute-start(bf16[64,2048]{1,0:T(8,128)(2,1)S(1)} %get-tuple-element.109), channel_id=1, source_target_pairs={{0,1},{1,0},{2,3},{3,2},{4,5},{5,4},{6,7},{7,6},{8,9},{9,8},{10,11... | collective-permute-start | bytes 786440 | tf_op jit(solution)/shard_map/ppermute | solution.py:521
  11.0 1.5 %collective-permute-start.1 = (bf16[64,2048]{1,0:T(8,128)(2,1)S(1)}, bf16[64,2048]{1,0:T(8,128)(2,1)S(1)}, u32[]{:S(2)}, u32[]{:S(2)}) collective-permute-start(bf16[64,2048]{1,0:T(8,128)(2,1)S(1)} %get-tuple-element.110), channel_id=1, source_target_pairs={{0,1},{1,0},{2,3},{3,2},{4,5},{5,4},{6,7},{7,6},{8,9},{9,8},{10,11... | collective-permute-start | bytes 786440 | tf_op jit(solution)/shard_map/ppermute | solution.py:521
  14.1 16.1 %collective-permute-start.2 = (bf16[128,2048]{1,0:T(8,128)(2,1)S(1)}, bf16[128,2048]{1,0:T(8,128)(2,1)S(1)}, u32[]{:S(2)}, u32[]{:S(2)}) collective-permute-start(bf16[128,2048]{1,0:T(8,128)(2,1)S(1)} %get-tuple-element.114), channel_id=1, source_target_pairs={{0,15},{1,2},{2,1},{3,4},{4,3},{5,6},{6,5},{7,8},{8,7},{9,10},{10,... | collective-permute-start | bytes 1572872 | tf_op jit(solution)/shard_map/ppermute | solution.py:524
  25.5 9.0 %collective-permute-start.4 = (bf16[128,2048]{1,0:T(8,128)(2,1)S(1)}, bf16[128,2048]{1,0:T(8,128)(2,1)S(1)}, u32[]{:S(2)}, u32[]{:S(2)}) collective-permute-start(bf16[128,2048]{1,0:T(8,128)(2,1)S(1)} %get-tuple-element.128), channel_id=1, source_target_pairs={{0,1},{1,0},{2,3},{3,2},{4,5},{5,4},{6,7},{7,6},{8,9},{9,8},{10,11... | collective-permute-start | bytes 1572872 | tf_op jit(solution)/shard_map/ppermute | solution.py:521
  32.6 16.8 %collective-permute-start.8 = (bf16[128,2048]{1,0:T(8,128)(2,1)S(1)}, bf16[128,2048]{1,0:T(8,128)(2,1)S(1)}, u32[]{:S(2)}, u32[]{:S(2)}) collective-permute-start(bf16[128,2048]{1,0:T(8,128)(2,1)S(1)} %get-tuple-element.156), channel_id=1, source_target_pairs={{0,15},{1,2},{2,1},{3,4},{4,3},{5,6},{6,5},{7,8},{8,7},{9,10},{10,... | collective-permute-start | bytes 1572872 | tf_op jit(solution)/shard_map/ppermute | solution.py:524
  36.8 1.6 %collective-permute-start.5 = (bf16[64,2048]{1,0:T(8,128)(2,1)S(1)}, bf16[64,2048]{1,0:T(8,128)(2,1)S(1)}, u32[]{:S(2)}, u32[]{:S(2)}) collective-permute-start(bf16[64,2048]{1,0:T(8,128)(2,1)S(1)} %get-tuple-element.137), channel_id=1, source_target_pairs={{0,1},{1,0},{2,3},{3,2},{4,5},{5,4},{6,7},{7,6},{8,9},{9,8},{10,11... | collective-permute-start | bytes 786440 | tf_op jit(solution)/shard_map/ppermute | solution.py:521
  36.8 1.9 %collective-permute-start.6 = (bf16[64,2048]{1,0:T(8,128)(2,1)S(1)}, bf16[64,2048]{1,0:T(8,128)(2,1)S(1)}, u32[]{:S(2)}, u32[]{:S(2)}) collective-permute-start(bf16[64,2048]{1,0:T(8,128)(2,1)S(1)} %get-tuple-element.138), channel_id=1, source_target_pairs={{0,1},{1,0},{2,3},{3,2},{4,5},{5,4},{6,7},{7,6},{8,9},{9,8},{10,11... | collective-permute-start | bytes 786440 | tf_op jit(solution)/shard_map/ppermute | solution.py:521
  40.6 16.4 %collective-permute-start.7 = (bf16[128,2048]{1,0:T(8,128)(2,1)S(1)}, bf16[128,2048]{1,0:T(8,128)(2,1)S(1)}, u32[]{:S(2)}, u32[]{:S(2)}) collective-permute-start(bf16[128,2048]{1,0:T(8,128)(2,1)S(1)} %get-tuple-element.155), channel_id=1, source_target_pairs={{0,15},{1,2},{2,1},{3,4},{4,3},{5,6},{6,5},{7,8},{8,7},{9,10},{10,... | collective-permute-start | bytes 1572872 | tf_op jit(solution)/shard_map/ppermute | solution.py:524
  51.1 1.9 %collective-permute-start.9 = (bf16[64,2048]{1,0:T(8,128)(2,1)S(1)}, bf16[64,2048]{1,0:T(8,128)(2,1)S(1)}, u32[]{:S(2)}, u32[]{:S(2)}) collective-permute-start(bf16[64,2048]{1,0:T(8,128)(2,1)S(1)} %get-tuple-element.161), channel_id=1, source_target_pairs={{0,1},{1,0},{2,3},{3,2},{4,5},{5,4},{6,7},{7,6},{8,9},{9,8},{10,11... | collective-permute-start | bytes 786440 | tf_op jit(solution)/shard_map/ppermute | solution.py:521
  51.1 1.9 %collective-permute-start.10 = (bf16[64,2048]{1,0:T(8,128)(2,1)S(1)}, bf16[64,2048]{1,0:T(8,128)(2,1)S(1)}, u32[]{:S(2)}, u32[]{:S(2)}) collective-permute-start(bf16[64,2048]{1,0:T(8,128)(2,1)S(1)} %get-tuple-element.162), channel_id=1, source_target_pairs={{0,1},{1,0},{2,3},{3,2},{4,5},{5,4},{6,7},{7,6},{8,9},{9,8},{10,11... | collective-permute-start | bytes 786440 | tf_op jit(solution)/shard_map/ppermute | solution.py:521
